TPU v7x, 256 devices: a whole 4x4x8 slice. The times are simulated.
256 devices in a mesh: alpha: 128 (over y, z, x), beta: 2 (over core).
Axes of the slice: x: 4, y: 4, z: 8, core: 2. Of those that a mesh axis runs over, the one named last changes fastest.
Arguments:
- coeffs: bfloat16 [1, 16384, 4096], P(None, 'alpha', 'beta'), may hold values from -6 to 6
- beta_list: int32 [32, 8], P('beta'), may hold values from 0 to 31
- beta_kind: int32 [32, 8], P('beta'), may hold values from 0 to 7
- opp_beta_kind: int32 [32, 8], P('beta'), may hold values from 0 to 7
- alpha_list: int32 [128, 4], replicated, may hold values from 0 to 127, as said below
- alpha_kind: int32 [128, 4], replicated, may hold values from 0 to 7
- opp_list: int32 [128, 3], replicated, may hold values from 0 to 127, as said below
- opp_kind: int32 [128, 3], replicated, may hold values from 0 to 7
- beta_table: bfloat16 [8, 128, 128], replicated, may hold values from -0.1875 to 0.1875
- alpha_table: bfloat16 [8, 128, 128], replicated, may hold values from -0.25 to 0.25
- opp_alpha_table: bfloat16 [8, 128, 128], replicated, may hold values from -0.3125 to 0.3125
- opp_beta_table: bfloat16 [8, 128, 128], replicated, may hold values from -0.1875 to 0.1875
Outputs:
- sigma_out: bfloat16 [1, 16384, 4096], P(None, 'alpha', 'beta')
Inputs may be any that keep to these rules, and one draw needn't show every extreme that they name: `alpha_list`: each entry of row i lies within 3 of i; the entries of a row are distinct. `opp_list`: each entry of row i lies within 3 of i; the entries of a row are distinct.
All inputs are finite; a program needn't handle non-finite values.
Results may differ from a plain program's by a relative error of at most 0.0034.
Values may be sent and summed in bfloat16 or wider, within the bound.
No kernel may reach another device: no remote copies, remote signals or barrier semaphores. Data moves between devices by JAX's collectives and lax.ppermute only.
A program may use at most 128 MiB of HBM per device.

v0:
```python
import jax
import jax.numpy as jnp
from jax import lax
from jax.sharding import PartitionSpec as P

REACH = 3


def from_everyone(value, axis):
    count = lax.axis_size(axis)
    return lax.all_to_all(
        jnp.broadcast_to(value[None], (count, *value.shape)), axis, 0, 0, tiled=True
    )


def joined_along(pieces, dim):
    lengths = list(pieces.shape[1:])
    lengths[dim] *= pieces.shape[0]
    return jnp.moveaxis(pieces, 0, dim).reshape(lengths)


def gather_directly(value, axis, dim):
    pieces = from_everyone(value, axis)
    return joined_along(pieces, dim)


def shifted(block, axis, distance):
    devices = range(lax.axis_size(axis))
    route = [(i - distance, i) for i in devices if i - distance in devices]
    return lax.ppermute(block, axis, route)


def beta_apply(row_data, sources, kind_ids, tile_table):
    root_count, row_count, col_count = row_data.shape
    tile_size = tile_table.shape[1]
    tiled = row_data.reshape(root_count, row_count, col_count // tile_size, tile_size)
    picked = jnp.take(tiled, sources, axis=2)
    tile_sets = jnp.take(tile_table, kind_ids, axis=0)
    summed = jnp.einsum("rajmt,jmst->rajs", picked, tile_sets, preferred_element_type=jnp.float32)
    return summed.reshape(root_count, row_count, -1)


def nearby_sum(stacked, sources, kind_ids, tile_table, own_block):
    summed = jnp.zeros(stacked.shape[1:], jnp.float32)
    for link in range(sources.shape[0]):
        position = sources[link] - own_block + REACH
        picked = lax.dynamic_index_in_dim(stacked, position, 0, keepdims=False)
        tile_one = lax.dynamic_index_in_dim(tile_table, kind_ids[link], 0, keepdims=False)
        summed = summed + jnp.einsum(
            "st,rtc->rsc", tile_one, picked, preferred_element_type=jnp.float32
        )
    return summed


def local(
    coeffs,
    beta_list,
    beta_kind,
    opp_beta_kind,
    alpha_list,
    alpha_kind,
    opp_list,
    opp_kind,
    beta_table,
    alpha_table,
    opp_alpha_table,
    opp_beta_table,
):
    whole_cols = gather_directly(coeffs, "beta", 2)
    beta_part = beta_apply(whole_cols, beta_list, beta_kind, beta_table)
    own_block = lax.axis_index("alpha")
    nearby = []
    for slot in range(2 * REACH + 1):
        if slot == REACH:
            nearby.append(coeffs)
        else:
            nearby.append(shifted(coeffs, "alpha", REACH - slot))
    stacked = jnp.stack(nearby)
    alpha_part = nearby_sum(
        stacked,
        lax.dynamic_index_in_dim(alpha_list, own_block, 0, keepdims=False),
        lax.dynamic_index_in_dim(alpha_kind, own_block, 0, keepdims=False),
        alpha_table,
        own_block,
    )
    half_sum = nearby_sum(
        stacked,
        lax.dynamic_index_in_dim(opp_list, own_block, 0, keepdims=False),
        lax.dynamic_index_in_dim(opp_kind, own_block, 0, keepdims=False),
        opp_alpha_table,
        own_block,
    ).astype(jnp.bfloat16)
    half_whole = gather_directly(half_sum, "beta", 2)
    mixed_part = beta_apply(half_whole, beta_list, opp_beta_kind, opp_beta_table)
    return (beta_part + alpha_part + mixed_part).astype(jnp.bfloat16)


def solution(mesh):
    placed = (
        P(None, "alpha", "beta"),
        P("beta", None),
        P("beta", None),
        P("beta", None),
        P(),
        P(),
        P(),
        P(),
        P(),
        P(),
        P(),
        P(),
    )
    return jax.shard_map(
        local, mesh=mesh, in_specs=placed, out_specs=P(None, "alpha", "beta"), check_vma=False
    )
```

profile of v0, /device:TPU:25, one launch (start us, length us, event | category | flops | bytes accessed | tf_op | source)
XLA Modules:
  0.0 101.3 jit_solution(2066790117416417074)
XLA Ops:
  0.0 4.5 %collective-permute-start = (bf16[1,128,2048]{2,1,0:T(8,128)(2,1)}, bf16[1,128,2048]{2,1,0:T(8,128)(2,1)}, u32[]{:S(2)}, u32[]{:S(2)}) collective-permute-start(bf16[1,128,2048]{2,1,0:T(8,128)(2,1)} %param.16), channel_id=1, source_target_pairs={{0,6},{2,8},{4,10},{6,12},{8,14},{10,16},{12,18},{14,20},{16,22},{... | collective-permute-start | bytes 1572872 | tf_op jit(solution)/shard_map/ppermute | solution.py:30
  4.6 3.8 %collective-permute-start.1 = (bf16[1,128,2048]{2,1,0:T(8,128)(2,1)}, bf16[1,128,2048]{2,1,0:T(8,128)(2,1)}, u32[]{:S(2)}, u32[]{:S(2)}) collective-permute-start(bf16[1,128,2048]{2,1,0:T(8,128)(2,1)} %param.16), channel_id=1, source_target_pairs={{0,4},{2,6},{4,8},{6,10},{8,12},{10,14},{12,16},{14,18},{16,20},{1... | collective-permute-start | bytes 1572872 | tf_op jit(solution)/shard_map/ppermute | solution.py:30
  8.4 2.5 %collective-permute-start.2 = (bf16[1,128,2048]{2,1,0:T(8,128)(2,1)}, bf16[1,128,2048]{2,1,0:T(8,128)(2,1)}, u32[]{:S(2)}, u32[]{:S(2)}) collective-permute-start(bf16[1,128,2048]{2,1,0:T(8,128)(2,1)} %param.16), channel_id=1, source_target_pairs={{0,2},{2,4},{4,6},{6,8},{8,10},{10,12},{12,14},{14,16},{16,18},{18... | collective-permute-start | bytes 1572872 | tf_op jit(solution)/shard_map/ppermute | solution.py:30
  10.9 7.0 %collective-permute-start.3 = (bf16[1,128,2048]{2,1,0:T(8,128)(2,1)}, bf16[1,128,2048]{2,1,0:T(8,128)(2,1)}, u32[]{:S(2)}, u32[]{:S(2)}) collective-permute-start(bf16[1,128,2048]{2,1,0:T(8,128)(2,1)} %param.16), channel_id=1, source_target_pairs={{2,0},{4,2},{6,4},{8,6},{10,8},{12,10},{14,12},{16,14},{18,16},{20... | collective-permute-start | bytes 1572872 | tf_op jit(solution)/shard_map/ppermute | solution.py:30
  17.9 2.2 %collective-permute-start.4 = (bf16[1,128,2048]{2,1,0:T(8,128)(2,1)}, bf16[1,128,2048]{2,1,0:T(8,128)(2,1)S(1)}, u32[]{:S(2)}, u32[]{:S(2)}) collective-permute-start(bf16[1,128,2048]{2,1,0:T(8,128)(2,1)} %param.16), channel_id=1, source_target_pairs={{4,0},{6,2},{8,4},{10,6},{12,8},{14,10},{16,12},{18,14},{20,16},{2... | collective-permute-start | bytes 1572872 | tf_op jit(solution)/shard_map/ppermute | solution.py:30
  20.1 1.3 %copy.38 = bf16[128,2048]{0,1:T(8,128)(2,1)S(1)} copy(bf16[128,2048]{1,0:T(8,128)(2,1)} %bitcast.139) | data formatting | bytes 1048576 | tf_op jit(solution)/shard_map/broadcast_in_dim | solution.py:12
  21.4 1.1 %broadcast_in_dim.37 = bf16[2,1,128,2048]{2,3,1,0:T(8,128)(2,1)} broadcast(bf16[128,2048]{0,1:T(8,128)(2,1)S(1)} %copy.38), dimensions={2,3} | broadcast | bytes 1572864 | tf_op jit(solution)/shard_map/broadcast_in_dim | solution.py:12
  22.5 5.2 %all-to-all-start = ((bf16[2,1,128,2048]{2,3,1,0:T(8,128)(2,1)}), bf16[2,1,128,2048]{2,3,1,0:T(8,128)(2,1)S(1)}, u32[]{:S(2)}, u32[]{:S(2)}) async-start(bf16[2,1,128,2048]{2,3,1,0:T(8,128)(2,1)} %broadcast_in_dim.37), calls=%async_computation | async-start | bytes 2097152 | tf_op jit(solution)/shard_map/all_to_all | solution.py:11
  30.4 3.0 %gather_fusion.1 = bf16[128,128,128]{2,1,0:T(8,128)(2,1)} fusion(bf16[128,32,128]{2,0,1:T(8,128)(2,1)S(1)} %bitcast.131, s32[1024]{0:T(1024)S(1)} %pad_clamp_fusion.1), kind=kCustom, calls=%fused_computation.1.clone | custom fusion | bytes 8389120 | tf_op jit(solution)/shard_map/jit(_take)/gather | solution.py:37
  33.4 3.1 %gather_fusion = bf16[128,128,128]{2,1,0:T(8,128)(2,1)} fusion(bf16[8,128,128]{2,1,0:T(8,128)(2,1)S(1)} %copy-done, s32[1024]{0:T(1024)S(1)} %pad_clamp_fusion.2), kind=kCustom, calls=%fused_computation.clone | custom fusion | bytes 8389120 | tf_op jit(solution)/shard_map/jit(_take)/gather | solution.py:38
  36.6 6.0 %fusion.2 = f32[16,128,128,1]{2,1,3,0:T(8,128)} fusion(bf16[1,128,16,8,128]{4,1,3,2,0:T(8,128)(2,1)} %bitcast.135, bf16[16,8,128,128]{3,2,1,0:T(8,128)(2,1)} %bitcast.136, pred[16,8]{1,0:T(8,128)(4,1)S(1)} %copy.37, pred[16,8]{1,0:T(8,128)(4,1)S(1)} %copy.35), kind=kOutput, calls=%fused_computation.6 | convolution fusion | flops 541065216 | bytes 9437440 | tf_op jit(solution)/shard_map/rajmt,jmst->rajs/dot_general | solution.py:39
  59.2 3.0 %gather_fusion.2 = bf16[128,128,128]{2,1,0:T(8,128)(2,1)} fusion(bf16[8,128,128]{2,1,0:T(8,128)(2,1)S(1)} %copy-done.1, s32[1024]{0:T(1024)S(1)} %pad_clamp_fusion), kind=kCustom, calls=%fused_computation.2.clone | custom fusion | bytes 8389120 | tf_op jit(solution)/shard_map/jit(_take)/gather | solution.py:38
  64.7 4.4 %collective-permute-start.5 = (bf16[1,128,2048]{2,1,0:T(8,128)(2,1)S(1)}, bf16[1,128,2048]{2,1,0:T(8,128)(2,1)S(1)}, u32[]{:S(2)}, u32[]{:S(2)}) collective-permute-start(bf16[1,128,2048]{2,1,0:T(8,128)(2,1)S(1)} %copy-done.4), channel_id=1, source_target_pairs={{6,0},{8,2},{10,4},{12,6},{14,8},{16,10},{18,12},{20,14},{22,16},{... | collective-permute-start | bytes 1572872 | tf_op jit(solution)/shard_map/ppermute | solution.py:30
  69.1 1.1 %bitcast_dynamic-update-slice_fusion.6 = bf16[7,1,128,2048]{3,2,1,0:T(8,128)(2,1)S(1)} fusion(bf16[1,128,2048]{2,1,0:T(8,128)(2,1)} %collective-permute-done), kind=kLoop, calls=%fused_computation.46 | loop fusion | bytes 1048576
  70.2 1.1 %bitcast_dynamic-update-slice_fusion.5 = bf16[7,1,128,2048]{3,2,1,0:T(8,128)(2,1)S(1)} fusion(bf16[7,1,128,2048]{3,2,1,0:T(8,128)(2,1)S(1)} %bitcast_dynamic-update-slice_fusion.6, bf16[1,128,2048]{2,1,0:T(8,128)(2,1)} %collective-permute-done.1), kind=kLoop, calls=%fused_computation.45 | loop fusion | bytes 1048576
  71.3 1.1 %bitcast_dynamic-update-slice_fusion.4 = bf16[7,1,128,2048]{3,2,1,0:T(8,128)(2,1)S(1)} fusion(bf16[7,1,128,2048]{3,2,1,0:T(8,128)(2,1)S(1)} %bitcast_dynamic-update-slice_fusion.5, bf16[1,128,2048]{2,1,0:T(8,128)(2,1)} %collective-permute-done.2), kind=kLoop, calls=%fused_computation.44 | loop fusion | bytes 1048576
  72.4 1.1 %bitcast_dynamic-update-slice_fusion.2 = bf16[7,1,128,2048]{3,2,1,0:T(8,128)(2,1)S(1)} fusion(bf16[7,1,128,2048]{3,2,1,0:T(8,128)(2,1)S(1)} %bitcast_dynamic-update-slice_fusion.3, bf16[1,128,2048]{2,1,0:T(8,128)(2,1)} %collective-permute-done.3), kind=kLoop, calls=%fused_computation.42 | loop fusion | bytes 1048576
  73.6 7.3 %collective-permute-done.5 = bf16[1,128,2048]{2,1,0:T(8,128)(2,1)S(1)} collective-permute-done((bf16[1,128,2048]{2,1,0:T(8,128)(2,1)S(1)}, bf16[1,128,2048]{2,1,0:T(8,128)(2,1)S(1)}, u32[]{:S(2)}, u32[]{:S(2)}) %collective-permute-start.5) | collective-permute-done | bytes 524320 | tf_op jit(solution)/shard_map/ppermute | solution.py:30
  81.0 1.1 %fusion.23 = f32[2048,128]{1,0:T(8,128)S(1)} fusion(bf16[7,1,128,2048]{3,2,1,0:T(8,128)(2,1)S(1)} %bitcast_dynamic-update-slice_fusion, s32[]{:T(128)S(6)} %select_n.84, bf16[8,128,128]{2,1,0:T(8,128)(2,1)} %param.26, s32[]{:T(128)S(6)} %select_n.85), kind=kOutput, calls=%fused_computation.32 | convolution fusion | flops 67108864 | bytes 1605640 | tf_op jit(solution)/shard_map/st,rtc->rsc/dot_general | solution.py:49
  82.1 1.1 %convolution_add_fusion.1 = f32[2048,128]{1,0:T(8,128)S(1)} fusion(f32[2048,128]{1,0:T(8,128)S(1)} %fusion.23, bf16[7,1,128,2048]{3,2,1,0:T(8,128)(2,1)S(1)} %bitcast_dynamic-update-slice_fusion, s32[]{:T(128)S(6)} %select_n.82, bf16[8,128,128]{2,1,0:T(8,128)(2,1)} %param.26, s32[]{:T(128)S(6)} %select_n.83), kind=kOutput, calls=%fused_computation.17 | convolution fusion | flops 67371008 | bytes 2654216 | tf_op jit(solution)/shard_map/st,rtc->rsc/dot_general | solution.py:49
  83.3 1.1 %fusion.17 = bf16[128,2048]{0,1:T(8,128)(2,1)S(1)} fusion(f32[2048,128]{1,0:T(8,128)S(1)} %convolution_add_fusion.1, bf16[7,1,128,2048]{3,2,1,0:T(8,128)(2,1)S(1)} %bitcast_dynamic-update-slice_fusion, s32[]{:T(128)S(6)} %select_n.86, bf16[8,128,128]{2,1,0:T(8,128)(2,1)} %param.26, s32[]{:T(128)S(6)} %select_n.87), kind=kOutput, calls=%fused_computation.26 | convolution fusion | flops 67633152 | bytes 2129928 | tf_op jit(solution)/shard_map/st,rtc->rsc/dot_general | solution.py:49
  84.5 5.4 %all_to_all.10 = bf16[2,1,128,2048]{2,3,1,0:T(8,128)(2,1)S(1)} all-to-all(bf16[2,1,128,2048]{2,3,1,0:T(8,128)(2,1)S(1)} %broadcast_in_dim.40), channel_id=1, replica_groups=mesh['alpha'=128,'beta'=2] {'beta'}, dimensions={0} | all-to-all | bytes 2097152 | tf_op jit(solution)/shard_map/all_to_all | solution.py:11
  90.5 3.1 %gather_fusion.3 = bf16[128,128,128]{2,1,0:T(8,128)(2,1)} fusion(bf16[128,32,128]{2,0,1:T(8,128)(2,1)S(1)} %bitcast.132, s32[1024]{0:T(1024)S(1)} %pad_clamp_fusion.1), kind=kCustom, calls=%fused_computation.3.clone | custom fusion | bytes 8389120 | tf_op jit(solution)/shard_map/jit(_take)/gather | solution.py:37
  93.7 5.0 %fusion = f32[16,128,128,1]{2,1,3,0:T(8,128)S(1)} fusion(bf16[1,128,16,8,128]{4,1,3,2,0:T(8,128)(2,1)} %bitcast.134, bf16[16,8,128,128]{3,2,1,0:T(8,128)(2,1)} %bitcast.133, pred[16,8]{1,0:T(8,128)(4,1)S(1)} %copy.42, pred[16,8]{1,0:T(8,128)(4,1)S(1)} %copy.37), kind=kOutput, calls=%fused_computation.4 | convolution fusion | flops 541065216 | bytes 9437440 | tf_op jit(solution)/shard_map/rajmt,jmst->rajs/dot_general | solution.py:39
  (67 shorter events, 8.0 us)
Async XLA Ops:
  0.0 33.4 %copy-start = (bf16[8,128,128]{2,1,0:T(8,128)(2,1)S(1)}, bf16[8,128,128]{2,1,0:T(8,128)(2,1)}, u32[]{:S(2)}) copy-start(bf16[8,128,128]{2,1,0:T(8,128)(2,1)} %param.24) | copy-start | bytes 786436
  0.0 27.7 %copy-start.8 = (s32[16,8]{0,1:T(8,128)S(1)}, s32[16,8]{0,1:T(8,128)}, u32[]{:S(2)}) copy-start(s32[16,8]{0,1:T(8,128)} %param.19) | copy-start | bytes 1540
  0.0 27.7 %copy-start.9 = (s32[16,8]{0,1:T(8,128)S(1)}, s32[16,8]{0,1:T(8,128)}, u32[]{:S(2)}) copy-start(s32[16,8]{0,1:T(8,128)} %param.17) | copy-start | bytes 1540
  0.0 27.7 %copy-start.7 = (s32[16,8]{0,1:T(8,128)S(1)}, s32[16,8]{0,1:T(8,128)}, u32[]{:S(2)}) copy-start(s32[16,8]{0,1:T(8,128)} %param.18) | copy-start | bytes 1540
  0.0 27.8 %copy-start.10 = (s32[128,3]{0,1:T(4,128)S(1)}, s32[128,3]{0,1:T(4,128)}, u32[]{:S(2)}) copy-start(s32[128,3]{0,1:T(4,128)} %param.23) | copy-start | bytes 4612
  0.0 27.8 %copy-start.11 = (s32[128,3]{0,1:T(4,128)S(1)}, s32[128,3]{0,1:T(4,128)}, u32[]{:S(2)}) copy-start(s32[128,3]{0,1:T(4,128)} %param.22) | copy-start | bytes 4612
  0.0 64.6 %collective-permute-start = (bf16[1,128,2048]{2,1,0:T(8,128)(2,1)}, bf16[1,128,2048]{2,1,0:T(8,128)(2,1)}, u32[]{:S(2)}, u32[]{:S(2)}) collective-permute-start(bf16[1,128,2048]{2,1,0:T(8,128)(2,1)} %param.16), channel_id=1, source_target_pairs={{0,6},{2,8},{4,10},{6,12},{8,14},{10,16},{12,18},{14,20},{16,22},{... | collective-permute-start | bytes 1572872 | tf_op jit(solution)/shard_map/ppermute | solution.py:30
  4.6 65.6 %collective-permute-start.1 = (bf16[1,128,2048]{2,1,0:T(8,128)(2,1)}, bf16[1,128,2048]{2,1,0:T(8,128)(2,1)}, u32[]{:S(2)}, u32[]{:S(2)}) collective-permute-start(bf16[1,128,2048]{2,1,0:T(8,128)(2,1)} %param.16), channel_id=1, source_target_pairs={{0,4},{2,6},{4,8},{6,10},{8,12},{10,14},{12,16},{14,18},{16,20},{1... | collective-permute-start | bytes 1572872 | tf_op jit(solution)/shard_map/ppermute | solution.py:30
  8.4 62.9 %collective-permute-start.2 = (bf16[1,128,2048]{2,1,0:T(8,128)(2,1)}, bf16[1,128,2048]{2,1,0:T(8,128)(2,1)}, u32[]{:S(2)}, u32[]{:S(2)}) collective-permute-start(bf16[1,128,2048]{2,1,0:T(8,128)(2,1)} %param.16), channel_id=1, source_target_pairs={{0,2},{2,4},{4,6},{6,8},{8,10},{10,12},{12,14},{14,16},{16,18},{18... | collective-permute-start | bytes 1572872 | tf_op jit(solution)/shard_map/ppermute | solution.py:30
  10.9 61.6 %collective-permute-start.3 = (bf16[1,128,2048]{2,1,0:T(8,128)(2,1)}, bf16[1,128,2048]{2,1,0:T(8,128)(2,1)}, u32[]{:S(2)}, u32[]{:S(2)}) collective-permute-start(bf16[1,128,2048]{2,1,0:T(8,128)(2,1)} %param.16), channel_id=1, source_target_pairs={{2,0},{4,2},{6,4},{8,6},{10,8},{12,10},{14,12},{16,14},{18,16},{20... | collective-permute-start | bytes 1572872 | tf_op jit(solution)/shard_map/ppermute | solution.py:30
  17.9 55.7 %collective-permute-start.4 = (bf16[1,128,2048]{2,1,0:T(8,128)(2,1)}, bf16[1,128,2048]{2,1,0:T(8,128)(2,1)S(1)}, u32[]{:S(2)}, u32[]{:S(2)}) collective-permute-start(bf16[1,128,2048]{2,1,0:T(8,128)(2,1)} %param.16), channel_id=1, source_target_pairs={{4,0},{6,2},{8,4},{10,6},{12,8},{14,10},{16,12},{18,14},{20,16},{2... | collective-permute-start | bytes 1572872 | tf_op jit(solution)/shard_map/ppermute | solution.py:30
  22.5 7.0 %all-to-all-start = ((bf16[2,1,128,2048]{2,3,1,0:T(8,128)(2,1)}), bf16[2,1,128,2048]{2,3,1,0:T(8,128)(2,1)S(1)}, u32[]{:S(2)}, u32[]{:S(2)}) async-start(bf16[2,1,128,2048]{2,3,1,0:T(8,128)(2,1)} %broadcast_in_dim.37), calls=%async_computation | async-start | bytes 2097152 | tf_op jit(solution)/shard_map/all_to_all | solution.py:11
  36.6 6.0 %copy-start.12 = (s32[128,4]{0,1:T(4,128)S(1)}, s32[128,4]{0,1:T(4,128)}, u32[]{:S(2)}) copy-start(s32[128,4]{0,1:T(4,128)} %param.21) | copy-start | bytes 6148
  36.6 6.0 %copy-start.13 = (s32[128,4]{0,1:T(4,128)S(1)}, s32[128,4]{0,1:T(4,128)}, u32[]{:S(2)}) copy-start(s32[128,4]{0,1:T(4,128)} %param.20) | copy-start | bytes 6148
  36.6 22.6 %copy-start.1 = (bf16[8,128,128]{2,1,0:T(8,128)(2,1)S(1)}, bf16[8,128,128]{2,1,0:T(8,128)(2,1)}, u32[]{:S(2)}) copy-start(bf16[8,128,128]{2,1,0:T(8,128)(2,1)} %param.27) | copy-start | bytes 786436
  59.2 5.5 %copy-start.4 = (bf16[1,128,2048]{2,1,0:T(8,128)(2,1)S(1)}, bf16[1,128,2048]{2,1,0:T(8,128)(2,1)}, u32[]{:S(2)}) copy-start(bf16[1,128,2048]{2,1,0:T(8,128)(2,1)} %param.16) | copy-start | bytes 1572868
  64.7 16.2 %collective-permute-start.5 = (bf16[1,128,2048]{2,1,0:T(8,128)(2,1)S(1)}, bf16[1,128,2048]{2,1,0:T(8,128)(2,1)S(1)}, u32[]{:S(2)}, u32[]{:S(2)}) collective-permute-start(bf16[1,128,2048]{2,1,0:T(8,128)(2,1)S(1)} %copy-done.4), channel_id=1, source_target_pairs={{6,0},{8,2},{10,4},{12,6},{14,8},{16,10},{18,12},{20,14},{22,16},{... | collective-permute-start | bytes 1572872 | tf_op jit(solution)/shard_map/ppermute | solution.py:30
  81.0 2.3 %copy-start.2 = (bf16[7,1,128,2048]{3,2,1,0:T(8,128)(2,1)}, bf16[7,1,128,2048]{3,2,1,0:T(8,128)(2,1)S(1)}, u32[]{:S(2)}) copy-start(bf16[7,1,128,2048]{3,2,1,0:T(8,128)(2,1)S(1)} %bitcast_dynamic-update-slice_fusion) | copy-start | bytes 11010052
  93.6 5.0 %copy-start.3 = (bf16[7,1,128,2048]{3,2,1,0:T(8,128)(2,1)S(1)}, bf16[7,1,128,2048]{3,2,1,0:T(8,128)(2,1)}, u32[]{:S(2)}) copy-start(bf16[7,1,128,2048]{3,2,1,0:T(8,128)(2,1)} %copy-done.2) | copy-start | bytes 11010052
  93.6 5.0 %copy-start.6 = (bf16[8,128,128]{2,1,0:T(8,128)(2,1)S(1)}, bf16[8,128,128]{2,1,0:T(8,128)(2,1)}, u32[]{:S(2)}) copy-start(bf16[8,128,128]{2,1,0:T(8,128)(2,1)} %param.25) | copy-start | bytes 786436
  98.7 1.2 %copy-start.5 = (f32[16,128,128,1]{2,1,3,0:T(8,128)S(1)}, f32[16,128,128,1]{2,1,3,0:T(8,128)}, u32[]{:S(2)}) copy-start(f32[16,128,128,1]{2,1,3,0:T(8,128)} %fusion.2) | copy-start | bytes 3145732
where the time goes:
time: 103 us; the launch traced here: 101 us
  starting transfers between devices  29.7 us (29%)
  local copies, waits for them, and re-layouts  24.9 us (24%)
  between operations  17.6 us (17%)
  matrix products  15.8 us (15%)
  waiting for transfers between devices  7.97 us (8%)
  blocking collectives  5.39 us (5%)
    ppermute x6, starting transfers between devices, shifted(): return lax.ppermute(block, axis, route)  24.4 us
    dot_general x2, matrix products, beta_apply(): jnp.einsum('rajmt,jmst->rajs', picked, tile_sets, preferred_element_type=...  11 us
    ppermute x6, waiting for transfers between devices, shifted(): return lax.ppermute(block, axis, route)  7.36 us
    gather x2, local copies, waits for them, and re-layouts, beta_apply(): picked = jnp.take(tiled, sources, axis=2)  6.15 us
    gather x2, local copies, waits for them, and re-layouts, beta_apply(): tile_sets = jnp.take(tile_table, kind_ids, axis=0)  6.15 us
    all_to_all x1, blocking collectives, from_everyone(): lax.all_to_all(jnp.broadcast_to(value[None], (count, *value.shape)), axis...  5.39 us
    all_to_all x1, starting transfers between devices, from_everyone(): lax.all_to_all(jnp.broadcast_to(value[None], (count, *value.shape)), axis...  5.23 us
    dot_general x7, matrix products, nearby_sum(): jnp.einsum('st,rtc->rsc', tile_one, picked, preferred_element_type=jnp.fl...  4.82 us
  transfers between devices with their start and end apart: 7, of which 2 were waited for; matrix products, arithmetic and copies ran while one was open for 25% of the time, Pallas kernels for 0%

commit v1 on v0

v1 whole, which is shorter than its diff:
```python
import functools

import jax
import jax.numpy as jnp
from jax import lax
from jax.experimental import pallas as pl
from jax.experimental.pallas import tpu as pltpu
from jax.sharding import Mesh, PartitionSpec as P

REACH = 3
RING = 4
TILE = 128
ANY = pl.BlockSpec(memory_space=pl.ANY)
SMEM = pl.BlockSpec(memory_space=pltpu.SMEM)
VMEM = pl.BlockSpec(memory_space=pltpu.VMEM)
LIMIT = 48 << 20


def cost(flops, moved):
    return pl.CostEstimate(flops=flops, bytes_accessed=moved, transcendentals=0)


def run_all(copies):
    for copy in copies:
        copy.start()
    for copy in copies:
        copy.wait()


def cut_kernel(place, whole, *rest):
    pieces, sems = rest[:RING], rest[RING]
    width = whole.shape[1] // RING
    copies = []
    for d in range(RING):
        quarter = lax.rem(place[0] + d, RING)
        cols = pl.ds(pl.multiple_of(quarter * width, width), width)
        copies.append(pltpu.make_async_copy(whole.at[:, cols], pieces[d], sems.at[d]))
    run_all(copies)


def cut(place, whole):
    rows, cols = whole.shape
    piece = jax.ShapeDtypeStruct((rows, cols // RING), whole.dtype)
    return pl.pallas_call(
        cut_kernel,
        out_shape=[piece] * RING,
        in_specs=[SMEM, ANY],
        out_specs=[ANY] * RING,
        scratch_shapes=[pltpu.SemaphoreType.DMA((RING,))],
        cost_estimate=cost(0, 4 * rows * cols),
        name="cut",
    )(place, whole)


def edge_kernel(place, p0, p1, p2, p3, up, down, sems):
    pieces = (p0, p1, p2, p3)
    for d in range(RING):
        block = lax.rem(place[0] - d + RING, RING)

        @pl.when(block > 0)
        def _():
            pltpu.make_async_copy(pieces[d], up.at[block - 1], sems.at[0, d]).start()

        @pl.when(block < RING - 1)
        def _():
            pltpu.make_async_copy(pieces[d], down.at[block], sems.at[1, d]).start()

    for d in range(RING):
        block = lax.rem(place[0] - d + RING, RING)

        @pl.when(block > 0)
        def _():
            pltpu.make_async_copy(pieces[d], up.at[block - 1], sems.at[0, d]).wait()

        @pl.when(block < RING - 1)
        def _():
            pltpu.make_async_copy(pieces[d], down.at[block], sems.at[1, d]).wait()


def edges(place, pieces):
    rows, cols = pieces[0].shape
    part = jax.ShapeDtypeStruct((REACH, rows, cols), pieces[0].dtype)
    return pl.pallas_call(
        edge_kernel,
        out_shape=[part] * 2,
        in_specs=[SMEM] + [ANY] * RING,
        out_specs=[ANY] * 2,
        scratch_shapes=[pltpu.SemaphoreType.DMA((2, RING))],
        cost_estimate=cost(0, 4 * REACH * rows * cols * 2),
        name="edges",
    )(place, *pieces)


def near_kernel(links, place, sources, kinds, p0, p1, p2, p3, above, below, table, *rest):
    outs, (held, sems) = rest[:RING], rest[RING:]
    copies = [
        pltpu.make_async_copy(above, held.at[pl.ds(0, REACH)], sems.at[4]),
        pltpu.make_async_copy(below, held.at[pl.ds(REACH + RING, REACH)], sems.at[5]),
    ]
    for d, piece in enumerate((p0, p1, p2, p3)):
        block = lax.rem(place[0] - d + RING, RING)
        copies.append(pltpu.make_async_copy(piece, held.at[REACH + block], sems.at[d]))
    run_all(copies)
    for d in range(RING):
        block = place[1] * RING + lax.rem(place[0] + d, RING)
        total = None
        for m in range(links):
            at = sources[block, m] - place[1] * RING + REACH
            term = jnp.dot(
                table[kinds[block, m]], held[at], preferred_element_type=jnp.float32
            )
            total = term if total is None else total + term
        outs[d][...] = total.astype(outs[d].dtype)


def near(place, sources, kinds, pieces, above, below, table, name):
    rows, cols = pieces[0].shape
    links = sources.shape[1]
    piece = jax.ShapeDtypeStruct((rows, cols), pieces[0].dtype)
    return pl.pallas_call(
        functools.partial(near_kernel, links),
        out_shape=[piece] * RING,
        in_specs=[SMEM] * 3 + [ANY] * (RING + 2) + [VMEM],
        out_specs=[VMEM] * RING,
        scratch_shapes=[
            pltpu.VMEM((RING + 2 * REACH, rows, cols), pieces[0].dtype),
            pltpu.SemaphoreType.DMA((RING + 2,)),
        ],
        cost_estimate=cost(2 * RING * links * rows * rows * cols, 14 * 2 * rows * cols),
        compiler_params=pltpu.CompilerParams(vmem_limit_bytes=LIMIT),
        name=name,
    )(place, sources, kinds, *pieces, above, below, table)


def far_kernel(count, links, slots, sources, kinds, *rest):
    pieces, table = rest[:count], rest[count]
    if len(rest) == count + 5:
        start, out, held, sems = rest[count + 1 :]
    else:
        start, (out, held, sems) = None, rest[count + 1 :]
    run_all(
        [
            pltpu.make_async_copy(pieces[n], held.at[slots[n]], sems.at[n])
            for n in range(count)
        ]
    )
    per_piece = held.shape[2] // TILE

    def body(tile, carry):
        picked, sets = [], []
        for m in range(links):
            source = sources[tile, m]
            cols = pl.ds(pl.multiple_of(lax.rem(source, per_piece) * TILE, TILE), TILE)
            picked.append(held[lax.div(source, per_piece), :, cols])
            sets.append(table[kinds[tile, m]])
        total = lax.dot_general(
            jnp.concatenate(picked, 1),
            jnp.concatenate(sets, 1),
            (((1,), (1,)), ((), ())),
            preferred_element_type=jnp.float32,
        )
        cols = pl.ds(pl.multiple_of(tile * TILE, TILE), TILE)
        if start is not None:
            total = total + start[:, cols]
        out[:, cols] = total
        return carry

    lax.fori_loop(0, out.shape[1] // TILE, body, 0, unroll=2)


def far(slots, sources, kinds, pieces, table, start, name):
    rows, cols = pieces[0].shape
    tiles, links = sources.shape
    count = len(pieces)
    extra = [] if start is None else [start]
    return pl.pallas_call(
        functools.partial(far_kernel, count, links),
        out_shape=jax.ShapeDtypeStruct((rows, tiles * TILE), jnp.float32),
        in_specs=[SMEM] * 3 + [ANY] * count + [VMEM] * (1 + len(extra)),
        out_specs=VMEM,
        scratch_shapes=[
            pltpu.VMEM((count, rows, cols), pieces[0].dtype),
            pltpu.SemaphoreType.DMA((count,)),
        ],
        cost_estimate=cost(2 * tiles * links * rows * TILE * TILE, 6 * rows * cols * count),
        compiler_params=pltpu.CompilerParams(vmem_limit_bytes=LIMIT),
        name=name,
    )(slots, sources, kinds, *pieces, table, *extra)


def last_kernel(place, start, p0, p1, p2, p3, out):
    width = p0.shape[1]
    for d, piece in enumerate((p0, p1, p2, p3)):
        quarter = lax.rem(place[0] - d + RING, RING)
        cols = pl.ds(pl.multiple_of(quarter * width, width), width)
        out[:, cols] = (start[:, cols] + piece[...].astype(jnp.float32)).astype(out.dtype)


def last(place, start, pieces):
    rows, cols = start.shape
    return pl.pallas_call(
        last_kernel,
        out_shape=jax.ShapeDtypeStruct((rows, cols), pieces[0].dtype),
        in_specs=[SMEM] + [VMEM] * (1 + RING),
        out_specs=VMEM,
        cost_estimate=cost(rows * cols, 8 * rows * cols),
        compiler_params=pltpu.CompilerParams(vmem_limit_bytes=LIMIT),
        name="last",
    )(place, start, *pieces)


def around(value, axis, distance):
    count = lax.axis_size(axis)
    return lax.ppermute(value, axis, [(i, (i + distance) % count) for i in range(count)])


def along(value, axis, distance):
    count = lax.axis_size(axis)
    return lax.ppermute(
        value, axis, [(i, i + distance) for i in range(count) if 0 <= i + distance < count]
    )


def exchanged(pieces):
    return [pieces[0]] + [around(pieces[d], "ring", d) for d in range(1, RING)]


def local(
    coeffs,
    beta_list,
    beta_kind,
    opp_beta_kind,
    alpha_list,
    alpha_kind,
    opp_list,
    opp_kind,
    beta_table,
    alpha_table,
    opp_alpha_table,
    opp_beta_table,
):
    own = coeffs[0]
    spot = lax.axis_index("ring").astype(jnp.int32)
    row = lax.axis_index("row").astype(jnp.int32)
    core = lax.axis_index("beta").astype(jnp.int32)
    place = jnp.stack([spot, row])
    order = jnp.arange(RING, dtype=jnp.int32)
    quarters = lax.rem(spot - order + RING, RING)
    half_slots = jnp.concatenate([core * RING + quarters, (1 - core) * RING + quarters])

    pieces = exchanged(cut(place, own))
    other = around(own, "beta", 1)
    up, down = edges(place, pieces)
    above = along(up, "row", 1)
    below = along(down, "row", -1)
    same = far(
        jnp.stack([core, 1 - core]), beta_list, beta_kind, [own, other], beta_table, None, "same"
    )
    half = exchanged(
        near(place, opp_list, opp_kind, pieces, above, below, opp_alpha_table, "half")
    )
    alpha = exchanged(
        near(place, alpha_list, alpha_kind, pieces, above, below, alpha_table, "alpha")
    )
    half_other = [around(piece, "beta", 1) for piece in half]
    mixed = far(
        half_slots, beta_list, opp_beta_kind, half + half_other, opp_beta_table, same, "mixed"
    )
    return last(place, mixed, alpha)[None]


def solution(mesh):
    split = Mesh(
        mesh.devices.reshape(-1, RING, mesh.devices.shape[1]), ("row", "ring", "beta")
    )
    vector = P(None, ("row", "ring"), "beta")
    lists = P("beta", None)
    placed = (vector, lists, lists, lists) + (P(),) * 8
    return jax.shard_map(
        local, mesh=split, in_specs=placed, out_specs=vector, check_vma=False
    )
```

time: 103 us -> 111 us (1.078); the launches traced: 101 us -> 111 us
  Pallas kernels: 0 us -> 63.6 us
  local copies, waits for them, and re-layouts: 24.9 us -> 6.7 us
  between operations: 17.6 us -> 0.24 us
  matrix products: 15.8 us -> 0 us
  blocking collectives: 5.39 us -> 0 us
  waiting for transfers between devices: 7.97 us -> 9.78 us
    pallas_call x0 -> x7, Pallas kernels: none -> 63.6 us  [the longest x1 25.8 us: edges(): pl.pallas_call(edge_kernel, out_shape=[part] * 2, in_specs=[SMEM] + [ANY]...]
    dot_general x9 -> x0, matrix products: 15.8 us -> none  [the longest x2 11 us: beta_apply(): jnp.einsum('rajmt,jmst->rajs', picked, tile_sets, preferred_element_type=...]
    gather x4 -> x0, local copies, waits for them, and re-layouts: 12.3 us -> none  [the longest x2 6.15 us: beta_apply(): picked = jnp.take(tiled, sources, axis=2)]
    all_to_all x1 -> x0, blocking collectives: 5.39 us -> none  [from_everyone(): lax.all_to_all(jnp.broadcast_to(value[None], (count, *value.shape)), axis...]
    all_to_all x1 -> x0, starting transfers between devices: 5.23 us -> none  [from_everyone(): lax.all_to_all(jnp.broadcast_to(value[None], (count, *value.shape)), axis...]
    ppermute x6 -> x16, starting transfers between devices: 24.4 us -> 29.4 us  [the longest x14 19.7 us: around(): lax.ppermute(value, axis, [(i, (i + distance) % count) for i in range(cou...]
    broadcast_in_dim x6 -> x0, local copies, waits for them, and re-layouts: 2.71 us -> none  [the longest x3 2.45 us: from_everyone(): jnp.broadcast_to(value[None], (count, *value.shape))]
    ppermute x6 -> x16, waiting for transfers between devices: 7.36 us -> 9.78 us  [the longest x2 4.99 us: along(): lax.ppermute(value, axis, [(i, i + distance) for i in range(count) if 0 <...]
  transfers between devices with their start and end apart: 7 -> 16, of which waited for: 2 -> 4; matrix products, arithmetic and copies ran while one was open for 25% -> 1% of each run, Pallas kernels for 0% -> 17%
where the time goes in v1:
time: 111 us
  Pallas kernels  63.6 us (57%)
  starting transfers between devices  29.4 us (26%)
  waiting for transfers between devices  9.78 us (9%)
  local copies, waits for them, and re-layouts  6.7 us (6%)
    pallas_call x1, Pallas kernels, edges(): pl.pallas_call(edge_kernel, out_shape=[part] * 2, in_specs=[SMEM] + [ANY]...  25.8 us
    ppermute x14, starting transfers between devices, around(): lax.ppermute(value, axis, [(i, (i + distance) % count) for i in range(cou...  19.7 us
    pallas_call x1, Pallas kernels, cut(): pl.pallas_call(cut_kernel, out_shape=[piece] * RING, in_specs=[SMEM, ANY]...  17.8 us
    pallas_call x2, Pallas kernels, near(): pl.pallas_call(functools.partial(near_kernel, links), out_shape=[piece] *...  10.2 us
    ppermute x2, starting transfers between devices, along(): lax.ppermute(value, axis, [(i, i + distance) for i in range(count) if 0 <...  9.71 us
    pallas_call x2, Pallas kernels, far(): pl.pallas_call(functools.partial(far_kernel, count, links), out_shape=jax...  8.33 us
    unnamed x61, local copies, waits for them, and re-layouts  6.7 us
    ppermute x2, waiting for transfers between devices, along(): lax.ppermute(value, axis, [(i, i + distance) for i in range(count) if 0 <...  4.99 us
  transfers between devices with their start and end apart: 16, of which 4 were waited for; matrix products, arithmetic and copies ran while one was open for 1% of the time, Pallas kernels for 17%

profile of v1, /device:TPU:25, one launch (start us, length us, event | category | flops | bytes accessed | tf_op | source)
XLA Modules:
  0.0 110.6 jit_solution(2214864137537647423)
XLA Ops:
  0.7 17.8 %cut.1 = (bf16[128,512]{1,0:T(8,128)(2,1)}, bf16[128,512]{1,0:T(8,128)(2,1)}, bf16[128,512]{1,0:T(8,128)(2,1)}, bf16[128,512]{1,0:T(8,128)(2,1)}) custom-call(s32[2]{0:T(128)} %pad_add_fusion.place, bf16[128,2048]{1,0:T(8,128)(2,1)} %bitcast.6), custom_call_target="tpu_custom_call" | custom-call | bytes 1048576 | tf_op jit(solution)/shard_map/cut/pallas_call | solution.py:44
  18.5 1.3 %collective-permute-start = (bf16[128,512]{1,0:T(8,128)(2,1)}, bf16[128,512]{1,0:T(8,128)(2,1)S(1)}, u32[]{:S(2)}, u32[]{:S(2)}) collective-permute-start(bf16[128,512]{1,0:T(8,128)(2,1)} %get-tuple-element.20), channel_id=1, source_target_pairs={{0,2},{2,4},{4,6},{6,0},{1,3},{3,5},{5,7},{7,1},{8,10},{10,12},{12... | collective-permute-start | bytes 393224 | tf_op jit(solution)/shard_map/ppermute | solution.py:214
  19.8 2.5 %collective-permute-start.1 = (bf16[128,512]{1,0:T(8,128)(2,1)}, bf16[128,512]{1,0:T(8,128)(2,1)S(1)}, u32[]{:S(2)}, u32[]{:S(2)}) collective-permute-start(bf16[128,512]{1,0:T(8,128)(2,1)} %get-tuple-element.21), channel_id=1, source_target_pairs={{0,4},{2,6},{4,0},{6,2},{1,5},{3,7},{5,1},{7,3},{8,12},{10,14},{12... | collective-permute-start | bytes 393224 | tf_op jit(solution)/shard_map/ppermute | solution.py:214
  22.2 1.2 %collective-permute-start.2 = (bf16[128,512]{1,0:T(8,128)(2,1)}, bf16[128,512]{1,0:T(8,128)(2,1)S(1)}, u32[]{:S(2)}, u32[]{:S(2)}) collective-permute-start(bf16[128,512]{1,0:T(8,128)(2,1)} %get-tuple-element.22), channel_id=1, source_target_pairs={{0,6},{2,0},{4,2},{6,4},{1,7},{3,1},{5,3},{7,5},{8,14},{10,8},{12,... | collective-permute-start | bytes 393224 | tf_op jit(solution)/shard_map/ppermute | solution.py:214
  23.4 1.0 collective-permute-done.p1
  24.3 3.8 %collective-permute-done.1.p2 = bf16[128,512]{1,0:T(8,128)(2,1)S(1)} collective-permute-done((bf16[128,512]{1,0:T(8,128)(2,1)}, bf16[128,512]{1,0:T(8,128)(2,1)S(1)}, u32[]{:S(2)}, u32[]{:S(2)}) %collective-permute-start.1) | collective-permute-done | bytes 131104 | tf_op jit(solution)/shard_map/ppermute | solution.py:214
  28.9 25.8 %edges.1 = (bf16[3,128,512]{2,1,0:T(8,128)(2,1)}, bf16[3,128,512]{2,1,0:T(8,128)(2,1)}) custom-call(s32[2]{0:T(128)} %pad_add_fusion.place, bf16[128,512]{1,0:T(8,128)(2,1)} %get-tuple-element.19.p0, bf16[128,512]{1,0:T(8,128)(2,1)} %copy-done.2, bf16[128,512]{1,0:T(8,128)(2,1)} %copy-done.5, bf16[128,512]{1,0:T(8,128)(2,1)} %copy-done.8), custom_call_target="tpu_custom_call" | custom-call | bytes 1572864 | tf_op jit(solution)/shard_map/edges/pallas_call | solution.py:83
  54.7 3.7 %collective-permute-start.3 = (bf16[3,128,512]{2,1,0:T(8,128)(2,1)}, bf16[3,128,512]{2,1,0:T(8,128)(2,1)S(1)}, u32[]{:S(2)}, u32[]{:S(2)}) collective-permute-start(bf16[3,128,512]{2,1,0:T(8,128)(2,1)} %get-tuple-element.23), channel_id=1, source_target_pairs={{0,8},{8,16},{16,24},{24,32},{32,40},{40,48},{48,56},{56,64},{64,7... | collective-permute-start | bytes 1179656 | tf_op jit(solution)/shard_map/ppermute | solution.py:219
  58.4 6.0 %collective-permute-start.4 = (bf16[3,128,512]{2,1,0:T(8,128)(2,1)}, bf16[3,128,512]{2,1,0:T(8,128)(2,1)S(1)}, u32[]{:S(2)}, u32[]{:S(2)}) collective-permute-start(bf16[3,128,512]{2,1,0:T(8,128)(2,1)} %get-tuple-element.24), channel_id=1, source_target_pairs={{8,0},{16,8},{24,16},{32,24},{40,32},{48,40},{56,48},{64,56},{72,6... | collective-permute-start | bytes 1179656 | tf_op jit(solution)/shard_map/ppermute | solution.py:219
  64.4 1.9 %collective-permute-start.12 = (bf16[128,2048]{1,0:T(8,128)(2,1)S(1)}, bf16[128,2048]{1,0:T(8,128)(2,1)S(1)}, u32[]{:S(2)}, u32[]{:S(2)}) collective-permute-start(bf16[128,2048]{1,0:T(8,128)(2,1)S(1)} %bitcast.7), channel_id=1, source_target_pairs={{0,1},{1,0},{2,3},{3,2},{4,5},{5,4},{6,7},{7,6},{8,9},{9,8},{10,11... | collective-permute-start | bytes 1572872 | tf_op jit(solution)/shard_map/ppermute | solution.py:214
  66.6 4.0 %collective-permute-done.3.above = bf16[3,128,512]{2,1,0:T(8,128)(2,1)S(1)} collective-permute-done((bf16[3,128,512]{2,1,0:T(8,128)(2,1)}, bf16[3,128,512]{2,1,0:T(8,128)(2,1)S(1)}, u32[]{:S(2)}, u32[]{:S(2)}) %collective-permute-start.3) | collective-permute-done | bytes 393248 | tf_op jit(solution)/shard_map/ppermute | solution.py:219
  70.6 1.0 collective-permute-done.4.below
  72.5 0.9 copy-done.6
  74.3 5.0 %half.1 = (bf16[128,512]{1,0:T(8,128)(2,1)S(1)}, bf16[128,512]{1,0:T(8,128)(2,1)S(1)}, bf16[128,512]{1,0:T(8,128)(2,1)}, bf16[128,512]{1,0:T(8,128)(2,1)}) custom-call(s32[2]{0:T(128)S(1)} %copy-done.19, s32[128,3]{1,0:T(8,128)S(1)} %copy.13.sources, s32[128,3]{1,0:T(8,128)S(1)} %copy.14.kinds, bf16[128,512]{1,0:T(8,128)(2,1)S(1)} %copy-done.1, ...), custom_call_target="tpu_custom_call" | custom-call | flops 201326592 | bytes 1835008 | tf_op jit(solution)/shard_map/half/pallas_call | solution.py:120
  79.4 1.3 %collective-permute-start.5 = (bf16[128,512]{1,0:T(8,128)(2,1)S(1)}, bf16[128,512]{1,0:T(8,128)(2,1)S(1)}, u32[]{:S(2)}, u32[]{:S(2)}) collective-permute-start(bf16[128,512]{1,0:T(8,128)(2,1)S(1)} %get-tuple-element.26), channel_id=1, source_target_pairs={{0,2},{2,4},{4,6},{6,0},{1,3},{3,5},{5,7},{7,1},{8,10},{10,12},{12... | collective-permute-start | bytes 393224 | tf_op jit(solution)/shard_map/ppermute | solution.py:214
  81.0 2.4 %collective-permute-start.6 = (bf16[128,512]{1,0:T(8,128)(2,1)}, bf16[128,512]{1,0:T(8,128)(2,1)S(1)}, u32[]{:S(2)}, u32[]{:S(2)}) collective-permute-start(bf16[128,512]{1,0:T(8,128)(2,1)} %get-tuple-element.27), channel_id=1, source_target_pairs={{0,4},{2,6},{4,0},{6,2},{1,5},{3,7},{5,1},{7,3},{8,12},{10,14},{12... | collective-permute-start | bytes 393224 | tf_op jit(solution)/shard_map/ppermute | solution.py:214
  83.5 3.4 %collective-permute-start.8 = (bf16[128,512]{1,0:T(8,128)(2,1)S(1)}, bf16[128,512]{1,0:T(8,128)(2,1)S(1)}, u32[]{:S(2)}, u32[]{:S(2)}) collective-permute-start(bf16[128,512]{1,0:T(8,128)(2,1)S(1)} %get-tuple-element.25.rest_0_), channel_id=1, source_target_pairs={{0,1},{1,0},{2,3},{3,2},{4,5},{5,4},{6,7},{7,6},{8,9},{9,8},{10,11... | collective-permute-start | bytes 393224 | tf_op jit(solution)/shard_map/ppermute | solution.py:214
  86.9 1.9 %collective-permute-start.9 = (bf16[128,512]{1,0:T(8,128)(2,1)S(1)}, bf16[128,512]{1,0:T(8,128)(2,1)S(1)}, u32[]{:S(2)}, u32[]{:S(2)}) collective-permute-start(bf16[128,512]{1,0:T(8,128)(2,1)S(1)} %collective-permute-done.5.rest_1_), channel_id=1, source_target_pairs={{0,1},{1,0},{2,3},{3,2},{4,5},{5,4},{6,7},{7,6},{8,9},{9,8},{10,11... | collective-permute-start | bytes 393224 | tf_op jit(solution)/shard_map/ppermute | solution.py:214
  88.9 5.2 %alpha.1 = (bf16[128,512]{1,0:T(8,128)(2,1)S(1)}, bf16[128,512]{1,0:T(8,128)(2,1)}, bf16[128,512]{1,0:T(8,128)(2,1)}, bf16[128,512]{1,0:T(8,128)(2,1)}) custom-call(s32[2]{0:T(128)S(1)} %copy-done.19, s32[128,4]{1,0:T(8,128)S(1)} %copy.19.sources, s32[128,4]{1,0:T(8,128)S(1)} %copy.20.kinds, bf16[128,512]{1,0:T(8,128)(2,1)S(1)} %copy-done.1, ...), custom_call_target="tpu_custom_call" | custom-call | flops 268435456 | bytes 1835008 | tf_op jit(solution)/shard_map/alpha/pallas_call | solution.py:120
  94.8 0.9 collective-permute-start.14
  95.7 1.6 %collective-permute-start.15 = (bf16[128,512]{1,0:T(8,128)(2,1)}, bf16[128,512]{1,0:T(8,128)(2,1)S(1)}, u32[]{:S(2)}, u32[]{:S(2)}) collective-permute-start(bf16[128,512]{1,0:T(8,128)(2,1)} %get-tuple-element.32), channel_id=1, source_target_pairs={{0,6},{2,0},{4,2},{6,4},{1,7},{3,1},{5,3},{7,5},{8,14},{10,8},{12,... | collective-permute-start | bytes 393224 | tf_op jit(solution)/shard_map/ppermute | solution.py:214
  100.7 3.5 %same.1.rest_9_ = f32[128,2048]{1,0:T(8,128)S(1)} custom-call(s32[2]{0:T(128)S(1)} %pad_add_fusion.2.slots, s32[16,8]{1,0:T(8,128)S(1)} %copy.17.sources, s32[16,8]{1,0:T(8,128)S(1)} %copy.16.kinds, bf16[128,2048]{1,0:T(8,128)(2,1)S(1)} %bitcast.8, bf16[128,2048]{1,0:T(8,128)(2,1)S(1)} %collective-permute-done.12.rest_1_, bf16[8,128,128]{2,1,0:T(8,128)(2,1)S(1)} %copy-done.14), custom_call_target="tpu_custom_call" | custom-call | flops 536870912 | bytes 3145728 | tf_op jit(solution)/shard_map/same/pallas_call | solution.py:176
  104.2 4.8 %mixed.1.start = f32[128,2048]{1,0:T(8,128)S(1)} custom-call(s32[8]{0:T(128)S(1)} %pad_add_fusion.1.slots, s32[16,8]{1,0:T(8,128)S(1)} %copy.17.sources, s32[16,8]{1,0:T(8,128)S(1)} %copy.18.kinds, bf16[128,512]{1,0:T(8,128)(2,1)S(1)} %get-tuple-element.25.rest_0_, bf16[128,512]{1,0:T(8,128)(2,1)S(1)} %collective-permute-done.5.rest_1_, ...), custom_call_target="tpu_custom_call" | custom-call | flops 536870912 | bytes 3145728 | tf_op jit(solution)/shard_map/mixed/pallas_call | solution.py:176
  109.1 1.5 %last.1 = bf16[128,2048]{1,0:T(8,128)(2,1)} custom-call(s32[2]{0:T(128)S(1)} %copy-done.19, f32[128,2048]{1,0:T(8,128)S(1)} %mixed.1.start, bf16[128,512]{1,0:T(8,128)(2,1)S(1)} %get-tuple-element.29.p0, bf16[128,512]{1,0:T(8,128)(2,1)S(1)} %collective-permute-done.13.p1, bf16[128,512]{1,0:T(8,128)(2,1)S(1)} %collective-permute-done.14.p2, ...), custom_call_target="tpu_custom_call" | custom-call | flops 262144 | bytes 2097152 | tf_op jit(solution)/shard_map/last/pallas_call | solution.py:201
  (80 shorter events, 8.0 us)
Async XLA Ops:
  0.7 63.8 %copy-start = (bf16[1,128,2048]{2,1,0:T(8,128)(2,1)S(1)}, bf16[1,128,2048]{2,1,0:T(8,128)(2,1)}, u32[]{:S(2)}) copy-start(bf16[1,128,2048]{2,1,0:T(8,128)(2,1)} %param.12) | copy-start | bytes 1572868
  18.5 5.9 %collective-permute-start = (bf16[128,512]{1,0:T(8,128)(2,1)}, bf16[128,512]{1,0:T(8,128)(2,1)S(1)}, u32[]{:S(2)}, u32[]{:S(2)}) collective-permute-start(bf16[128,512]{1,0:T(8,128)(2,1)} %get-tuple-element.20), channel_id=1, source_target_pairs={{0,2},{2,4},{4,6},{6,0},{1,3},{3,5},{5,7},{7,1},{8,10},{10,12},{12... | collective-permute-start | bytes 393224 | tf_op jit(solution)/shard_map/ppermute | solution.py:214
  19.8 8.4 %collective-permute-start.1 = (bf16[128,512]{1,0:T(8,128)(2,1)}, bf16[128,512]{1,0:T(8,128)(2,1)S(1)}, u32[]{:S(2)}, u32[]{:S(2)}) collective-permute-start(bf16[128,512]{1,0:T(8,128)(2,1)} %get-tuple-element.21), channel_id=1, source_target_pairs={{0,4},{2,6},{4,0},{6,2},{1,5},{3,7},{5,1},{7,3},{8,12},{10,14},{12... | collective-permute-start | bytes 393224 | tf_op jit(solution)/shard_map/ppermute | solution.py:214
  22.2 5.9 %collective-permute-start.2 = (bf16[128,512]{1,0:T(8,128)(2,1)}, bf16[128,512]{1,0:T(8,128)(2,1)S(1)}, u32[]{:S(2)}, u32[]{:S(2)}) collective-permute-start(bf16[128,512]{1,0:T(8,128)(2,1)} %get-tuple-element.22), channel_id=1, source_target_pairs={{0,6},{2,0},{4,2},{6,4},{1,7},{3,1},{5,3},{7,5},{8,14},{10,8},{12,... | collective-permute-start | bytes 393224 | tf_op jit(solution)/shard_map/ppermute | solution.py:214
  28.9 37.5 %copy-start.23 = (s32[128,3]{0,1:T(4,128)S(1)}, s32[128,3]{0,1:T(4,128)}, u32[]{:S(2)}) copy-start(s32[128,3]{0,1:T(4,128)} %param.18) | copy-start | bytes 4612
  28.9 37.6 %copy-start.24 = (s32[128,3]{0,1:T(4,128)S(1)}, s32[128,3]{0,1:T(4,128)}, u32[]{:S(2)}) copy-start(s32[128,3]{0,1:T(4,128)} %param.19) | copy-start | bytes 4612
  28.9 42.7 %copy-start.11 = (bf16[8,128,128]{2,1,0:T(8,128)(2,1)S(1)}, bf16[8,128,128]{2,1,0:T(8,128)(2,1)}, u32[]{:S(2)}) copy-start(bf16[8,128,128]{2,1,0:T(8,128)(2,1)} %table.2) | copy-start | bytes 786436
  54.7 16.9 %copy-start.1 = (bf16[128,512]{1,0:T(8,128)(2,1)S(1)}, bf16[128,512]{1,0:T(8,128)(2,1)}, u32[]{:S(2)}) copy-start(bf16[128,512]{1,0:T(8,128)(2,1)} %get-tuple-element.19.p0) | copy-start | bytes 393220
  54.7 15.9 %collective-permute-start.3 = (bf16[3,128,512]{2,1,0:T(8,128)(2,1)}, bf16[3,128,512]{2,1,0:T(8,128)(2,1)S(1)}, u32[]{:S(2)}, u32[]{:S(2)}) collective-permute-start(bf16[3,128,512]{2,1,0:T(8,128)(2,1)} %get-tuple-element.23), channel_id=1, source_target_pairs={{0,8},{8,16},{16,24},{24,32},{32,40},{40,48},{48,56},{56,64},{64,7... | collective-permute-start | bytes 1179656 | tf_op jit(solution)/shard_map/ppermute | solution.py:219
  58.4 13.2 %collective-permute-start.4 = (bf16[3,128,512]{2,1,0:T(8,128)(2,1)}, bf16[3,128,512]{2,1,0:T(8,128)(2,1)S(1)}, u32[]{:S(2)}, u32[]{:S(2)}) collective-permute-start(bf16[3,128,512]{2,1,0:T(8,128)(2,1)} %get-tuple-element.24), channel_id=1, source_target_pairs={{8,0},{16,8},{24,16},{32,24},{40,32},{48,40},{56,48},{64,56},{72,6... | collective-permute-start | bytes 1179656 | tf_op jit(solution)/shard_map/ppermute | solution.py:219
  64.4 29.7 %collective-permute-start.12 = (bf16[128,2048]{1,0:T(8,128)(2,1)S(1)}, bf16[128,2048]{1,0:T(8,128)(2,1)S(1)}, u32[]{:S(2)}, u32[]{:S(2)}) collective-permute-start(bf16[128,2048]{1,0:T(8,128)(2,1)S(1)} %bitcast.7), channel_id=1, source_target_pairs={{0,1},{1,0},{2,3},{3,2},{4,5},{5,4},{6,7},{7,6},{8,9},{9,8},{10,11... | collective-permute-start | bytes 1572872 | tf_op jit(solution)/shard_map/ppermute | solution.py:214
  74.3 14.6 %copy-start.7 = (bf16[128,512]{1,0:T(8,128)(2,1)S(1)}, bf16[128,512]{1,0:T(8,128)(2,1)}, u32[]{:S(2)}) copy-start(bf16[128,512]{1,0:T(8,128)(2,1)} %copy-done.5) | copy-start | bytes 393220
  74.3 14.6 %copy-start.10 = (bf16[128,512]{1,0:T(8,128)(2,1)S(1)}, bf16[128,512]{1,0:T(8,128)(2,1)}, u32[]{:S(2)}) copy-start(bf16[128,512]{1,0:T(8,128)(2,1)} %copy-done.8) | copy-start | bytes 393220
  74.3 14.6 %copy-start.12 = (bf16[8,128,128]{2,1,0:T(8,128)(2,1)S(1)}, bf16[8,128,128]{2,1,0:T(8,128)(2,1)}, u32[]{:S(2)}) copy-start(bf16[8,128,128]{2,1,0:T(8,128)(2,1)} %table.3) | copy-start | bytes 786436
  79.4 7.5 %collective-permute-start.5 = (bf16[128,512]{1,0:T(8,128)(2,1)S(1)}, bf16[128,512]{1,0:T(8,128)(2,1)S(1)}, u32[]{:S(2)}, u32[]{:S(2)}) collective-permute-start(bf16[128,512]{1,0:T(8,128)(2,1)S(1)} %get-tuple-element.26), channel_id=1, source_target_pairs={{0,2},{2,4},{4,6},{6,0},{1,3},{3,5},{5,7},{7,1},{8,10},{10,12},{12... | collective-permute-start | bytes 393224 | tf_op jit(solution)/shard_map/ppermute | solution.py:214
  81.0 13.8 %collective-permute-start.6 = (bf16[128,512]{1,0:T(8,128)(2,1)}, bf16[128,512]{1,0:T(8,128)(2,1)S(1)}, u32[]{:S(2)}, u32[]{:S(2)}) collective-permute-start(bf16[128,512]{1,0:T(8,128)(2,1)} %get-tuple-element.27), channel_id=1, source_target_pairs={{0,4},{2,6},{4,0},{6,2},{1,5},{3,7},{5,1},{7,3},{8,12},{10,14},{12... | collective-permute-start | bytes 393224 | tf_op jit(solution)/shard_map/ppermute | solution.py:214
  83.3 12.4 %collective-permute-start.7 = (bf16[128,512]{1,0:T(8,128)(2,1)}, bf16[128,512]{1,0:T(8,128)(2,1)}, u32[]{:S(2)}, u32[]{:S(2)}) collective-permute-start(bf16[128,512]{1,0:T(8,128)(2,1)} %get-tuple-element.28), channel_id=1, source_target_pairs={{0,6},{2,0},{4,2},{6,4},{1,7},{3,1},{5,3},{7,5},{8,14},{10,8},{12,... | collective-permute-start | bytes 393224 | tf_op jit(solution)/shard_map/ppermute | solution.py:214
  83.5 13.8 %collective-permute-start.8 = (bf16[128,512]{1,0:T(8,128)(2,1)S(1)}, bf16[128,512]{1,0:T(8,128)(2,1)S(1)}, u32[]{:S(2)}, u32[]{:S(2)}) collective-permute-start(bf16[128,512]{1,0:T(8,128)(2,1)S(1)} %get-tuple-element.25.rest_0_), channel_id=1, source_target_pairs={{0,1},{1,0},{2,3},{3,2},{4,5},{5,4},{6,7},{7,6},{8,9},{9,8},{10,11... | collective-permute-start | bytes 393224 | tf_op jit(solution)/shard_map/ppermute | solution.py:214
  86.9 11.6 %collective-permute-start.9 = (bf16[128,512]{1,0:T(8,128)(2,1)S(1)}, bf16[128,512]{1,0:T(8,128)(2,1)S(1)}, u32[]{:S(2)}, u32[]{:S(2)}) collective-permute-start(bf16[128,512]{1,0:T(8,128)(2,1)S(1)} %collective-permute-done.5.rest_1_), channel_id=1, source_target_pairs={{0,1},{1,0},{2,3},{3,2},{4,5},{5,4},{6,7},{7,6},{8,9},{9,8},{10,11... | collective-permute-start | bytes 393224 | tf_op jit(solution)/shard_map/ppermute | solution.py:214
  94.1 15.0 %collective-permute-start.13 = (bf16[128,512]{1,0:T(8,128)(2,1)}, bf16[128,512]{1,0:T(8,128)(2,1)S(1)}, u32[]{:S(2)}, u32[]{:S(2)}) collective-permute-start(bf16[128,512]{1,0:T(8,128)(2,1)} %get-tuple-element.30), channel_id=1, source_target_pairs={{0,2},{2,4},{4,6},{6,0},{1,3},{3,5},{5,7},{7,1},{8,10},{10,12},{12... | collective-permute-start | bytes 393224 | tf_op jit(solution)/shard_map/ppermute | solution.py:214
  94.8 14.4 %collective-permute-start.14 = (bf16[128,512]{1,0:T(8,128)(2,1)}, bf16[128,512]{1,0:T(8,128)(2,1)S(1)}, u32[]{:S(2)}, u32[]{:S(2)}) collective-permute-start(bf16[128,512]{1,0:T(8,128)(2,1)} %get-tuple-element.31), channel_id=1, source_target_pairs={{0,4},{2,6},{4,0},{6,2},{1,5},{3,7},{5,1},{7,3},{8,12},{10,14},{12... | collective-permute-start | bytes 393224 | tf_op jit(solution)/shard_map/ppermute | solution.py:214
  95.7 13.4 %collective-permute-start.15 = (bf16[128,512]{1,0:T(8,128)(2,1)}, bf16[128,512]{1,0:T(8,128)(2,1)S(1)}, u32[]{:S(2)}, u32[]{:S(2)}) collective-permute-start(bf16[128,512]{1,0:T(8,128)(2,1)} %get-tuple-element.32), channel_id=1, source_target_pairs={{0,6},{2,0},{4,2},{6,4},{1,7},{3,1},{5,3},{7,5},{8,14},{10,8},{12,... | collective-permute-start | bytes 393224 | tf_op jit(solution)/shard_map/ppermute | solution.py:214
  97.9 6.3 %collective-permute-start.10 = (bf16[128,512]{1,0:T(8,128)(2,1)S(1)}, bf16[128,512]{1,0:T(8,128)(2,1)S(1)}, u32[]{:S(2)}, u32[]{:S(2)}) collective-permute-start(bf16[128,512]{1,0:T(8,128)(2,1)S(1)} %collective-permute-done.6.rest_2_), channel_id=1, source_target_pairs={{0,1},{1,0},{2,3},{3,2},{4,5},{5,4},{6,7},{7,6},{8,9},{9,8},{10,11... | collective-permute-start | bytes 393224 | tf_op jit(solution)/shard_map/ppermute | solution.py:214
  99.2 5.0 %collective-permute-start.11 = (bf16[128,512]{1,0:T(8,128)(2,1)}, bf16[128,512]{1,0:T(8,128)(2,1)S(1)}, u32[]{:S(2)}, u32[]{:S(2)}) collective-permute-start(bf16[128,512]{1,0:T(8,128)(2,1)} %collective-permute-done.7.rest_3_), channel_id=1, source_target_pairs={{0,1},{1,0},{2,3},{3,2},{4,5},{5,4},{6,7},{7,6},{8,9},{9,8},{10,11... | collective-permute-start | bytes 393224 | tf_op jit(solution)/shard_map/ppermute | solution.py:214
  (19 other events, 65.1 us)

commit v2 on v0

v2 whole, which is shorter than its diff:
```python
import functools

import jax
import jax.numpy as jnp
from jax import lax
from jax.experimental import pallas as pl
from jax.experimental.pallas import tpu as pltpu
from jax.sharding import Mesh, PartitionSpec as P

REACH = 3
RING = 4
TILE = 128
SMEM = pl.BlockSpec(memory_space=pltpu.SMEM)
ANY = pl.BlockSpec(memory_space=pl.ANY)
VMEM = pl.BlockSpec(memory_space=pltpu.VMEM)
LIMIT = 10 << 20
MARK = 1 << 20


def cost(flops, moved):
    return pl.CostEstimate(flops=flops, bytes_accessed=moved, transcendentals=0)


def cut_kernel(whole, *pieces):
    spot = lax.axis_index("ring")
    width = whole.shape[1] // RING
    for d in range(RING):
        quarter = lax.bitwise_xor(spot, d)
        cols = pl.ds(pl.multiple_of(quarter * width, width), width)
        pieces[d][...] = whole[:, cols]


def cut(whole):
    rows, cols = whole.shape
    piece = jax.ShapeDtypeStruct((rows, cols // RING), whole.dtype)
    return pl.pallas_call(
        cut_kernel,
        out_shape=[piece] * RING,
        in_specs=[VMEM],
        out_specs=[VMEM] * RING,
        cost_estimate=cost(0, 4 * rows * cols),
        compiler_params=pltpu.CompilerParams(vmem_limit_bytes=LIMIT),
        name="cut",
    )(whole)


def edge_kernel(p0, p1, p2, p3, even, odd):
    spot = lax.axis_index("ring")
    parity = lax.rem(lax.axis_index("row"), 2)
    for d, piece in enumerate((p0, p1, p2, p3)):
        block = lax.bitwise_xor(spot, d)
        for part, shift in ((even, 1 - parity), (odd, parity)):
            at = block - shift

            @pl.when((at >= 0) & (at < REACH))
            def _():
                part[at] = piece[...]


def edges(pieces):
    rows, cols = pieces[0].shape
    part = jax.ShapeDtypeStruct((REACH, rows, cols), pieces[0].dtype)
    return pl.pallas_call(
        edge_kernel,
        out_shape=[part] * 2,
        in_specs=[VMEM] * RING,
        out_specs=[VMEM] * 2,
        cost_estimate=cost(0, 4 * REACH * rows * cols * 2),
        compiler_params=pltpu.CompilerParams(vmem_limit_bytes=LIMIT),
        name="edges",
    )(*pieces)


def near_kernel(links, sources, kinds, p0, p1, p2, p3, even, odd, table, *rest):
    outs, held = rest[:RING], rest[RING]
    spot, row = lax.axis_index("ring"), lax.axis_index("row")
    parity = lax.rem(row, 2)
    for d, piece in enumerate((p0, p1, p2, p3)):
        held[RING + lax.bitwise_xor(spot, d)] = piece[...]
    for part, below in ((even, 1 - parity), (odd, parity)):
        base = below * 2 * RING + (1 - below)
        for n in range(REACH):
            held[base + n] = part[n]
    first = (row - 1) * RING
    for d in range(RING):
        target = lax.bitwise_xor(spot, d)
        tiles = [table[kinds[target, m]] for m in range(links)]
        picked = [held[sources[target, m] - first] for m in range(links)]
        total = jnp.dot(
            jnp.concatenate(tiles, 1),
            jnp.concatenate(picked, 0),
            preferred_element_type=jnp.float32,
        )
        outs[d][...] = total.astype(outs[d].dtype)


def near(sources, kinds, pieces, even, odd, table, name):
    rows, cols = pieces[0].shape
    links = sources.shape[1]
    piece = jax.ShapeDtypeStruct((rows, cols), pieces[0].dtype)
    return pl.pallas_call(
        functools.partial(near_kernel, links),
        out_shape=[piece] * RING,
        in_specs=[SMEM] * 2 + [VMEM] * (RING + 3),
        out_specs=[VMEM] * RING,
        scratch_shapes=[pltpu.VMEM((3 * RING, rows, cols), pieces[0].dtype)],
        cost_estimate=cost(0, rows * cols),
        compiler_params=pltpu.CompilerParams(vmem_limit_bytes=LIMIT),
        name=name,
    )(sources, kinds, *pieces, even, odd, table)


def beta_tile(held, table, sources, kinds, tile, links):
    per_piece = held.shape[2] // TILE
    picked, sets = [], []
    for m in range(links):
        source = sources[tile, m]
        cols = pl.ds(pl.multiple_of(lax.rem(source, per_piece) * TILE, TILE), TILE)
        picked.append(held[lax.div(source, per_piece), :, cols])
        sets.append(table[kinds[tile, m]])
    return jnp.dot(
        jnp.concatenate(picked, 1),
        jnp.concatenate(sets, 0),
        preferred_element_type=jnp.float32,
    )


def same_kernel(links, sources, kinds, own, other, table, opp_table, out, turned, held, flat):
    core = lax.axis_index("beta")
    held[core] = own[...]
    held[1 - core] = other[...]
    for kind in range(table.shape[0]):
        flat[kind] = table[kind].T
        turned[kind] = opp_table[kind].T

    def body(tile, carry):
        cols = pl.ds(pl.multiple_of(tile * TILE, TILE), TILE)
        out[:, cols] = beta_tile(held, flat, sources, kinds, tile, links)
        return carry

    lax.fori_loop(0, out.shape[1] // TILE, body, 0, unroll=4)


def same_part(sources, kinds, own, other, table, opp_table):
    rows, cols = own.shape
    return pl.pallas_call(
        functools.partial(same_kernel, sources.shape[1]),
        out_shape=[
            jax.ShapeDtypeStruct((rows, cols), jnp.float32),
            jax.ShapeDtypeStruct(opp_table.shape, opp_table.dtype),
        ],
        in_specs=[SMEM] * 2 + [VMEM] * 4,
        out_specs=[VMEM] * 2,
        scratch_shapes=[
            pltpu.VMEM((2, rows, cols), own.dtype),
            pltpu.VMEM(table.shape, table.dtype),
        ],
        cost_estimate=cost(0, rows * cols),
        compiler_params=pltpu.CompilerParams(vmem_limit_bytes=LIMIT),
        name="same",
    )(sources, kinds, own, other, table, opp_table)


def mixed_kernel(links, sources, kinds, table, start, mark, *rest):
    half, other, alpha = rest[:RING], rest[RING : 2 * RING], rest[2 * RING : 3 * RING]
    out, held, added = rest[3 * RING :]
    spot, core = lax.axis_index("ring"), lax.axis_index("beta")
    for d in range(RING):
        quarter = lax.bitwise_xor(spot, d)
        held[core * RING + quarter] = half[d][...]
        held[(1 - core) * RING + quarter] = other[d][...]
        added[quarter] = alpha[d][...]
    per_piece = held.shape[2] // TILE

    def body(tile, carry):
        cols = pl.ds(pl.multiple_of(tile * TILE, TILE), TILE)
        part = pl.ds(pl.multiple_of(lax.rem(tile, per_piece) * TILE, TILE), TILE)
        total = beta_tile(held, table, sources, kinds, tile, links) + start[:, cols]
        total = total + added[lax.div(tile, per_piece), :, part].astype(jnp.float32)
        out[:, cols] = total.astype(out.dtype)
        return carry

    lax.fori_loop(0, out.shape[1] // TILE, body, 0, unroll=4)


def mixed_part(sources, kinds, table, start, mark, half, other, alpha):
    rows, cols = start.shape
    kind = half[0].dtype
    return pl.pallas_call(
        functools.partial(mixed_kernel, sources.shape[1]),
        out_shape=jax.ShapeDtypeStruct((rows, cols), kind),
        in_specs=[SMEM] * 2 + [VMEM] * 2 + [ANY] + [VMEM] * (3 * RING),
        out_specs=VMEM,
        scratch_shapes=[
            pltpu.VMEM((2 * RING, rows, cols // RING), kind),
            pltpu.VMEM((RING, rows, cols // RING), kind),
        ],
        cost_estimate=cost(0, rows * cols),
        compiler_params=pltpu.CompilerParams(vmem_limit_bytes=LIMIT),
        name="mixed",
    )(sources, kinds, table, start, mark, *half, *other, *alpha)


def mark_kernel(*refs):
    refs[-1][...] = jnp.zeros_like(refs[-1])


def marked(pieces):
    return pl.pallas_call(
        mark_kernel,
        out_shape=jax.ShapeDtypeStruct((8, TILE), jnp.float32),
        in_specs=[ANY] * len(pieces),
        out_specs=VMEM,
        cost_estimate=cost(0, MARK),
        compiler_params=pltpu.CompilerParams(vmem_limit_bytes=LIMIT),
        name="mark",
    )(*pieces)


def swapped(value, axis, flip):
    return lax.ppermute(value, axis, [(i, i ^ flip) for i in range(lax.axis_size(axis))])


def exchanged(pieces):
    return [pieces[0]] + [swapped(pieces[d], "ring", d) for d in range(1, RING)]


def handed(value, parity):
    count = lax.axis_size("row")
    pairs = [(row, row + 1) for row in range(parity, count - 1, 2)]
    return lax.ppermute(value, "row", pairs + [(there, here) for here, there in pairs])


def local(
    coeffs,
    beta_list,
    beta_kind,
    opp_beta_kind,
    alpha_list,
    alpha_kind,
    opp_list,
    opp_kind,
    beta_table,
    alpha_table,
    opp_alpha_table,
    opp_beta_table,
):
    own = coeffs[0]
    row = lax.axis_index("row")

    def mine(lists):
        return lax.dynamic_slice_in_dim(lists, row * RING, RING, 0)

    pieces = exchanged(cut(own))
    other = swapped(own, "beta", 1)
    same, turned = same_part(
        beta_list, beta_kind, own, other, beta_table, opp_beta_table
    )
    even, odd = edges(pieces)
    even, odd = handed(even, 0), handed(odd, 1)
    even, odd, same = lax.optimization_barrier((even, odd, same))
    half = exchanged(near(mine(opp_list), mine(opp_kind), pieces, even, odd, opp_alpha_table, "half"))
    formed = near(mine(alpha_list), mine(alpha_kind), pieces, even, odd, alpha_table, "alpha")
    half, mark = lax.optimization_barrier((half, formed[0]))
    alpha = exchanged(formed)
    half_other = [swapped(piece, "beta", 1) for piece in half]
    mark = marked(alpha[1:])
    total = mixed_part(
        beta_list, opp_beta_kind, turned, same, mark, half, half_other, alpha
    )
    return total[None]


def solution(mesh):
    split = Mesh(
        mesh.devices.reshape(-1, RING, mesh.devices.shape[1]), ("row", "ring", "beta")
    )
    vector = P(None, ("row", "ring"), "beta")
    lists = P("beta", None)
    placed = (vector, lists, lists, lists) + (P(),) * 8
    return jax.shard_map(
        local, mesh=split, in_specs=placed, out_specs=vector, check_vma=False
    )
```

time: 103 us -> 53.4 us (0.52); the launches traced: 101 us -> 53.1 us
  local copies, waits for them, and re-layouts: 24.9 us -> 2.08 us
  between operations: 17.6 us -> 0.14 us
  matrix products: 15.8 us -> 0 us
  Pallas kernels: 0 us -> 11.7 us
  blocking collectives: 5.39 us -> 0 us
  waiting for transfers between devices: 7.97 us -> 10.6 us
    dot_general x9 -> x0, matrix products: 15.8 us -> none  [the longest x2 11 us: beta_apply(): jnp.einsum('rajmt,jmst->rajs', picked, tile_sets, preferred_element_type=...]
    gather x4 -> x0, local copies, waits for them, and re-layouts: 12.3 us -> none  [the longest x2 6.15 us: beta_apply(): picked = jnp.take(tiled, sources, axis=2)]
    pallas_call x0 -> x7, Pallas kernels: none -> 11.7 us  [the longest x1 3.53 us: mixed_part(): pl.pallas_call(functools.partial(mixed_kernel, sources.shape[1]), out_sha...]
    all_to_all x1 -> x0, blocking collectives: 5.39 us -> none  [from_everyone(): lax.all_to_all(jnp.broadcast_to(value[None], (count, *value.shape)), axis...]
    all_to_all x1 -> x0, starting transfers between devices: 5.23 us -> none  [from_everyone(): lax.all_to_all(jnp.broadcast_to(value[None], (count, *value.shape)), axis...]
    ppermute x6 -> x16, starting transfers between devices: 24.4 us -> 28.7 us  [the longest x14 20.3 us: swapped(): lax.ppermute(value, axis, [(i, i ^ flip) for i in range(lax.axis_size(axi...]
    ppermute x6 -> x16, waiting for transfers between devices: 7.36 us -> 10.6 us  [the longest x14 7.41 us: swapped(): lax.ppermute(value, axis, [(i, i ^ flip) for i in range(lax.axis_size(axi...]
    broadcast_in_dim x6 -> x0, local copies, waits for them, and re-layouts: 2.71 us -> none  [the longest x3 2.45 us: from_everyone(): jnp.broadcast_to(value[None], (count, *value.shape))]
  transfers between devices with their start and end apart: 7 -> 16, of which waited for: 2 -> 4; matrix products, arithmetic and copies ran while one was open for 25% -> 1% of each run, Pallas kernels for 0% -> 10%
where the time goes in v2:
time: 53.4 us; the launch traced here: 53.1 us
  starting transfers between devices  28.7 us (54%)
  Pallas kernels  11.7 us (22%)
  waiting for transfers between devices  10.6 us (20%)
  local copies, waits for them, and re-layouts  2.08 us (4%)
    ppermute x14, starting transfers between devices, swapped(): lax.ppermute(value, axis, [(i, i ^ flip) for i in range(lax.axis_size(axi...  20.3 us
    ppermute x2, starting transfers between devices, handed(): lax.ppermute(value, 'row', pairs + [(there, here) for here, there in pairs])  8.38 us
    ppermute x14, waiting for transfers between devices, swapped(): lax.ppermute(value, axis, [(i, i ^ flip) for i in range(lax.axis_size(axi...  7.41 us
    pallas_call x1, Pallas kernels, mixed_part(): pl.pallas_call(functools.partial(mixed_kernel, sources.shape[1]), out_sha...  3.53 us
    pallas_call x1, Pallas kernels, same_part(): pl.pallas_call(functools.partial(same_kernel, sources.shape[1]), out_shap...  3.19 us
    ppermute x2, waiting for transfers between devices, handed(): lax.ppermute(value, 'row', pairs + [(there, here) for here, there in pairs])  3.17 us
    pallas_call x2, Pallas kernels, near(): pl.pallas_call(functools.partial(near_kernel, links), out_shape=[piece] *...  2.91 us
    unnamed x33, local copies, waits for them, and re-layouts  1.93 us
  transfers between devices with their start and end apart: 16, of which 4 were waited for; matrix products, arithmetic and copies ran while one was open for 1% of the time, Pallas kernels for 10%

profile of v2, /device:TPU:25, one launch (start us, length us, event | category | flops | bytes accessed | tf_op | source)
XLA Modules:
  0.0 53.1 jit_solution(6973521299522546204)
XLA Ops:
  0.0 1.1 %cut.1 = (bf16[128,512]{1,0:T(8,128)(2,1)S(1)}, bf16[128,512]{1,0:T(8,128)(2,1)S(1)}, bf16[128,512]{1,0:T(8,128)(2,1)S(1)}, bf16[128,512]{1,0:T(8,128)(2,1)S(1)}) custom-call(bf16[128,2048]{1,0:T(8,128)(2,1)} %bitcast.own.whole), custom_call_target="tpu_custom_call" | custom-call | bytes 1048576 | tf_op jit(solution)/shard_map/cut/pallas_call | solution.py:36
  1.1 1.3 %collective-permute-start.1 = (bf16[128,512]{1,0:T(8,128)(2,1)S(1)}, bf16[128,512]{1,0:T(8,128)(2,1)S(1)}, u32[]{:S(2)}, u32[]{:S(2)}) collective-permute-start(bf16[128,512]{1,0:T(8,128)(2,1)S(1)} %get-tuple-element.30), channel_id=1, source_target_pairs={{0,2},{2,0},{4,6},{6,4},{1,3},{3,1},{5,7},{7,5},{8,10},{10,8},{12,... | collective-permute-start | bytes 393224 | tf_op jit(solution)/shard_map/ppermute | solution.py:221
  2.4 2.4 %collective-permute-start.2 = (bf16[128,512]{1,0:T(8,128)(2,1)S(1)}, bf16[128,512]{1,0:T(8,128)(2,1)S(1)}, u32[]{:S(2)}, u32[]{:S(2)}) collective-permute-start(bf16[128,512]{1,0:T(8,128)(2,1)S(1)} %get-tuple-element.31), channel_id=1, source_target_pairs={{0,4},{2,6},{4,0},{6,2},{1,5},{3,7},{5,1},{7,3},{8,12},{10,14},{12... | collective-permute-start | bytes 393224 | tf_op jit(solution)/shard_map/ppermute | solution.py:221
  5.0 1.5 %collective-permute-start = (bf16[128,2048]{1,0:T(8,128)(2,1)}, bf16[128,2048]{1,0:T(8,128)(2,1)S(1)}, u32[]{:S(2)}, u32[]{:S(2)}) collective-permute-start(bf16[128,2048]{1,0:T(8,128)(2,1)} %bitcast.own.whole), channel_id=1, source_target_pairs={{0,1},{1,0},{2,3},{3,2},{4,5},{5,4},{6,7},{7,6},{8,9},{9,8},{10,11... | collective-permute-start | bytes 1572872 | tf_op jit(solution)/shard_map/ppermute | solution.py:221
  6.5 4.0 %collective-permute-done.2.p2 = bf16[128,512]{1,0:T(8,128)(2,1)S(1)} collective-permute-done((bf16[128,512]{1,0:T(8,128)(2,1)S(1)}, bf16[128,512]{1,0:T(8,128)(2,1)S(1)}, u32[]{:S(2)}, u32[]{:S(2)}) %collective-permute-start.2) | collective-permute-done | bytes 131104 | tf_op jit(solution)/shard_map/ppermute | solution.py:221
  10.5 2.5 %collective-permute-done.3.p3 = bf16[128,512]{1,0:T(8,128)(2,1)S(1)} collective-permute-done((bf16[128,512]{1,0:T(8,128)(2,1)S(1)}, bf16[128,512]{1,0:T(8,128)(2,1)S(1)}, u32[]{:S(2)}, u32[]{:S(2)}) %collective-permute-start.3) | collective-permute-done | bytes 131104 | tf_op jit(solution)/shard_map/ppermute | solution.py:221
  13.1 0.9 %edges.1 = (bf16[3,128,512]{2,1,0:T(8,128)(2,1)}, bf16[3,128,512]{2,1,0:T(8,128)(2,1)}) custom-call(bf16[128,512]{1,0:T(8,128)(2,1)S(1)} %get-tuple-element.29.p0, bf16[128,512]{1,0:T(8,128)(2,1)S(1)} %collective-permute-done.1.p1, bf16[128,512]{1,0:T(8,128)(2,1)S(1)} %collective-permute-done.2.p2, bf16[128,512]{1,0:T(8,128)(2,1)S(1)} %collective-permute-done.3.p3), custom_call_target="tpu_custom_call" | custom-call | bytes 1572864 | tf_op jit(solution)/shard_map/edges/pallas_call | solution.py:63
  14.0 1.6 %collective-permute-start.4 = (bf16[3,128,512]{2,1,0:T(8,128)(2,1)}, bf16[3,128,512]{2,1,0:T(8,128)(2,1)S(1)}, u32[]{:S(2)}, u32[]{:S(2)}) collective-permute-start(bf16[3,128,512]{2,1,0:T(8,128)(2,1)} %get-tuple-element.33), channel_id=1, source_target_pairs={{0,8},{16,24},{32,40},{48,56},{64,72},{80,88},{96,104},{112,120},{... | collective-permute-start | bytes 1179656 | tf_op jit(solution)/shard_map/ppermute | solution.py:231
  15.7 6.7 %collective-permute-start.5 = (bf16[3,128,512]{2,1,0:T(8,128)(2,1)}, bf16[3,128,512]{2,1,0:T(8,128)(2,1)S(1)}, u32[]{:S(2)}, u32[]{:S(2)}) collective-permute-start(bf16[3,128,512]{2,1,0:T(8,128)(2,1)} %get-tuple-element.34), channel_id=1, source_target_pairs={{8,16},{24,32},{40,48},{56,64},{72,80},{88,96},{104,112},{120,128}... | collective-permute-start | bytes 1179656 | tf_op jit(solution)/shard_map/ppermute | solution.py:231
  22.5 0.6 %copy-done.7 = s32[16,8]{0,1:T(8,128)S(1)} copy-done((s32[16,8]{0,1:T(8,128)S(1)}, s32[16,8]{0,1:T(8,128)}, u32[]{:S(2)}) %copy-start.7) | copy-done | bytes 536
  23.2 0.7 %copy-done.10 = s32[128,3]{0,1:T(4,128)S(1)} copy-done((s32[128,3]{0,1:T(4,128)S(1)}, s32[128,3]{0,1:T(4,128)}, u32[]{:S(2)}) %copy-start.10) | copy-done | bytes 1560
  24.1 3.2 %same.1 = (f32[128,2048]{1,0:T(8,128)S(1)}, bf16[8,128,128]{2,1,0:T(8,128)(2,1)S(1)}) custom-call(s32[16,8]{1,0:T(8,128)S(1)} %copy.19.sources, s32[16,8]{1,0:T(8,128)S(1)} %copy.14.kinds, bf16[128,2048]{1,0:T(8,128)(2,1)} %bitcast.own.whole, bf16[128,2048]{1,0:T(8,128)(2,1)S(1)} %collective-permute-done.other, bf16[8,128,128]{2,1,0:T(8,128)(2,1)S(1)} %copy-done, ...), custom_call_target="tpu_custom_call" | custom-call | bytes 262144 | tf_op jit(solution)/shard_map/same/pallas_call | solution.py:146
  27.4 3.2 %collective-permute-done.5.odd = bf16[3,128,512]{2,1,0:T(8,128)(2,1)S(1)} collective-permute-done((bf16[3,128,512]{2,1,0:T(8,128)(2,1)}, bf16[3,128,512]{2,1,0:T(8,128)(2,1)S(1)}, u32[]{:S(2)}, u32[]{:S(2)}) %collective-permute-start.5) | collective-permute-done | bytes 393248 | tf_op jit(solution)/shard_map/ppermute | solution.py:231
  30.5 1.8 %half.1 = (bf16[128,512]{1,0:T(8,128)(2,1)S(1)}, bf16[128,512]{1,0:T(8,128)(2,1)}, bf16[128,512]{1,0:T(8,128)(2,1)}, bf16[128,512]{1,0:T(8,128)(2,1)}) custom-call(s32[4,3]{1,0:T(4,128)S(1)} %copy.23.sources, s32[4,3]{1,0:T(4,128)S(1)} %copy.24.kinds, bf16[128,512]{1,0:T(8,128)(2,1)S(1)} %get-tuple-element.29.p0, ...), custom_call_target="tpu_custom_call" | custom-call | bytes 65536 | tf_op jit(solution)/shard_map/half/pallas_call | solution.py:101
  32.4 1.2 %collective-permute-start.11 = (bf16[128,512]{1,0:T(8,128)(2,1)}, bf16[128,512]{1,0:T(8,128)(2,1)S(1)}, u32[]{:S(2)}, u32[]{:S(2)}) collective-permute-start(bf16[128,512]{1,0:T(8,128)(2,1)} %get-tuple-element.45), channel_id=1, source_target_pairs={{0,6},{2,4},{4,2},{6,0},{1,7},{3,5},{5,3},{7,1},{8,14},{10,12},{12... | collective-permute-start | bytes 393224 | tf_op jit(solution)/shard_map/ppermute | solution.py:221
  33.6 1.4 %collective-permute-start.9 = (bf16[128,512]{1,0:T(8,128)(2,1)}, bf16[128,512]{1,0:T(8,128)(2,1)S(1)}, u32[]{:S(2)}, u32[]{:S(2)}) collective-permute-start(bf16[128,512]{1,0:T(8,128)(2,1)} %get-tuple-element.43), channel_id=1, source_target_pairs={{0,2},{2,0},{4,6},{6,4},{1,3},{3,1},{5,7},{7,5},{8,10},{10,8},{12,... | collective-permute-start | bytes 393224 | tf_op jit(solution)/shard_map/ppermute | solution.py:221
  35.3 1.1 %alpha.1 = (bf16[128,512]{1,0:T(8,128)(2,1)S(1)}, bf16[128,512]{1,0:T(8,128)(2,1)S(1)}, bf16[128,512]{1,0:T(8,128)(2,1)S(1)}, bf16[128,512]{1,0:T(8,128)(2,1)S(1)}) custom-call(s32[4,4]{1,0:T(4,128)S(1)} %copy.21.sources, s32[4,4]{1,0:T(4,128)S(1)} %copy.22.kinds, bf16[128,512]{1,0:T(8,128)(2,1)S(1)} %get-tuple-element.29.p0, ...), custom_call_target="tpu_custom_call" | custom-call | bytes 65536 | tf_op jit(solution)/shard_map/alpha/pallas_call | solution.py:101
  36.6 2.1 %collective-permute-start.7 = (bf16[128,512]{1,0:T(8,128)(2,1)S(1)}, bf16[128,512]{1,0:T(8,128)(2,1)S(1)}, u32[]{:S(2)}, u32[]{:S(2)}) collective-permute-start(bf16[128,512]{1,0:T(8,128)(2,1)S(1)} %get-tuple-element.40), channel_id=1, source_target_pairs={{0,4},{2,6},{4,0},{6,2},{1,5},{3,7},{5,1},{7,3},{8,12},{10,14},{12... | collective-permute-start | bytes 393224 | tf_op jit(solution)/shard_map/ppermute | solution.py:221
  38.7 1.7 %collective-permute-start.8 = (bf16[128,512]{1,0:T(8,128)(2,1)S(1)}, bf16[128,512]{1,0:T(8,128)(2,1)S(1)}, u32[]{:S(2)}, u32[]{:S(2)}) collective-permute-start(bf16[128,512]{1,0:T(8,128)(2,1)S(1)} %get-tuple-element.41), channel_id=1, source_target_pairs={{0,6},{2,4},{4,2},{6,0},{1,7},{3,5},{5,3},{7,1},{8,14},{10,12},{12... | collective-permute-start | bytes 393224 | tf_op jit(solution)/shard_map/ppermute | solution.py:221
  40.4 3.8 %collective-permute-start.12 = (bf16[128,512]{1,0:T(8,128)(2,1)S(1)}, bf16[128,512]{1,0:T(8,128)(2,1)S(1)}, u32[]{:S(2)}, u32[]{:S(2)}) collective-permute-start(bf16[128,512]{1,0:T(8,128)(2,1)S(1)} %get-tuple-element.47.rest_0_), channel_id=1, source_target_pairs={{0,1},{1,0},{2,3},{3,2},{4,5},{5,4},{6,7},{7,6},{8,9},{9,8},{10,11... | collective-permute-start | bytes 393224 | tf_op jit(solution)/shard_map/ppermute | solution.py:221
  44.3 1.3 %collective-permute-start.14 = (bf16[128,512]{1,0:T(8,128)(2,1)S(1)}, bf16[128,512]{1,0:T(8,128)(2,1)S(1)}, u32[]{:S(2)}, u32[]{:S(2)}) collective-permute-start(bf16[128,512]{1,0:T(8,128)(2,1)S(1)} %collective-permute-done.10.rest_2_), channel_id=1, source_target_pairs={{0,1},{1,0},{2,3},{3,2},{4,5},{5,4},{6,7},{7,6},{8,9},{9,8},{10,11... | collective-permute-start | bytes 393224 | tf_op jit(solution)/shard_map/ppermute | solution.py:221
  45.7 3.0 %collective-permute-start.15 = (bf16[128,512]{1,0:T(8,128)(2,1)S(1)}, bf16[128,512]{1,0:T(8,128)(2,1)S(1)}, u32[]{:S(2)}, u32[]{:S(2)}) collective-permute-start(bf16[128,512]{1,0:T(8,128)(2,1)S(1)} %collective-permute-done.11.rest_3_), channel_id=1, source_target_pairs={{0,1},{1,0},{2,3},{3,2},{4,5},{5,4},{6,7},{7,6},{8,9},{9,8},{10,11... | collective-permute-start | bytes 393224 | tf_op jit(solution)/shard_map/ppermute | solution.py:221
  48.7 0.9 %collective-permute-done.15.rest_7_ = bf16[128,512]{1,0:T(8,128)(2,1)S(1)} collective-permute-done((bf16[128,512]{1,0:T(8,128)(2,1)S(1)}, bf16[128,512]{1,0:T(8,128)(2,1)S(1)}, u32[]{:S(2)}, u32[]{:S(2)}) %collective-permute-start.15) | collective-permute-done | bytes 131104 | tf_op jit(solution)/shard_map/ppermute | solution.py:221
  49.6 3.5 %mixed.1 = bf16[128,2048]{1,0:T(8,128)(2,1)} custom-call(s32[16,8]{1,0:T(8,128)S(1)} %copy.19.sources, s32[16,8]{1,0:T(8,128)S(1)} %copy.20.kinds, bf16[8,128,128]{2,1,0:T(8,128)(2,1)S(1)} %copy-done.5, f32[128,2048]{1,0:T(8,128)S(1)} %get-tuple-element.36.start, f32[8,128]{1,0:T(8,128)S(1)} %mark.1, bf16[128,512]{1,0:T(8,128)(2,1)S(1)} %get-tuple-element.47.rest_0_, ...), custom_call_target="tpu_custom_call" | custom-call | bytes 262144 | tf_op jit(solution)/shard_map/mixed/pallas_call | solution.py:189
  (50 shorter events, 1.3 us)
Async XLA Ops:
  1.1 5.5 %collective-permute-start.1 = (bf16[128,512]{1,0:T(8,128)(2,1)S(1)}, bf16[128,512]{1,0:T(8,128)(2,1)S(1)}, u32[]{:S(2)}, u32[]{:S(2)}) collective-permute-start(bf16[128,512]{1,0:T(8,128)(2,1)S(1)} %get-tuple-element.30), channel_id=1, source_target_pairs={{0,2},{2,0},{4,6},{6,4},{1,3},{3,1},{5,7},{7,5},{8,10},{10,8},{12,... | collective-permute-start | bytes 393224 | tf_op jit(solution)/shard_map/ppermute | solution.py:221
  2.4 8.2 %collective-permute-start.2 = (bf16[128,512]{1,0:T(8,128)(2,1)S(1)}, bf16[128,512]{1,0:T(8,128)(2,1)S(1)}, u32[]{:S(2)}, u32[]{:S(2)}) collective-permute-start(bf16[128,512]{1,0:T(8,128)(2,1)S(1)} %get-tuple-element.31), channel_id=1, source_target_pairs={{0,4},{2,6},{4,0},{6,2},{1,5},{3,7},{5,1},{7,3},{8,12},{10,14},{12... | collective-permute-start | bytes 393224 | tf_op jit(solution)/shard_map/ppermute | solution.py:221
  4.8 8.2 %collective-permute-start.3 = (bf16[128,512]{1,0:T(8,128)(2,1)S(1)}, bf16[128,512]{1,0:T(8,128)(2,1)S(1)}, u32[]{:S(2)}, u32[]{:S(2)}) collective-permute-start(bf16[128,512]{1,0:T(8,128)(2,1)S(1)} %get-tuple-element.32), channel_id=1, source_target_pairs={{0,6},{2,4},{4,2},{6,0},{1,7},{3,5},{5,3},{7,1},{8,14},{10,12},{12... | collective-permute-start | bytes 393224 | tf_op jit(solution)/shard_map/ppermute | solution.py:221
  5.0 19.1 %collective-permute-start = (bf16[128,2048]{1,0:T(8,128)(2,1)}, bf16[128,2048]{1,0:T(8,128)(2,1)S(1)}, u32[]{:S(2)}, u32[]{:S(2)}) collective-permute-start(bf16[128,2048]{1,0:T(8,128)(2,1)} %bitcast.own.whole), channel_id=1, source_target_pairs={{0,1},{1,0},{2,3},{3,2},{4,5},{5,4},{6,7},{7,6},{8,9},{9,8},{10,11... | collective-permute-start | bytes 1572872 | tf_op jit(solution)/shard_map/ppermute | solution.py:221
  13.0 11.1 %copy-start = (bf16[8,128,128]{2,1,0:T(8,128)(2,1)S(1)}, bf16[8,128,128]{2,1,0:T(8,128)(2,1)}, u32[]{:S(2)}) copy-start(bf16[8,128,128]{2,1,0:T(8,128)(2,1)} %table.3) | copy-start | bytes 786436
  13.1 11.1 %copy-start.1 = (bf16[8,128,128]{2,1,0:T(8,128)(2,1)S(1)}, bf16[8,128,128]{2,1,0:T(8,128)(2,1)}, u32[]{:S(2)}) copy-start(bf16[8,128,128]{2,1,0:T(8,128)(2,1)} %opp_table.1) | copy-start | bytes 786436
  14.0 8.4 %copy-start.6 = (s32[16,8]{0,1:T(8,128)S(1)}, s32[16,8]{0,1:T(8,128)}, u32[]{:S(2)}) copy-start(s32[16,8]{0,1:T(8,128)} %param.13) | copy-start | bytes 1540
  14.0 13.4 %collective-permute-start.4 = (bf16[3,128,512]{2,1,0:T(8,128)(2,1)}, bf16[3,128,512]{2,1,0:T(8,128)(2,1)S(1)}, u32[]{:S(2)}, u32[]{:S(2)}) collective-permute-start(bf16[3,128,512]{2,1,0:T(8,128)(2,1)} %get-tuple-element.33), channel_id=1, source_target_pairs={{0,8},{16,24},{32,40},{48,56},{64,72},{80,88},{96,104},{112,120},{... | collective-permute-start | bytes 1179656 | tf_op jit(solution)/shard_map/ppermute | solution.py:231
  15.7 14.9 %collective-permute-start.5 = (bf16[3,128,512]{2,1,0:T(8,128)(2,1)}, bf16[3,128,512]{2,1,0:T(8,128)(2,1)S(1)}, u32[]{:S(2)}, u32[]{:S(2)}) collective-permute-start(bf16[3,128,512]{2,1,0:T(8,128)(2,1)} %get-tuple-element.34), channel_id=1, source_target_pairs={{8,16},{24,32},{40,48},{56,64},{72,80},{88,96},{104,112},{120,128}... | collective-permute-start | bytes 1179656 | tf_op jit(solution)/shard_map/ppermute | solution.py:231
  24.1 6.4 %copy-start.2 = (bf16[8,128,128]{2,1,0:T(8,128)(2,1)S(1)}, bf16[8,128,128]{2,1,0:T(8,128)(2,1)}, u32[]{:S(2)}) copy-start(bf16[8,128,128]{2,1,0:T(8,128)(2,1)} %table.5) | copy-start | bytes 786436
  27.3 5.0 %copy-start.4 = (bf16[8,128,128]{2,1,0:T(8,128)(2,1)}, bf16[8,128,128]{2,1,0:T(8,128)(2,1)S(1)}, u32[]{:S(2)}) copy-start(bf16[8,128,128]{2,1,0:T(8,128)(2,1)S(1)} %get-tuple-element.28.table) | copy-start | bytes 786436
  30.5 4.8 %copy-start.3 = (bf16[8,128,128]{2,1,0:T(8,128)(2,1)S(1)}, bf16[8,128,128]{2,1,0:T(8,128)(2,1)}, u32[]{:S(2)}) copy-start(bf16[8,128,128]{2,1,0:T(8,128)(2,1)} %table.4) | copy-start | bytes 786436
  32.3 6.4 %collective-permute-start.10 = (bf16[128,512]{1,0:T(8,128)(2,1)}, bf16[128,512]{1,0:T(8,128)(2,1)S(1)}, u32[]{:S(2)}, u32[]{:S(2)}) collective-permute-start(bf16[128,512]{1,0:T(8,128)(2,1)} %get-tuple-element.44), channel_id=1, source_target_pairs={{0,4},{2,6},{4,0},{6,2},{1,5},{3,7},{5,1},{7,3},{8,12},{10,14},{12... | collective-permute-start | bytes 393224 | tf_op jit(solution)/shard_map/ppermute | solution.py:221
  32.4 8.0 %collective-permute-start.11 = (bf16[128,512]{1,0:T(8,128)(2,1)}, bf16[128,512]{1,0:T(8,128)(2,1)S(1)}, u32[]{:S(2)}, u32[]{:S(2)}) collective-permute-start(bf16[128,512]{1,0:T(8,128)(2,1)} %get-tuple-element.45), channel_id=1, source_target_pairs={{0,6},{2,4},{4,2},{6,0},{1,7},{3,5},{5,3},{7,1},{8,14},{10,12},{12... | collective-permute-start | bytes 393224 | tf_op jit(solution)/shard_map/ppermute | solution.py:221
  33.6 6.8 %collective-permute-start.9 = (bf16[128,512]{1,0:T(8,128)(2,1)}, bf16[128,512]{1,0:T(8,128)(2,1)S(1)}, u32[]{:S(2)}, u32[]{:S(2)}) collective-permute-start(bf16[128,512]{1,0:T(8,128)(2,1)} %get-tuple-element.43), channel_id=1, source_target_pairs={{0,2},{2,0},{4,6},{6,4},{1,3},{3,1},{5,7},{7,5},{8,10},{10,8},{12,... | collective-permute-start | bytes 393224 | tf_op jit(solution)/shard_map/ppermute | solution.py:221
  35.3 13.3 %copy-start.8 = (s32[16,8]{0,1:T(8,128)S(1)}, s32[16,8]{0,1:T(8,128)}, u32[]{:S(2)}) copy-start(s32[16,8]{0,1:T(8,128)} %param.15) | copy-start | bytes 1540
  36.5 13.1 %copy-start.5 = (bf16[8,128,128]{2,1,0:T(8,128)(2,1)S(1)}, bf16[8,128,128]{2,1,0:T(8,128)(2,1)}, u32[]{:S(2)}) copy-start(bf16[8,128,128]{2,1,0:T(8,128)(2,1)} %copy-done.4) | copy-start | bytes 786436
  36.5 7.9 %collective-permute-start.6 = (bf16[128,512]{1,0:T(8,128)(2,1)S(1)}, bf16[128,512]{1,0:T(8,128)(2,1)S(1)}, u32[]{:S(2)}, u32[]{:S(2)}) collective-permute-start(bf16[128,512]{1,0:T(8,128)(2,1)S(1)} %get-tuple-element.39), channel_id=1, source_target_pairs={{0,2},{2,0},{4,6},{6,4},{1,3},{3,1},{5,7},{7,5},{8,10},{10,8},{12,... | collective-permute-start | bytes 393224 | tf_op jit(solution)/shard_map/ppermute | solution.py:221
  36.6 9.0 %collective-permute-start.7 = (bf16[128,512]{1,0:T(8,128)(2,1)S(1)}, bf16[128,512]{1,0:T(8,128)(2,1)S(1)}, u32[]{:S(2)}, u32[]{:S(2)}) collective-permute-start(bf16[128,512]{1,0:T(8,128)(2,1)S(1)} %get-tuple-element.40), channel_id=1, source_target_pairs={{0,4},{2,6},{4,0},{6,2},{1,5},{3,7},{5,1},{7,3},{8,12},{10,14},{12... | collective-permute-start | bytes 393224 | tf_op jit(solution)/shard_map/ppermute | solution.py:221
  38.7 10.0 %collective-permute-start.8 = (bf16[128,512]{1,0:T(8,128)(2,1)S(1)}, bf16[128,512]{1,0:T(8,128)(2,1)S(1)}, u32[]{:S(2)}, u32[]{:S(2)}) collective-permute-start(bf16[128,512]{1,0:T(8,128)(2,1)S(1)} %get-tuple-element.41), channel_id=1, source_target_pairs={{0,6},{2,4},{4,2},{6,0},{1,7},{3,5},{5,3},{7,1},{8,14},{10,12},{12... | collective-permute-start | bytes 393224 | tf_op jit(solution)/shard_map/ppermute | solution.py:221
  40.4 8.3 %collective-permute-start.12 = (bf16[128,512]{1,0:T(8,128)(2,1)S(1)}, bf16[128,512]{1,0:T(8,128)(2,1)S(1)}, u32[]{:S(2)}, u32[]{:S(2)}) collective-permute-start(bf16[128,512]{1,0:T(8,128)(2,1)S(1)} %get-tuple-element.47.rest_0_), channel_id=1, source_target_pairs={{0,1},{1,0},{2,3},{3,2},{4,5},{5,4},{6,7},{7,6},{8,9},{9,8},{10,11... | collective-permute-start | bytes 393224 | tf_op jit(solution)/shard_map/ppermute | solution.py:221
  44.2 4.5 %collective-permute-start.13 = (bf16[128,512]{1,0:T(8,128)(2,1)S(1)}, bf16[128,512]{1,0:T(8,128)(2,1)S(1)}, u32[]{:S(2)}, u32[]{:S(2)}) collective-permute-start(bf16[128,512]{1,0:T(8,128)(2,1)S(1)} %collective-permute-done.9.rest_1_), channel_id=1, source_target_pairs={{0,1},{1,0},{2,3},{3,2},{4,5},{5,4},{6,7},{7,6},{8,9},{9,8},{10,11... | collective-permute-start | bytes 393224 | tf_op jit(solution)/shard_map/ppermute | solution.py:221
  44.3 4.4 %collective-permute-start.14 = (bf16[128,512]{1,0:T(8,128)(2,1)S(1)}, bf16[128,512]{1,0:T(8,128)(2,1)S(1)}, u32[]{:S(2)}, u32[]{:S(2)}) collective-permute-start(bf16[128,512]{1,0:T(8,128)(2,1)S(1)} %collective-permute-done.10.rest_2_), channel_id=1, source_target_pairs={{0,1},{1,0},{2,3},{3,2},{4,5},{5,4},{6,7},{7,6},{8,9},{9,8},{10,11... | collective-permute-start | bytes 393224 | tf_op jit(solution)/shard_map/ppermute | solution.py:221
  45.7 3.9 %collective-permute-start.15 = (bf16[128,512]{1,0:T(8,128)(2,1)S(1)}, bf16[128,512]{1,0:T(8,128)(2,1)S(1)}, u32[]{:S(2)}, u32[]{:S(2)}) collective-permute-start(bf16[128,512]{1,0:T(8,128)(2,1)S(1)} %collective-permute-done.11.rest_3_), channel_id=1, source_target_pairs={{0,1},{1,0},{2,3},{3,2},{4,5},{5,4},{6,7},{7,6},{8,9},{9,8},{10,11... | collective-permute-start | bytes 393224 | tf_op jit(solution)/shard_map/ppermute | solution.py:221
  (5 other events, 7.6 us)

commit v3 on v2

--- a/solution.py
+++ b/solution.py
@@ -44,7 +44,7 @@
     )(whole)
 
 
-def edge_kernel(p0, p1, p2, p3, even, odd):
+def edge_kernel(p0, p1, p3, p2, even, odd):
     spot = lax.axis_index("ring")
     parity = lax.rem(lax.axis_index("row"), 2)
     for d, piece in enumerate((p0, p1, p2, p3)):
@@ -68,7 +68,7 @@
         cost_estimate=cost(0, 4 * REACH * rows * cols * 2),
         compiler_params=pltpu.CompilerParams(vmem_limit_bytes=LIMIT),
         name="edges",
-    )(*pieces)
+    )(*[pieces[d] for d in (0, 1, 3, 2)])
 
 
 def near_kernel(links, sources, kinds, p0, p1, p2, p3, even, odd, table, *rest):
@@ -261,10 +261,12 @@
     even, odd, same = lax.optimization_barrier((even, odd, same))
     half = exchanged(near(mine(opp_list), mine(opp_kind), pieces, even, odd, opp_alpha_table, "half"))
     formed = near(mine(alpha_list), mine(alpha_kind), pieces, even, odd, alpha_table, "alpha")
+    half = [half[d] for d in (0, 2, 1, 3)]
     half, mark = lax.optimization_barrier((half, formed[0]))
+    half = [half[d] for d in (0, 2, 1, 3)]
     alpha = exchanged(formed)
     half_other = [swapped(piece, "beta", 1) for piece in half]
-    mark = marked(alpha[1:])
+    mark = marked([alpha[d] for d in (1, 3, 2)])
     total = mixed_part(
         beta_list, opp_beta_kind, turned, same, mark, half, half_other, alpha
     )

time: 53.4 us -> 48.8 us (0.914)
  waiting for transfers between devices: 10.6 us -> 7.74 us
  starting transfers between devices: 28.7 us -> 26.9 us
    ppermute x14, waiting for transfers between devices: 7.41 us -> 5.28 us  [swapped(): lax.ppermute(value, axis, [(i, i ^ flip) for i in range(lax.axis_size(axi...]
    ppermute x14, starting transfers between devices: 20.3 us -> 18.6 us  [swapped(): lax.ppermute(value, axis, [(i, i ^ flip) for i in range(lax.axis_size(axi...]
    ppermute x2, waiting for transfers between devices: 3.17 us -> 2.46 us  [handed(): lax.ppermute(value, 'row', pairs + [(there, here) for here, there in pairs])]
  transfers between devices with their start and end apart: 16 -> 16, of which waited for: 4 -> 4; matrix products, arithmetic and copies ran while one was open for 1% -> 2% of each run, Pallas kernels for 10% -> 11%
where the time goes in v3:
time: 48.8 us; the launch traced here: 48.6 us
  starting transfers between devices  26.9 us (55%)
  Pallas kernels  11.7 us (24%)
  waiting for transfers between devices  7.74 us (16%)
  local copies, waits for them, and re-layouts  2.08 us (4%)
    ppermute x14, starting transfers between devices, swapped(): lax.ppermute(value, axis, [(i, i ^ flip) for i in range(lax.axis_size(axi...  18.6 us
    ppermute x2, starting transfers between devices, handed(): lax.ppermute(value, 'row', pairs + [(there, here) for here, there in pairs])  8.38 us
    ppermute x14, waiting for transfers between devices, swapped(): lax.ppermute(value, axis, [(i, i ^ flip) for i in range(lax.axis_size(axi...  5.28 us
    pallas_call x1, Pallas kernels, mixed_part(): pl.pallas_call(functools.partial(mixed_kernel, sources.shape[1]), out_sha...  3.53 us
    pallas_call x1, Pallas kernels, same_part(): pl.pallas_call(functools.partial(same_kernel, sources.shape[1]), out_shap...  3.19 us
    pallas_call x2, Pallas kernels, near(): pl.pallas_call(functools.partial(near_kernel, links), out_shape=[piece] *...  2.91 us
    ppermute x2, waiting for transfers between devices, handed(): lax.ppermute(value, 'row', pairs + [(there, here) for here, there in pairs])  2.46 us
    unnamed x33, local copies, waits for them, and re-layouts  1.93 us
  transfers between devices with their start and end apart: 16, of which 4 were waited for; matrix products, arithmetic and copies ran while one was open for 2% of the time, Pallas kernels for 11%

profile of v3, /device:TPU:25, one launch (start us, length us, event | category | flops | bytes accessed | tf_op | source)
XLA Modules:
  0.0 48.6 jit_solution(1414744660404475820)
XLA Ops:
  0.0 1.1 %cut.1 = (bf16[128,512]{1,0:T(8,128)(2,1)S(1)}, bf16[128,512]{1,0:T(8,128)(2,1)S(1)}, bf16[128,512]{1,0:T(8,128)(2,1)S(1)}, bf16[128,512]{1,0:T(8,128)(2,1)S(1)}) custom-call(bf16[128,2048]{1,0:T(8,128)(2,1)} %bitcast.own.whole), custom_call_target="tpu_custom_call" | custom-call | bytes 1048576 | tf_op jit(solution)/shard_map/cut/pallas_call | solution.py:36
  1.1 1.3 %collective-permute-start.1 = (bf16[128,512]{1,0:T(8,128)(2,1)S(1)}, bf16[128,512]{1,0:T(8,128)(2,1)S(1)}, u32[]{:S(2)}, u32[]{:S(2)}) collective-permute-start(bf16[128,512]{1,0:T(8,128)(2,1)S(1)} %get-tuple-element.30), channel_id=1, source_target_pairs={{0,2},{2,0},{4,6},{6,4},{1,3},{3,1},{5,7},{7,5},{8,10},{10,8},{12,... | collective-permute-start | bytes 393224 | tf_op jit(solution)/shard_map/ppermute | solution.py:221
  2.4 1.8 %collective-permute-start.2 = (bf16[128,512]{1,0:T(8,128)(2,1)S(1)}, bf16[128,512]{1,0:T(8,128)(2,1)S(1)}, u32[]{:S(2)}, u32[]{:S(2)}) collective-permute-start(bf16[128,512]{1,0:T(8,128)(2,1)S(1)} %get-tuple-element.31), channel_id=1, source_target_pairs={{0,6},{2,4},{4,2},{6,0},{1,7},{3,5},{5,3},{7,1},{8,14},{10,12},{12... | collective-permute-start | bytes 393224 | tf_op jit(solution)/shard_map/ppermute | solution.py:221
  4.2 0.6 %collective-permute-start.3 = (bf16[128,512]{1,0:T(8,128)(2,1)S(1)}, bf16[128,512]{1,0:T(8,128)(2,1)S(1)}, u32[]{:S(2)}, u32[]{:S(2)}) collective-permute-start(bf16[128,512]{1,0:T(8,128)(2,1)S(1)} %get-tuple-element.32), channel_id=1, source_target_pairs={{0,4},{2,6},{4,0},{6,2},{1,5},{3,7},{5,1},{7,3},{8,12},{10,14},{12... | collective-permute-start | bytes 393224 | tf_op jit(solution)/shard_map/ppermute | solution.py:221
  4.8 1.2 %collective-permute-start = (bf16[128,2048]{1,0:T(8,128)(2,1)}, bf16[128,2048]{1,0:T(8,128)(2,1)S(1)}, u32[]{:S(2)}, u32[]{:S(2)}) collective-permute-start(bf16[128,2048]{1,0:T(8,128)(2,1)} %bitcast.own.whole), channel_id=1, source_target_pairs={{0,1},{1,0},{2,3},{3,2},{4,5},{5,4},{6,7},{7,6},{8,9},{9,8},{10,11... | collective-permute-start | bytes 1572872 | tf_op jit(solution)/shard_map/ppermute | solution.py:221
  6.1 1.3 %collective-permute-done.2.p3 = bf16[128,512]{1,0:T(8,128)(2,1)S(1)} collective-permute-done((bf16[128,512]{1,0:T(8,128)(2,1)S(1)}, bf16[128,512]{1,0:T(8,128)(2,1)S(1)}, u32[]{:S(2)}, u32[]{:S(2)}) %collective-permute-start.2) | collective-permute-done | bytes 131104 | tf_op jit(solution)/shard_map/ppermute | solution.py:221
  7.4 3.0 %collective-permute-done.3.p2 = bf16[128,512]{1,0:T(8,128)(2,1)S(1)} collective-permute-done((bf16[128,512]{1,0:T(8,128)(2,1)S(1)}, bf16[128,512]{1,0:T(8,128)(2,1)S(1)}, u32[]{:S(2)}, u32[]{:S(2)}) %collective-permute-start.3) | collective-permute-done | bytes 131104 | tf_op jit(solution)/shard_map/ppermute | solution.py:221
  10.4 0.9 %edges.1 = (bf16[3,128,512]{2,1,0:T(8,128)(2,1)}, bf16[3,128,512]{2,1,0:T(8,128)(2,1)}) custom-call(bf16[128,512]{1,0:T(8,128)(2,1)S(1)} %get-tuple-element.29.p0, bf16[128,512]{1,0:T(8,128)(2,1)S(1)} %collective-permute-done.1.p1, bf16[128,512]{1,0:T(8,128)(2,1)S(1)} %collective-permute-done.2.p3, bf16[128,512]{1,0:T(8,128)(2,1)S(1)} %collective-permute-done.3.p2), custom_call_target="tpu_custom_call" | custom-call | bytes 1572864 | tf_op jit(solution)/shard_map/edges/pallas_call | solution.py:63
  11.4 1.6 %collective-permute-start.4 = (bf16[3,128,512]{2,1,0:T(8,128)(2,1)}, bf16[3,128,512]{2,1,0:T(8,128)(2,1)S(1)}, u32[]{:S(2)}, u32[]{:S(2)}) collective-permute-start(bf16[3,128,512]{2,1,0:T(8,128)(2,1)} %get-tuple-element.33), channel_id=1, source_target_pairs={{0,8},{16,24},{32,40},{48,56},{64,72},{80,88},{96,104},{112,120},{... | collective-permute-start | bytes 1179656 | tf_op jit(solution)/shard_map/ppermute | solution.py:231
  13.0 6.7 %collective-permute-start.5 = (bf16[3,128,512]{2,1,0:T(8,128)(2,1)}, bf16[3,128,512]{2,1,0:T(8,128)(2,1)S(1)}, u32[]{:S(2)}, u32[]{:S(2)}) collective-permute-start(bf16[3,128,512]{2,1,0:T(8,128)(2,1)} %get-tuple-element.34), channel_id=1, source_target_pairs={{8,16},{24,32},{40,48},{56,64},{72,80},{88,96},{104,112},{120,128}... | collective-permute-start | bytes 1179656 | tf_op jit(solution)/shard_map/ppermute | solution.py:231
  19.9 0.6 %copy-done.7 = s32[16,8]{0,1:T(8,128)S(1)} copy-done((s32[16,8]{0,1:T(8,128)S(1)}, s32[16,8]{0,1:T(8,128)}, u32[]{:S(2)}) %copy-start.7) | copy-done | bytes 536
  20.6 0.7 %copy-done.10 = s32[128,3]{0,1:T(4,128)S(1)} copy-done((s32[128,3]{0,1:T(4,128)S(1)}, s32[128,3]{0,1:T(4,128)}, u32[]{:S(2)}) %copy-start.10) | copy-done | bytes 1560
  21.5 3.2 %same.1 = (f32[128,2048]{1,0:T(8,128)S(1)}, bf16[8,128,128]{2,1,0:T(8,128)(2,1)S(1)}) custom-call(s32[16,8]{1,0:T(8,128)S(1)} %copy.19.sources, s32[16,8]{1,0:T(8,128)S(1)} %copy.14.kinds, bf16[128,2048]{1,0:T(8,128)(2,1)} %bitcast.own.whole, bf16[128,2048]{1,0:T(8,128)(2,1)S(1)} %collective-permute-done.other, bf16[8,128,128]{2,1,0:T(8,128)(2,1)S(1)} %copy-done, ...), custom_call_target="tpu_custom_call" | custom-call | bytes 262144 | tf_op jit(solution)/shard_map/same/pallas_call | solution.py:146
  24.8 2.5 %collective-permute-done.5.odd = bf16[3,128,512]{2,1,0:T(8,128)(2,1)S(1)} collective-permute-done((bf16[3,128,512]{2,1,0:T(8,128)(2,1)}, bf16[3,128,512]{2,1,0:T(8,128)(2,1)S(1)}, u32[]{:S(2)}, u32[]{:S(2)}) %collective-permute-start.5) | collective-permute-done | bytes 393248 | tf_op jit(solution)/shard_map/ppermute | solution.py:231
  27.2 1.8 %half.1 = (bf16[128,512]{1,0:T(8,128)(2,1)S(1)}, bf16[128,512]{1,0:T(8,128)(2,1)}, bf16[128,512]{1,0:T(8,128)(2,1)}, bf16[128,512]{1,0:T(8,128)(2,1)}) custom-call(s32[4,3]{1,0:T(4,128)S(1)} %copy.23.sources, s32[4,3]{1,0:T(4,128)S(1)} %copy.24.kinds, bf16[128,512]{1,0:T(8,128)(2,1)S(1)} %get-tuple-element.29.p0, ...), custom_call_target="tpu_custom_call" | custom-call | bytes 65536 | tf_op jit(solution)/shard_map/half/pallas_call | solution.py:101
  29.6 2.8 %collective-permute-start.9 = (bf16[128,512]{1,0:T(8,128)(2,1)}, bf16[128,512]{1,0:T(8,128)(2,1)S(1)}, u32[]{:S(2)}, u32[]{:S(2)}) collective-permute-start(bf16[128,512]{1,0:T(8,128)(2,1)} %get-tuple-element.43), channel_id=1, source_target_pairs={{0,4},{2,6},{4,0},{6,2},{1,5},{3,7},{5,1},{7,3},{8,12},{10,14},{12... | collective-permute-start | bytes 393224 | tf_op jit(solution)/shard_map/ppermute | solution.py:221
  32.6 1.1 %alpha.1 = (bf16[128,512]{1,0:T(8,128)(2,1)S(1)}, bf16[128,512]{1,0:T(8,128)(2,1)S(1)}, bf16[128,512]{1,0:T(8,128)(2,1)S(1)}, bf16[128,512]{1,0:T(8,128)(2,1)S(1)}) custom-call(s32[4,4]{1,0:T(4,128)S(1)} %copy.21.sources, s32[4,4]{1,0:T(4,128)S(1)} %copy.22.kinds, bf16[128,512]{1,0:T(8,128)(2,1)S(1)} %get-tuple-element.29.p0, ...), custom_call_target="tpu_custom_call" | custom-call | bytes 65536 | tf_op jit(solution)/shard_map/alpha/pallas_call | solution.py:101
  34.0 0.6 %collective-permute-start.7 = (bf16[128,512]{1,0:T(8,128)(2,1)S(1)}, bf16[128,512]{1,0:T(8,128)(2,1)S(1)}, u32[]{:S(2)}, u32[]{:S(2)}) collective-permute-start(bf16[128,512]{1,0:T(8,128)(2,1)S(1)} %get-tuple-element.40), channel_id=1, source_target_pairs={{0,6},{2,4},{4,2},{6,0},{1,7},{3,5},{5,3},{7,1},{8,14},{10,12},{12... | collective-permute-start | bytes 393224 | tf_op jit(solution)/shard_map/ppermute | solution.py:221
  34.6 2.5 %collective-permute-start.8 = (bf16[128,512]{1,0:T(8,128)(2,1)S(1)}, bf16[128,512]{1,0:T(8,128)(2,1)S(1)}, u32[]{:S(2)}, u32[]{:S(2)}) collective-permute-start(bf16[128,512]{1,0:T(8,128)(2,1)S(1)} %get-tuple-element.41), channel_id=1, source_target_pairs={{0,4},{2,6},{4,0},{6,2},{1,5},{3,7},{5,1},{7,3},{8,12},{10,14},{12... | collective-permute-start | bytes 393224 | tf_op jit(solution)/shard_map/ppermute | solution.py:221
  37.1 4.6 %collective-permute-start.12 = (bf16[128,512]{1,0:T(8,128)(2,1)S(1)}, bf16[128,512]{1,0:T(8,128)(2,1)S(1)}, u32[]{:S(2)}, u32[]{:S(2)}) collective-permute-start(bf16[128,512]{1,0:T(8,128)(2,1)S(1)} %get-tuple-element.47.rest_0_), channel_id=1, source_target_pairs={{0,1},{1,0},{2,3},{3,2},{4,5},{5,4},{6,7},{7,6},{8,9},{9,8},{10,11... | collective-permute-start | bytes 393224 | tf_op jit(solution)/shard_map/ppermute | solution.py:221
  41.7 1.0 %collective-permute-start.14 = (bf16[128,512]{1,0:T(8,128)(2,1)S(1)}, bf16[128,512]{1,0:T(8,128)(2,1)S(1)}, u32[]{:S(2)}, u32[]{:S(2)}) collective-permute-start(bf16[128,512]{1,0:T(8,128)(2,1)S(1)} %collective-permute-done.9.rest_2_), channel_id=1, source_target_pairs={{0,1},{1,0},{2,3},{3,2},{4,5},{5,4},{6,7},{7,6},{8,9},{9,8},{10,11... | collective-permute-start | bytes 393224 | tf_op jit(solution)/shard_map/ppermute | solution.py:221
  42.7 1.3 %collective-permute-start.15 = (bf16[128,512]{1,0:T(8,128)(2,1)S(1)}, bf16[128,512]{1,0:T(8,128)(2,1)S(1)}, u32[]{:S(2)}, u32[]{:S(2)}) collective-permute-start(bf16[128,512]{1,0:T(8,128)(2,1)S(1)} %collective-permute-done.11.rest_3_), channel_id=1, source_target_pairs={{0,1},{1,0},{2,3},{3,2},{4,5},{5,4},{6,7},{7,6},{8,9},{9,8},{10,11... | collective-permute-start | bytes 393224 | tf_op jit(solution)/shard_map/ppermute | solution.py:221
  44.1 0.9 %collective-permute-done.15.rest_7_ = bf16[128,512]{1,0:T(8,128)(2,1)S(1)} collective-permute-done((bf16[128,512]{1,0:T(8,128)(2,1)S(1)}, bf16[128,512]{1,0:T(8,128)(2,1)S(1)}, u32[]{:S(2)}, u32[]{:S(2)}) %collective-permute-start.15) | collective-permute-done | bytes 131104 | tf_op jit(solution)/shard_map/ppermute | solution.py:221
  45.0 3.5 %mixed.1 = bf16[128,2048]{1,0:T(8,128)(2,1)} custom-call(s32[16,8]{1,0:T(8,128)S(1)} %copy.19.sources, s32[16,8]{1,0:T(8,128)S(1)} %copy.20.kinds, bf16[8,128,128]{2,1,0:T(8,128)(2,1)S(1)} %copy-done.5, f32[128,2048]{1,0:T(8,128)S(1)} %get-tuple-element.36.start, f32[8,128]{1,0:T(8,128)S(1)} %mark.1, bf16[128,512]{1,0:T(8,128)(2,1)S(1)} %get-tuple-element.47.rest_0_, ...), custom_call_target="tpu_custom_call" | custom-call | bytes 262144 | tf_op jit(solution)/shard_map/mixed/pallas_call | solution.py:189
  (50 shorter events, 1.6 us)
Async XLA Ops:
  1.1 5.0 %collective-permute-start.1 = (bf16[128,512]{1,0:T(8,128)(2,1)S(1)}, bf16[128,512]{1,0:T(8,128)(2,1)S(1)}, u32[]{:S(2)}, u32[]{:S(2)}) collective-permute-start(bf16[128,512]{1,0:T(8,128)(2,1)S(1)} %get-tuple-element.30), channel_id=1, source_target_pairs={{0,2},{2,0},{4,6},{6,4},{1,3},{3,1},{5,7},{7,5},{8,10},{10,8},{12,... | collective-permute-start | bytes 393224 | tf_op jit(solution)/shard_map/ppermute | solution.py:221
  2.4 5.0 %collective-permute-start.2 = (bf16[128,512]{1,0:T(8,128)(2,1)S(1)}, bf16[128,512]{1,0:T(8,128)(2,1)S(1)}, u32[]{:S(2)}, u32[]{:S(2)}) collective-permute-start(bf16[128,512]{1,0:T(8,128)(2,1)S(1)} %get-tuple-element.31), channel_id=1, source_target_pairs={{0,6},{2,4},{4,2},{6,0},{1,7},{3,5},{5,3},{7,1},{8,14},{10,12},{12... | collective-permute-start | bytes 393224 | tf_op jit(solution)/shard_map/ppermute | solution.py:221
  4.2 6.2 %collective-permute-start.3 = (bf16[128,512]{1,0:T(8,128)(2,1)S(1)}, bf16[128,512]{1,0:T(8,128)(2,1)S(1)}, u32[]{:S(2)}, u32[]{:S(2)}) collective-permute-start(bf16[128,512]{1,0:T(8,128)(2,1)S(1)} %get-tuple-element.32), channel_id=1, source_target_pairs={{0,4},{2,6},{4,0},{6,2},{1,5},{3,7},{5,1},{7,3},{8,12},{10,14},{12... | collective-permute-start | bytes 393224 | tf_op jit(solution)/shard_map/ppermute | solution.py:221
  4.8 16.7 %collective-permute-start = (bf16[128,2048]{1,0:T(8,128)(2,1)}, bf16[128,2048]{1,0:T(8,128)(2,1)S(1)}, u32[]{:S(2)}, u32[]{:S(2)}) collective-permute-start(bf16[128,2048]{1,0:T(8,128)(2,1)} %bitcast.own.whole), channel_id=1, source_target_pairs={{0,1},{1,0},{2,3},{3,2},{4,5},{5,4},{6,7},{7,6},{8,9},{9,8},{10,11... | collective-permute-start | bytes 1572872 | tf_op jit(solution)/shard_map/ppermute | solution.py:221
  10.4 11.1 %copy-start = (bf16[8,128,128]{2,1,0:T(8,128)(2,1)S(1)}, bf16[8,128,128]{2,1,0:T(8,128)(2,1)}, u32[]{:S(2)}) copy-start(bf16[8,128,128]{2,1,0:T(8,128)(2,1)} %table.3) | copy-start | bytes 786436
  10.4 11.1 %copy-start.1 = (bf16[8,128,128]{2,1,0:T(8,128)(2,1)S(1)}, bf16[8,128,128]{2,1,0:T(8,128)(2,1)}, u32[]{:S(2)}) copy-start(bf16[8,128,128]{2,1,0:T(8,128)(2,1)} %opp_table.1) | copy-start | bytes 786436
  11.4 8.4 %copy-start.6 = (s32[16,8]{0,1:T(8,128)S(1)}, s32[16,8]{0,1:T(8,128)}, u32[]{:S(2)}) copy-start(s32[16,8]{0,1:T(8,128)} %param.13) | copy-start | bytes 1540
  11.4 13.4 %collective-permute-start.4 = (bf16[3,128,512]{2,1,0:T(8,128)(2,1)}, bf16[3,128,512]{2,1,0:T(8,128)(2,1)S(1)}, u32[]{:S(2)}, u32[]{:S(2)}) collective-permute-start(bf16[3,128,512]{2,1,0:T(8,128)(2,1)} %get-tuple-element.33), channel_id=1, source_target_pairs={{0,8},{16,24},{32,40},{48,56},{64,72},{80,88},{96,104},{112,120},{... | collective-permute-start | bytes 1179656 | tf_op jit(solution)/shard_map/ppermute | solution.py:231
  13.0 14.2 %collective-permute-start.5 = (bf16[3,128,512]{2,1,0:T(8,128)(2,1)}, bf16[3,128,512]{2,1,0:T(8,128)(2,1)S(1)}, u32[]{:S(2)}, u32[]{:S(2)}) collective-permute-start(bf16[3,128,512]{2,1,0:T(8,128)(2,1)} %get-tuple-element.34), channel_id=1, source_target_pairs={{8,16},{24,32},{40,48},{56,64},{72,80},{88,96},{104,112},{120,128}... | collective-permute-start | bytes 1179656 | tf_op jit(solution)/shard_map/ppermute | solution.py:231
  21.5 5.7 %copy-start.2 = (bf16[8,128,128]{2,1,0:T(8,128)(2,1)S(1)}, bf16[8,128,128]{2,1,0:T(8,128)(2,1)}, u32[]{:S(2)}) copy-start(bf16[8,128,128]{2,1,0:T(8,128)(2,1)} %table.5) | copy-start | bytes 786436
  24.7 4.3 %copy-start.4 = (bf16[8,128,128]{2,1,0:T(8,128)(2,1)}, bf16[8,128,128]{2,1,0:T(8,128)(2,1)S(1)}, u32[]{:S(2)}) copy-start(bf16[8,128,128]{2,1,0:T(8,128)(2,1)S(1)} %get-tuple-element.28.table) | copy-start | bytes 786436
  27.2 5.4 %copy-start.3 = (bf16[8,128,128]{2,1,0:T(8,128)(2,1)S(1)}, bf16[8,128,128]{2,1,0:T(8,128)(2,1)}, u32[]{:S(2)}) copy-start(bf16[8,128,128]{2,1,0:T(8,128)(2,1)} %table.4) | copy-start | bytes 786436
  29.0 5.6 %collective-permute-start.10 = (bf16[128,512]{1,0:T(8,128)(2,1)}, bf16[128,512]{1,0:T(8,128)(2,1)S(1)}, u32[]{:S(2)}, u32[]{:S(2)}) collective-permute-start(bf16[128,512]{1,0:T(8,128)(2,1)} %get-tuple-element.44), channel_id=1, source_target_pairs={{0,2},{2,0},{4,6},{6,4},{1,3},{3,1},{5,7},{7,5},{8,10},{10,8},{12,... | collective-permute-start | bytes 393224 | tf_op jit(solution)/shard_map/ppermute | solution.py:221
  29.1 8.0 %collective-permute-start.11 = (bf16[128,512]{1,0:T(8,128)(2,1)}, bf16[128,512]{1,0:T(8,128)(2,1)S(1)}, u32[]{:S(2)}, u32[]{:S(2)}) collective-permute-start(bf16[128,512]{1,0:T(8,128)(2,1)} %get-tuple-element.45), channel_id=1, source_target_pairs={{0,6},{2,4},{4,2},{6,0},{1,7},{3,5},{5,3},{7,1},{8,14},{10,12},{12... | collective-permute-start | bytes 393224 | tf_op jit(solution)/shard_map/ppermute | solution.py:221
  29.6 7.6 %collective-permute-start.9 = (bf16[128,512]{1,0:T(8,128)(2,1)}, bf16[128,512]{1,0:T(8,128)(2,1)S(1)}, u32[]{:S(2)}, u32[]{:S(2)}) collective-permute-start(bf16[128,512]{1,0:T(8,128)(2,1)} %get-tuple-element.43), channel_id=1, source_target_pairs={{0,4},{2,6},{4,0},{6,2},{1,5},{3,7},{5,1},{7,3},{8,12},{10,14},{12... | collective-permute-start | bytes 393224 | tf_op jit(solution)/shard_map/ppermute | solution.py:221
  32.6 11.4 %copy-start.8 = (s32[16,8]{0,1:T(8,128)S(1)}, s32[16,8]{0,1:T(8,128)}, u32[]{:S(2)}) copy-start(s32[16,8]{0,1:T(8,128)} %param.15) | copy-start | bytes 1540
  33.8 11.3 %copy-start.5 = (bf16[8,128,128]{2,1,0:T(8,128)(2,1)S(1)}, bf16[8,128,128]{2,1,0:T(8,128)(2,1)}, u32[]{:S(2)}) copy-start(bf16[8,128,128]{2,1,0:T(8,128)(2,1)} %copy-done.4) | copy-start | bytes 786436
  33.8 8.0 %collective-permute-start.6 = (bf16[128,512]{1,0:T(8,128)(2,1)S(1)}, bf16[128,512]{1,0:T(8,128)(2,1)S(1)}, u32[]{:S(2)}, u32[]{:S(2)}) collective-permute-start(bf16[128,512]{1,0:T(8,128)(2,1)S(1)} %get-tuple-element.39), channel_id=1, source_target_pairs={{0,2},{2,0},{4,6},{6,4},{1,3},{3,1},{5,7},{7,5},{8,10},{10,8},{12,... | collective-permute-start | bytes 393224 | tf_op jit(solution)/shard_map/ppermute | solution.py:221
  34.0 8.8 %collective-permute-start.7 = (bf16[128,512]{1,0:T(8,128)(2,1)S(1)}, bf16[128,512]{1,0:T(8,128)(2,1)S(1)}, u32[]{:S(2)}, u32[]{:S(2)}) collective-permute-start(bf16[128,512]{1,0:T(8,128)(2,1)S(1)} %get-tuple-element.40), channel_id=1, source_target_pairs={{0,6},{2,4},{4,2},{6,0},{1,7},{3,5},{5,3},{7,1},{8,14},{10,12},{12... | collective-permute-start | bytes 393224 | tf_op jit(solution)/shard_map/ppermute | solution.py:221
  34.6 9.5 %collective-permute-start.8 = (bf16[128,512]{1,0:T(8,128)(2,1)S(1)}, bf16[128,512]{1,0:T(8,128)(2,1)S(1)}, u32[]{:S(2)}, u32[]{:S(2)}) collective-permute-start(bf16[128,512]{1,0:T(8,128)(2,1)S(1)} %get-tuple-element.41), channel_id=1, source_target_pairs={{0,4},{2,6},{4,0},{6,2},{1,5},{3,7},{5,1},{7,3},{8,12},{10,14},{12... | collective-permute-start | bytes 393224 | tf_op jit(solution)/shard_map/ppermute | solution.py:221
  37.1 7.0 %collective-permute-start.12 = (bf16[128,512]{1,0:T(8,128)(2,1)S(1)}, bf16[128,512]{1,0:T(8,128)(2,1)S(1)}, u32[]{:S(2)}, u32[]{:S(2)}) collective-permute-start(bf16[128,512]{1,0:T(8,128)(2,1)S(1)} %get-tuple-element.47.rest_0_), channel_id=1, source_target_pairs={{0,1},{1,0},{2,3},{3,2},{4,5},{5,4},{6,7},{7,6},{8,9},{9,8},{10,11... | collective-permute-start | bytes 393224 | tf_op jit(solution)/shard_map/ppermute | solution.py:221
  41.7 2.4 %collective-permute-start.13 = (bf16[128,512]{1,0:T(8,128)(2,1)S(1)}, bf16[128,512]{1,0:T(8,128)(2,1)S(1)}, u32[]{:S(2)}, u32[]{:S(2)}) collective-permute-start(bf16[128,512]{1,0:T(8,128)(2,1)S(1)} %collective-permute-done.10.rest_1_), channel_id=1, source_target_pairs={{0,1},{1,0},{2,3},{3,2},{4,5},{5,4},{6,7},{7,6},{8,9},{9,8},{10,11... | collective-permute-start | bytes 393224 | tf_op jit(solution)/shard_map/ppermute | solution.py:221
  41.7 2.4 %collective-permute-start.14 = (bf16[128,512]{1,0:T(8,128)(2,1)S(1)}, bf16[128,512]{1,0:T(8,128)(2,1)S(1)}, u32[]{:S(2)}, u32[]{:S(2)}) collective-permute-start(bf16[128,512]{1,0:T(8,128)(2,1)S(1)} %collective-permute-done.9.rest_2_), channel_id=1, source_target_pairs={{0,1},{1,0},{2,3},{3,2},{4,5},{5,4},{6,7},{7,6},{8,9},{9,8},{10,11... | collective-permute-start | bytes 393224 | tf_op jit(solution)/shard_map/ppermute | solution.py:221
  42.7 2.3 %collective-permute-start.15 = (bf16[128,512]{1,0:T(8,128)(2,1)S(1)}, bf16[128,512]{1,0:T(8,128)(2,1)S(1)}, u32[]{:S(2)}, u32[]{:S(2)}) collective-permute-start(bf16[128,512]{1,0:T(8,128)(2,1)S(1)} %collective-permute-done.11.rest_3_), channel_id=1, source_target_pairs={{0,1},{1,0},{2,3},{3,2},{4,5},{5,4},{6,7},{7,6},{8,9},{9,8},{10,11... | collective-permute-start | bytes 393224 | tf_op jit(solution)/shard_map/ppermute | solution.py:221
  (5 other events, 8.8 us)

commit v4 on v3

--- a/solution.py
+++ b/solution.py
@@ -138,7 +138,7 @@
         out[:, cols] = beta_tile(held, flat, sources, kinds, tile, links)
         return carry
 
-    lax.fori_loop(0, out.shape[1] // TILE, body, 0, unroll=4)
+    lax.fori_loop(0, out.shape[1] // TILE, body, 0, unroll=16)
 
 
 def same_part(sources, kinds, own, other, table, opp_table):
@@ -180,7 +180,7 @@
         out[:, cols] = total.astype(out.dtype)
         return carry
 
-    lax.fori_loop(0, out.shape[1] // TILE, body, 0, unroll=4)
+    lax.fori_loop(0, out.shape[1] // TILE, body, 0, unroll=16)
 
 
 def mixed_part(sources, kinds, table, start, mark, half, other, alpha):

time: 48.8 us -> 48.4 us (level)
  Pallas kernels: 11.7 us -> 10.8 us
  transfers between devices with their start and end apart: 16 -> 16, of which waited for: 4 -> 4; matrix products, arithmetic and copies ran while one was open for 2% -> 2% of each run, Pallas kernels for 11% -> 10%
where the time goes in v4:
time: 48.4 us; the launch traced here: 48.2 us
  starting transfers between devices  26.9 us (56%)
  Pallas kernels  10.8 us (22%)
  waiting for transfers between devices  8.22 us (17%)
  local copies, waits for them, and re-layouts  2.08 us (4%)
    ppermute x14, starting transfers between devices, swapped(): lax.ppermute(value, axis, [(i, i ^ flip) for i in range(lax.axis_size(axi...  18.6 us
    ppermute x2, starting transfers between devices, handed(): lax.ppermute(value, 'row', pairs + [(there, here) for here, there in pairs])  8.38 us
    ppermute x14, waiting for transfers between devices, swapped(): lax.ppermute(value, axis, [(i, i ^ flip) for i in range(lax.axis_size(axi...  5.28 us
    pallas_call x1, Pallas kernels, mixed_part(): pl.pallas_call(functools.partial(mixed_kernel, sources.shape[1]), out_sha...  3.16 us
    ppermute x2, waiting for transfers between devices, handed(): lax.ppermute(value, 'row', pairs + [(there, here) for here, there in pairs])  2.95 us
    pallas_call x2, Pallas kernels, near(): pl.pallas_call(functools.partial(near_kernel, links), out_shape=[piece] *...  2.91 us
    pallas_call x1, Pallas kernels, same_part(): pl.pallas_call(functools.partial(same_kernel, sources.shape[1]), out_shap...  2.71 us
    unnamed x33, local copies, waits for them, and re-layouts  1.93 us
  transfers between devices with their start and end apart: 16, of which 4 were waited for; matrix products, arithmetic and copies ran while one was open for 2% of the time, Pallas kernels for 10%

profile of v4, /device:TPU:25, one launch (start us, length us, event | category | flops | bytes accessed | tf_op | source)
XLA Modules:
  0.0 48.2 jit_solution(8885576264783250118)
XLA Ops:
  0.0 1.1 %cut.1 = (bf16[128,512]{1,0:T(8,128)(2,1)S(1)}, bf16[128,512]{1,0:T(8,128)(2,1)S(1)}, bf16[128,512]{1,0:T(8,128)(2,1)S(1)}, bf16[128,512]{1,0:T(8,128)(2,1)S(1)}) custom-call(bf16[128,2048]{1,0:T(8,128)(2,1)} %bitcast.own.whole), custom_call_target="tpu_custom_call" | custom-call | bytes 1048576 | tf_op jit(solution)/shard_map/cut/pallas_call | solution.py:36
  1.1 1.3 %collective-permute-start.1 = (bf16[128,512]{1,0:T(8,128)(2,1)S(1)}, bf16[128,512]{1,0:T(8,128)(2,1)S(1)}, u32[]{:S(2)}, u32[]{:S(2)}) collective-permute-start(bf16[128,512]{1,0:T(8,128)(2,1)S(1)} %get-tuple-element.30), channel_id=1, source_target_pairs={{0,2},{2,0},{4,6},{6,4},{1,3},{3,1},{5,7},{7,5},{8,10},{10,8},{12,... | collective-permute-start | bytes 393224 | tf_op jit(solution)/shard_map/ppermute | solution.py:221
  2.4 1.8 %collective-permute-start.2 = (bf16[128,512]{1,0:T(8,128)(2,1)S(1)}, bf16[128,512]{1,0:T(8,128)(2,1)S(1)}, u32[]{:S(2)}, u32[]{:S(2)}) collective-permute-start(bf16[128,512]{1,0:T(8,128)(2,1)S(1)} %get-tuple-element.31), channel_id=1, source_target_pairs={{0,6},{2,4},{4,2},{6,0},{1,7},{3,5},{5,3},{7,1},{8,14},{10,12},{12... | collective-permute-start | bytes 393224 | tf_op jit(solution)/shard_map/ppermute | solution.py:221
  4.2 0.6 %collective-permute-start.3 = (bf16[128,512]{1,0:T(8,128)(2,1)S(1)}, bf16[128,512]{1,0:T(8,128)(2,1)S(1)}, u32[]{:S(2)}, u32[]{:S(2)}) collective-permute-start(bf16[128,512]{1,0:T(8,128)(2,1)S(1)} %get-tuple-element.32), channel_id=1, source_target_pairs={{0,4},{2,6},{4,0},{6,2},{1,5},{3,7},{5,1},{7,3},{8,12},{10,14},{12... | collective-permute-start | bytes 393224 | tf_op jit(solution)/shard_map/ppermute | solution.py:221
  4.8 1.2 %collective-permute-start = (bf16[128,2048]{1,0:T(8,128)(2,1)}, bf16[128,2048]{1,0:T(8,128)(2,1)S(1)}, u32[]{:S(2)}, u32[]{:S(2)}) collective-permute-start(bf16[128,2048]{1,0:T(8,128)(2,1)} %bitcast.own.whole), channel_id=1, source_target_pairs={{0,1},{1,0},{2,3},{3,2},{4,5},{5,4},{6,7},{7,6},{8,9},{9,8},{10,11... | collective-permute-start | bytes 1572872 | tf_op jit(solution)/shard_map/ppermute | solution.py:221
  6.1 1.3 %collective-permute-done.2.p3 = bf16[128,512]{1,0:T(8,128)(2,1)S(1)} collective-permute-done((bf16[128,512]{1,0:T(8,128)(2,1)S(1)}, bf16[128,512]{1,0:T(8,128)(2,1)S(1)}, u32[]{:S(2)}, u32[]{:S(2)}) %collective-permute-start.2) | collective-permute-done | bytes 131104 | tf_op jit(solution)/shard_map/ppermute | solution.py:221
  7.4 3.0 %collective-permute-done.3.p2 = bf16[128,512]{1,0:T(8,128)(2,1)S(1)} collective-permute-done((bf16[128,512]{1,0:T(8,128)(2,1)S(1)}, bf16[128,512]{1,0:T(8,128)(2,1)S(1)}, u32[]{:S(2)}, u32[]{:S(2)}) %collective-permute-start.3) | collective-permute-done | bytes 131104 | tf_op jit(solution)/shard_map/ppermute | solution.py:221
  10.4 0.9 %edges.1 = (bf16[3,128,512]{2,1,0:T(8,128)(2,1)}, bf16[3,128,512]{2,1,0:T(8,128)(2,1)}) custom-call(bf16[128,512]{1,0:T(8,128)(2,1)S(1)} %get-tuple-element.29.p0, bf16[128,512]{1,0:T(8,128)(2,1)S(1)} %collective-permute-done.1.p1, bf16[128,512]{1,0:T(8,128)(2,1)S(1)} %collective-permute-done.2.p3, bf16[128,512]{1,0:T(8,128)(2,1)S(1)} %collective-permute-done.3.p2), custom_call_target="tpu_custom_call" | custom-call | bytes 1572864 | tf_op jit(solution)/shard_map/edges/pallas_call | solution.py:63
  11.4 1.6 %collective-permute-start.4 = (bf16[3,128,512]{2,1,0:T(8,128)(2,1)}, bf16[3,128,512]{2,1,0:T(8,128)(2,1)S(1)}, u32[]{:S(2)}, u32[]{:S(2)}) collective-permute-start(bf16[3,128,512]{2,1,0:T(8,128)(2,1)} %get-tuple-element.33), channel_id=1, source_target_pairs={{0,8},{16,24},{32,40},{48,56},{64,72},{80,88},{96,104},{112,120},{... | collective-permute-start | bytes 1179656 | tf_op jit(solution)/shard_map/ppermute | solution.py:231
  13.0 6.7 %collective-permute-start.5 = (bf16[3,128,512]{2,1,0:T(8,128)(2,1)}, bf16[3,128,512]{2,1,0:T(8,128)(2,1)S(1)}, u32[]{:S(2)}, u32[]{:S(2)}) collective-permute-start(bf16[3,128,512]{2,1,0:T(8,128)(2,1)} %get-tuple-element.34), channel_id=1, source_target_pairs={{8,16},{24,32},{40,48},{56,64},{72,80},{88,96},{104,112},{120,128}... | collective-permute-start | bytes 1179656 | tf_op jit(solution)/shard_map/ppermute | solution.py:231
  19.9 0.6 %copy-done.7 = s32[16,8]{0,1:T(8,128)S(1)} copy-done((s32[16,8]{0,1:T(8,128)S(1)}, s32[16,8]{0,1:T(8,128)}, u32[]{:S(2)}) %copy-start.7) | copy-done | bytes 536
  20.6 0.7 %copy-done.10 = s32[128,3]{0,1:T(4,128)S(1)} copy-done((s32[128,3]{0,1:T(4,128)S(1)}, s32[128,3]{0,1:T(4,128)}, u32[]{:S(2)}) %copy-start.10) | copy-done | bytes 1560
  21.5 2.7 %same.1 = (f32[128,2048]{1,0:T(8,128)S(1)}, bf16[8,128,128]{2,1,0:T(8,128)(2,1)S(1)}) custom-call(s32[16,8]{1,0:T(8,128)S(1)} %copy.19.sources, s32[16,8]{1,0:T(8,128)S(1)} %copy.14.kinds, bf16[128,2048]{1,0:T(8,128)(2,1)} %bitcast.own.whole, bf16[128,2048]{1,0:T(8,128)(2,1)S(1)} %collective-permute-done.other, bf16[8,128,128]{2,1,0:T(8,128)(2,1)S(1)} %copy-done, ...), custom_call_target="tpu_custom_call" | custom-call | bytes 262144 | tf_op jit(solution)/shard_map/same/pallas_call | solution.py:146
  24.3 2.9 %collective-permute-done.5.odd = bf16[3,128,512]{2,1,0:T(8,128)(2,1)S(1)} collective-permute-done((bf16[3,128,512]{2,1,0:T(8,128)(2,1)}, bf16[3,128,512]{2,1,0:T(8,128)(2,1)S(1)}, u32[]{:S(2)}, u32[]{:S(2)}) %collective-permute-start.5) | collective-permute-done | bytes 393248 | tf_op jit(solution)/shard_map/ppermute | solution.py:231
  27.2 1.8 %half.1 = (bf16[128,512]{1,0:T(8,128)(2,1)S(1)}, bf16[128,512]{1,0:T(8,128)(2,1)}, bf16[128,512]{1,0:T(8,128)(2,1)}, bf16[128,512]{1,0:T(8,128)(2,1)}) custom-call(s32[4,3]{1,0:T(4,128)S(1)} %copy.23.sources, s32[4,3]{1,0:T(4,128)S(1)} %copy.24.kinds, bf16[128,512]{1,0:T(8,128)(2,1)S(1)} %get-tuple-element.29.p0, ...), custom_call_target="tpu_custom_call" | custom-call | bytes 65536 | tf_op jit(solution)/shard_map/half/pallas_call | solution.py:101
  29.6 2.8 %collective-permute-start.9 = (bf16[128,512]{1,0:T(8,128)(2,1)}, bf16[128,512]{1,0:T(8,128)(2,1)S(1)}, u32[]{:S(2)}, u32[]{:S(2)}) collective-permute-start(bf16[128,512]{1,0:T(8,128)(2,1)} %get-tuple-element.43), channel_id=1, source_target_pairs={{0,4},{2,6},{4,0},{6,2},{1,5},{3,7},{5,1},{7,3},{8,12},{10,14},{12... | collective-permute-start | bytes 393224 | tf_op jit(solution)/shard_map/ppermute | solution.py:221
  32.6 1.1 %alpha.1 = (bf16[128,512]{1,0:T(8,128)(2,1)S(1)}, bf16[128,512]{1,0:T(8,128)(2,1)S(1)}, bf16[128,512]{1,0:T(8,128)(2,1)S(1)}, bf16[128,512]{1,0:T(8,128)(2,1)S(1)}) custom-call(s32[4,4]{1,0:T(4,128)S(1)} %copy.21.sources, s32[4,4]{1,0:T(4,128)S(1)} %copy.22.kinds, bf16[128,512]{1,0:T(8,128)(2,1)S(1)} %get-tuple-element.29.p0, ...), custom_call_target="tpu_custom_call" | custom-call | bytes 65536 | tf_op jit(solution)/shard_map/alpha/pallas_call | solution.py:101
  34.0 0.6 %collective-permute-start.7 = (bf16[128,512]{1,0:T(8,128)(2,1)S(1)}, bf16[128,512]{1,0:T(8,128)(2,1)S(1)}, u32[]{:S(2)}, u32[]{:S(2)}) collective-permute-start(bf16[128,512]{1,0:T(8,128)(2,1)S(1)} %get-tuple-element.40), channel_id=1, source_target_pairs={{0,6},{2,4},{4,2},{6,0},{1,7},{3,5},{5,3},{7,1},{8,14},{10,12},{12... | collective-permute-start | bytes 393224 | tf_op jit(solution)/shard_map/ppermute | solution.py:221
  34.6 2.5 %collective-permute-start.8 = (bf16[128,512]{1,0:T(8,128)(2,1)S(1)}, bf16[128,512]{1,0:T(8,128)(2,1)S(1)}, u32[]{:S(2)}, u32[]{:S(2)}) collective-permute-start(bf16[128,512]{1,0:T(8,128)(2,1)S(1)} %get-tuple-element.41), channel_id=1, source_target_pairs={{0,4},{2,6},{4,0},{6,2},{1,5},{3,7},{5,1},{7,3},{8,12},{10,14},{12... | collective-permute-start | bytes 393224 | tf_op jit(solution)/shard_map/ppermute | solution.py:221
  37.1 4.6 %collective-permute-start.12 = (bf16[128,512]{1,0:T(8,128)(2,1)S(1)}, bf16[128,512]{1,0:T(8,128)(2,1)S(1)}, u32[]{:S(2)}, u32[]{:S(2)}) collective-permute-start(bf16[128,512]{1,0:T(8,128)(2,1)S(1)} %get-tuple-element.47.rest_0_), channel_id=1, source_target_pairs={{0,1},{1,0},{2,3},{3,2},{4,5},{5,4},{6,7},{7,6},{8,9},{9,8},{10,11... | collective-permute-start | bytes 393224 | tf_op jit(solution)/shard_map/ppermute | solution.py:221
  41.7 1.0 %collective-permute-start.14 = (bf16[128,512]{1,0:T(8,128)(2,1)S(1)}, bf16[128,512]{1,0:T(8,128)(2,1)S(1)}, u32[]{:S(2)}, u32[]{:S(2)}) collective-permute-start(bf16[128,512]{1,0:T(8,128)(2,1)S(1)} %collective-permute-done.9.rest_2_), channel_id=1, source_target_pairs={{0,1},{1,0},{2,3},{3,2},{4,5},{5,4},{6,7},{7,6},{8,9},{9,8},{10,11... | collective-permute-start | bytes 393224 | tf_op jit(solution)/shard_map/ppermute | solution.py:221
  42.7 1.3 %collective-permute-start.15 = (bf16[128,512]{1,0:T(8,128)(2,1)S(1)}, bf16[128,512]{1,0:T(8,128)(2,1)S(1)}, u32[]{:S(2)}, u32[]{:S(2)}) collective-permute-start(bf16[128,512]{1,0:T(8,128)(2,1)S(1)} %collective-permute-done.11.rest_3_), channel_id=1, source_target_pairs={{0,1},{1,0},{2,3},{3,2},{4,5},{5,4},{6,7},{7,6},{8,9},{9,8},{10,11... | collective-permute-start | bytes 393224 | tf_op jit(solution)/shard_map/ppermute | solution.py:221
  44.1 0.9 %collective-permute-done.15.rest_7_ = bf16[128,512]{1,0:T(8,128)(2,1)S(1)} collective-permute-done((bf16[128,512]{1,0:T(8,128)(2,1)S(1)}, bf16[128,512]{1,0:T(8,128)(2,1)S(1)}, u32[]{:S(2)}, u32[]{:S(2)}) %collective-permute-start.15) | collective-permute-done | bytes 131104 | tf_op jit(solution)/shard_map/ppermute | solution.py:221
  45.0 3.2 %mixed.1 = bf16[128,2048]{1,0:T(8,128)(2,1)} custom-call(s32[16,8]{1,0:T(8,128)S(1)} %copy.19.sources, s32[16,8]{1,0:T(8,128)S(1)} %copy.20.kinds, bf16[8,128,128]{2,1,0:T(8,128)(2,1)S(1)} %copy-done.5, f32[128,2048]{1,0:T(8,128)S(1)} %get-tuple-element.36.start, f32[8,128]{1,0:T(8,128)S(1)} %mark.1, bf16[128,512]{1,0:T(8,128)(2,1)S(1)} %get-tuple-element.47.rest_0_, ...), custom_call_target="tpu_custom_call" | custom-call | bytes 262144 | tf_op jit(solution)/shard_map/mixed/pallas_call | solution.py:189
  (50 shorter events, 1.6 us)
Async XLA Ops:
  1.1 5.0 %collective-permute-start.1 = (bf16[128,512]{1,0:T(8,128)(2,1)S(1)}, bf16[128,512]{1,0:T(8,128)(2,1)S(1)}, u32[]{:S(2)}, u32[]{:S(2)}) collective-permute-start(bf16[128,512]{1,0:T(8,128)(2,1)S(1)} %get-tuple-element.30), channel_id=1, source_target_pairs={{0,2},{2,0},{4,6},{6,4},{1,3},{3,1},{5,7},{7,5},{8,10},{10,8},{12,... | collective-permute-start | bytes 393224 | tf_op jit(solution)/shard_map/ppermute | solution.py:221
  2.4 5.0 %collective-permute-start.2 = (bf16[128,512]{1,0:T(8,128)(2,1)S(1)}, bf16[128,512]{1,0:T(8,128)(2,1)S(1)}, u32[]{:S(2)}, u32[]{:S(2)}) collective-permute-start(bf16[128,512]{1,0:T(8,128)(2,1)S(1)} %get-tuple-element.31), channel_id=1, source_target_pairs={{0,6},{2,4},{4,2},{6,0},{1,7},{3,5},{5,3},{7,1},{8,14},{10,12},{12... | collective-permute-start | bytes 393224 | tf_op jit(solution)/shard_map/ppermute | solution.py:221
  4.2 6.2 %collective-permute-start.3 = (bf16[128,512]{1,0:T(8,128)(2,1)S(1)}, bf16[128,512]{1,0:T(8,128)(2,1)S(1)}, u32[]{:S(2)}, u32[]{:S(2)}) collective-permute-start(bf16[128,512]{1,0:T(8,128)(2,1)S(1)} %get-tuple-element.32), channel_id=1, source_target_pairs={{0,4},{2,6},{4,0},{6,2},{1,5},{3,7},{5,1},{7,3},{8,12},{10,14},{12... | collective-permute-start | bytes 393224 | tf_op jit(solution)/shard_map/ppermute | solution.py:221
  4.8 16.7 %collective-permute-start = (bf16[128,2048]{1,0:T(8,128)(2,1)}, bf16[128,2048]{1,0:T(8,128)(2,1)S(1)}, u32[]{:S(2)}, u32[]{:S(2)}) collective-permute-start(bf16[128,2048]{1,0:T(8,128)(2,1)} %bitcast.own.whole), channel_id=1, source_target_pairs={{0,1},{1,0},{2,3},{3,2},{4,5},{5,4},{6,7},{7,6},{8,9},{9,8},{10,11... | collective-permute-start | bytes 1572872 | tf_op jit(solution)/shard_map/ppermute | solution.py:221
  10.4 11.1 %copy-start = (bf16[8,128,128]{2,1,0:T(8,128)(2,1)S(1)}, bf16[8,128,128]{2,1,0:T(8,128)(2,1)}, u32[]{:S(2)}) copy-start(bf16[8,128,128]{2,1,0:T(8,128)(2,1)} %table.3) | copy-start | bytes 786436
  10.4 11.1 %copy-start.1 = (bf16[8,128,128]{2,1,0:T(8,128)(2,1)S(1)}, bf16[8,128,128]{2,1,0:T(8,128)(2,1)}, u32[]{:S(2)}) copy-start(bf16[8,128,128]{2,1,0:T(8,128)(2,1)} %opp_table.1) | copy-start | bytes 786436
  11.4 8.4 %copy-start.6 = (s32[16,8]{0,1:T(8,128)S(1)}, s32[16,8]{0,1:T(8,128)}, u32[]{:S(2)}) copy-start(s32[16,8]{0,1:T(8,128)} %param.13) | copy-start | bytes 1540
  11.4 12.9 %collective-permute-start.4 = (bf16[3,128,512]{2,1,0:T(8,128)(2,1)}, bf16[3,128,512]{2,1,0:T(8,128)(2,1)S(1)}, u32[]{:S(2)}, u32[]{:S(2)}) collective-permute-start(bf16[3,128,512]{2,1,0:T(8,128)(2,1)} %get-tuple-element.33), channel_id=1, source_target_pairs={{0,8},{16,24},{32,40},{48,56},{64,72},{80,88},{96,104},{112,120},{... | collective-permute-start | bytes 1179656 | tf_op jit(solution)/shard_map/ppermute | solution.py:231
  13.0 14.2 %collective-permute-start.5 = (bf16[3,128,512]{2,1,0:T(8,128)(2,1)}, bf16[3,128,512]{2,1,0:T(8,128)(2,1)S(1)}, u32[]{:S(2)}, u32[]{:S(2)}) collective-permute-start(bf16[3,128,512]{2,1,0:T(8,128)(2,1)} %get-tuple-element.34), channel_id=1, source_target_pairs={{8,16},{24,32},{40,48},{56,64},{72,80},{88,96},{104,112},{120,128}... | collective-permute-start | bytes 1179656 | tf_op jit(solution)/shard_map/ppermute | solution.py:231
  21.5 5.7 %copy-start.2 = (bf16[8,128,128]{2,1,0:T(8,128)(2,1)S(1)}, bf16[8,128,128]{2,1,0:T(8,128)(2,1)}, u32[]{:S(2)}) copy-start(bf16[8,128,128]{2,1,0:T(8,128)(2,1)} %table.5) | copy-start | bytes 786436
  24.3 4.7 %copy-start.4 = (bf16[8,128,128]{2,1,0:T(8,128)(2,1)}, bf16[8,128,128]{2,1,0:T(8,128)(2,1)S(1)}, u32[]{:S(2)}) copy-start(bf16[8,128,128]{2,1,0:T(8,128)(2,1)S(1)} %get-tuple-element.28.table) | copy-start | bytes 786436
  27.2 5.4 %copy-start.3 = (bf16[8,128,128]{2,1,0:T(8,128)(2,1)S(1)}, bf16[8,128,128]{2,1,0:T(8,128)(2,1)}, u32[]{:S(2)}) copy-start(bf16[8,128,128]{2,1,0:T(8,128)(2,1)} %table.4) | copy-start | bytes 786436
  29.0 5.6 %collective-permute-start.10 = (bf16[128,512]{1,0:T(8,128)(2,1)}, bf16[128,512]{1,0:T(8,128)(2,1)S(1)}, u32[]{:S(2)}, u32[]{:S(2)}) collective-permute-start(bf16[128,512]{1,0:T(8,128)(2,1)} %get-tuple-element.44), channel_id=1, source_target_pairs={{0,2},{2,0},{4,6},{6,4},{1,3},{3,1},{5,7},{7,5},{8,10},{10,8},{12,... | collective-permute-start | bytes 393224 | tf_op jit(solution)/shard_map/ppermute | solution.py:221
  29.1 8.0 %collective-permute-start.11 = (bf16[128,512]{1,0:T(8,128)(2,1)}, bf16[128,512]{1,0:T(8,128)(2,1)S(1)}, u32[]{:S(2)}, u32[]{:S(2)}) collective-permute-start(bf16[128,512]{1,0:T(8,128)(2,1)} %get-tuple-element.45), channel_id=1, source_target_pairs={{0,6},{2,4},{4,2},{6,0},{1,7},{3,5},{5,3},{7,1},{8,14},{10,12},{12... | collective-permute-start | bytes 393224 | tf_op jit(solution)/shard_map/ppermute | solution.py:221
  29.6 7.6 %collective-permute-start.9 = (bf16[128,512]{1,0:T(8,128)(2,1)}, bf16[128,512]{1,0:T(8,128)(2,1)S(1)}, u32[]{:S(2)}, u32[]{:S(2)}) collective-permute-start(bf16[128,512]{1,0:T(8,128)(2,1)} %get-tuple-element.43), channel_id=1, source_target_pairs={{0,4},{2,6},{4,0},{6,2},{1,5},{3,7},{5,1},{7,3},{8,12},{10,14},{12... | collective-permute-start | bytes 393224 | tf_op jit(solution)/shard_map/ppermute | solution.py:221
  32.6 11.4 %copy-start.8 = (s32[16,8]{0,1:T(8,128)S(1)}, s32[16,8]{0,1:T(8,128)}, u32[]{:S(2)}) copy-start(s32[16,8]{0,1:T(8,128)} %param.15) | copy-start | bytes 1540
  33.8 11.3 %copy-start.5 = (bf16[8,128,128]{2,1,0:T(8,128)(2,1)S(1)}, bf16[8,128,128]{2,1,0:T(8,128)(2,1)}, u32[]{:S(2)}) copy-start(bf16[8,128,128]{2,1,0:T(8,128)(2,1)} %copy-done.4) | copy-start | bytes 786436
  33.8 8.0 %collective-permute-start.6 = (bf16[128,512]{1,0:T(8,128)(2,1)S(1)}, bf16[128,512]{1,0:T(8,128)(2,1)S(1)}, u32[]{:S(2)}, u32[]{:S(2)}) collective-permute-start(bf16[128,512]{1,0:T(8,128)(2,1)S(1)} %get-tuple-element.39), channel_id=1, source_target_pairs={{0,2},{2,0},{4,6},{6,4},{1,3},{3,1},{5,7},{7,5},{8,10},{10,8},{12,... | collective-permute-start | bytes 393224 | tf_op jit(solution)/shard_map/ppermute | solution.py:221
  34.0 8.8 %collective-permute-start.7 = (bf16[128,512]{1,0:T(8,128)(2,1)S(1)}, bf16[128,512]{1,0:T(8,128)(2,1)S(1)}, u32[]{:S(2)}, u32[]{:S(2)}) collective-permute-start(bf16[128,512]{1,0:T(8,128)(2,1)S(1)} %get-tuple-element.40), channel_id=1, source_target_pairs={{0,6},{2,4},{4,2},{6,0},{1,7},{3,5},{5,3},{7,1},{8,14},{10,12},{12... | collective-permute-start | bytes 393224 | tf_op jit(solution)/shard_map/ppermute | solution.py:221
  34.6 9.5 %collective-permute-start.8 = (bf16[128,512]{1,0:T(8,128)(2,1)S(1)}, bf16[128,512]{1,0:T(8,128)(2,1)S(1)}, u32[]{:S(2)}, u32[]{:S(2)}) collective-permute-start(bf16[128,512]{1,0:T(8,128)(2,1)S(1)} %get-tuple-element.41), channel_id=1, source_target_pairs={{0,4},{2,6},{4,0},{6,2},{1,5},{3,7},{5,1},{7,3},{8,12},{10,14},{12... | collective-permute-start | bytes 393224 | tf_op jit(solution)/shard_map/ppermute | solution.py:221
  37.1 7.0 %collective-permute-start.12 = (bf16[128,512]{1,0:T(8,128)(2,1)S(1)}, bf16[128,512]{1,0:T(8,128)(2,1)S(1)}, u32[]{:S(2)}, u32[]{:S(2)}) collective-permute-start(bf16[128,512]{1,0:T(8,128)(2,1)S(1)} %get-tuple-element.47.rest_0_), channel_id=1, source_target_pairs={{0,1},{1,0},{2,3},{3,2},{4,5},{5,4},{6,7},{7,6},{8,9},{9,8},{10,11... | collective-permute-start | bytes 393224 | tf_op jit(solution)/shard_map/ppermute | solution.py:221
  41.7 2.4 %collective-permute-start.13 = (bf16[128,512]{1,0:T(8,128)(2,1)S(1)}, bf16[128,512]{1,0:T(8,128)(2,1)S(1)}, u32[]{:S(2)}, u32[]{:S(2)}) collective-permute-start(bf16[128,512]{1,0:T(8,128)(2,1)S(1)} %collective-permute-done.10.rest_1_), channel_id=1, source_target_pairs={{0,1},{1,0},{2,3},{3,2},{4,5},{5,4},{6,7},{7,6},{8,9},{9,8},{10,11... | collective-permute-start | bytes 393224 | tf_op jit(solution)/shard_map/ppermute | solution.py:221
  41.7 2.4 %collective-permute-start.14 = (bf16[128,512]{1,0:T(8,128)(2,1)S(1)}, bf16[128,512]{1,0:T(8,128)(2,1)S(1)}, u32[]{:S(2)}, u32[]{:S(2)}) collective-permute-start(bf16[128,512]{1,0:T(8,128)(2,1)S(1)} %collective-permute-done.9.rest_2_), channel_id=1, source_target_pairs={{0,1},{1,0},{2,3},{3,2},{4,5},{5,4},{6,7},{7,6},{8,9},{9,8},{10,11... | collective-permute-start | bytes 393224 | tf_op jit(solution)/shard_map/ppermute | solution.py:221
  42.7 2.3 %collective-permute-start.15 = (bf16[128,512]{1,0:T(8,128)(2,1)S(1)}, bf16[128,512]{1,0:T(8,128)(2,1)S(1)}, u32[]{:S(2)}, u32[]{:S(2)}) collective-permute-start(bf16[128,512]{1,0:T(8,128)(2,1)S(1)} %collective-permute-done.11.rest_3_), channel_id=1, source_target_pairs={{0,1},{1,0},{2,3},{3,2},{4,5},{5,4},{6,7},{7,6},{8,9},{9,8},{10,11... | collective-permute-start | bytes 393224 | tf_op jit(solution)/shard_map/ppermute | solution.py:221
  (5 other events, 8.8 us)

commit v5 on v4

--- a/solution.py
+++ b/solution.py
@@ -251,6 +251,7 @@
     def mine(lists):
         return lax.dynamic_slice_in_dim(lists, row * RING, RING, 0)
 
+    near_lists = [mine(part) for part in (opp_list, opp_kind, alpha_list, alpha_kind)]
     pieces = exchanged(cut(own))
     other = swapped(own, "beta", 1)
     same, turned = same_part(
@@ -258,9 +259,9 @@
     )
     even, odd = edges(pieces)
     even, odd = handed(even, 0), handed(odd, 1)
-    even, odd, same = lax.optimization_barrier((even, odd, same))
-    half = exchanged(near(mine(opp_list), mine(opp_kind), pieces, even, odd, opp_alpha_table, "half"))
-    formed = near(mine(alpha_list), mine(alpha_kind), pieces, even, odd, alpha_table, "alpha")
+    even, odd, same, near_lists = lax.optimization_barrier((even, odd, same, near_lists))
+    half = exchanged(near(*near_lists[:2], pieces, even, odd, opp_alpha_table, "half"))
+    formed = near(*near_lists[2:], pieces, even, odd, alpha_table, "alpha")
     half = [half[d] for d in (0, 2, 1, 3)]
     half, mark = lax.optimization_barrier((half, formed[0]))
     half = [half[d] for d in (0, 2, 1, 3)]

time: 48.4 us -> 47.6 us (0.983)
  waiting for transfers between devices: 8.22 us -> 6.87 us
  local copies, waits for them, and re-layouts: 2.08 us -> 3.16 us
  Pallas kernels: 10.8 us -> 10.2 us
    ppermute x2, waiting for transfers between devices: 2.95 us -> 1.59 us  [handed(): lax.ppermute(value, 'row', pairs + [(there, here) for here, there in pairs])]
    unnamed x33 -> x29, local copies, waits for them, and re-layouts: 1.93 us -> 2.64 us
    pallas_call x2, Pallas kernels: 2.91 us -> 2.26 us  [near(): pl.pallas_call(functools.partial(near_kernel, links), out_shape=[piece] *...]
where the time goes in v5:
time: 47.6 us; the launch traced here: 47.3 us
  starting transfers between devices  27 us (57%)
  Pallas kernels  10.2 us (21%)
  waiting for transfers between devices  6.87 us (14%)
  local copies, waits for them, and re-layouts  3.16 us (7%)
    ppermute x14, starting transfers between devices, swapped(): lax.ppermute(value, axis, [(i, i ^ flip) for i in range(lax.axis_size(axi...  18.6 us
    ppermute x2, starting transfers between devices, handed(): lax.ppermute(value, 'row', pairs + [(there, here) for here, there in pairs])  8.38 us
    ppermute x14, waiting for transfers between devices, swapped(): lax.ppermute(value, axis, [(i, i ^ flip) for i in range(lax.axis_size(axi...  5.28 us
    pallas_call x1, Pallas kernels, mixed_part(): pl.pallas_call(functools.partial(mixed_kernel, sources.shape[1]), out_sha...  3.17 us
    pallas_call x1, Pallas kernels, same_part(): pl.pallas_call(functools.partial(same_kernel, sources.shape[1]), out_shap...  2.7 us
    unnamed x29, local copies, waits for them, and re-layouts  2.64 us
    pallas_call x2, Pallas kernels, near(): pl.pallas_call(functools.partial(near_kernel, links), out_shape=[piece] *...  2.26 us
    ppermute x2, waiting for transfers between devices, handed(): lax.ppermute(value, 'row', pairs + [(there, here) for here, there in pairs])  1.59 us
  transfers between devices with their start and end apart: 16, of which 4 were waited for; matrix products, arithmetic and copies ran while one was open for 2% of the time, Pallas kernels for 10%

profile of v5, /device:TPU:25, one launch (start us, length us, event | category | flops | bytes accessed | tf_op | source)
XLA Modules:
  0.0 47.3 jit_solution(18322747312155767453)
XLA Ops:
  0.0 1.1 %cut.1 = (bf16[128,512]{1,0:T(8,128)(2,1)S(1)}, bf16[128,512]{1,0:T(8,128)(2,1)S(1)}, bf16[128,512]{1,0:T(8,128)(2,1)S(1)}, bf16[128,512]{1,0:T(8,128)(2,1)S(1)}) custom-call(bf16[128,2048]{1,0:T(8,128)(2,1)} %bitcast.own.whole), custom_call_target="tpu_custom_call" | custom-call | bytes 1048576 | tf_op jit(solution)/shard_map/cut/pallas_call | solution.py:36
  1.1 1.3 %collective-permute-start.1 = (bf16[128,512]{1,0:T(8,128)(2,1)S(1)}, bf16[128,512]{1,0:T(8,128)(2,1)S(1)}, u32[]{:S(2)}, u32[]{:S(2)}) collective-permute-start(bf16[128,512]{1,0:T(8,128)(2,1)S(1)} %get-tuple-element.34), channel_id=1, source_target_pairs={{0,2},{2,0},{4,6},{6,4},{1,3},{3,1},{5,7},{7,5},{8,10},{10,8},{12,... | collective-permute-start | bytes 393224 | tf_op jit(solution)/shard_map/ppermute | solution.py:221
  2.4 1.8 %collective-permute-start.2 = (bf16[128,512]{1,0:T(8,128)(2,1)S(1)}, bf16[128,512]{1,0:T(8,128)(2,1)S(1)}, u32[]{:S(2)}, u32[]{:S(2)}) collective-permute-start(bf16[128,512]{1,0:T(8,128)(2,1)S(1)} %get-tuple-element.35), channel_id=1, source_target_pairs={{0,6},{2,4},{4,2},{6,0},{1,7},{3,5},{5,3},{7,1},{8,14},{10,12},{12... | collective-permute-start | bytes 393224 | tf_op jit(solution)/shard_map/ppermute | solution.py:221
  4.2 0.6 %collective-permute-start.3 = (bf16[128,512]{1,0:T(8,128)(2,1)S(1)}, bf16[128,512]{1,0:T(8,128)(2,1)S(1)}, u32[]{:S(2)}, u32[]{:S(2)}) collective-permute-start(bf16[128,512]{1,0:T(8,128)(2,1)S(1)} %get-tuple-element.36), channel_id=1, source_target_pairs={{0,4},{2,6},{4,0},{6,2},{1,5},{3,7},{5,1},{7,3},{8,12},{10,14},{12... | collective-permute-start | bytes 393224 | tf_op jit(solution)/shard_map/ppermute | solution.py:221
  4.8 1.2 %collective-permute-start = (bf16[128,2048]{1,0:T(8,128)(2,1)}, bf16[128,2048]{1,0:T(8,128)(2,1)S(1)}, u32[]{:S(2)}, u32[]{:S(2)}) collective-permute-start(bf16[128,2048]{1,0:T(8,128)(2,1)} %bitcast.own.whole), channel_id=1, source_target_pairs={{0,1},{1,0},{2,3},{3,2},{4,5},{5,4},{6,7},{7,6},{8,9},{9,8},{10,11... | collective-permute-start | bytes 1572872 | tf_op jit(solution)/shard_map/ppermute | solution.py:221
  6.1 1.3 %collective-permute-done.2.p3 = bf16[128,512]{1,0:T(8,128)(2,1)S(1)} collective-permute-done((bf16[128,512]{1,0:T(8,128)(2,1)S(1)}, bf16[128,512]{1,0:T(8,128)(2,1)S(1)}, u32[]{:S(2)}, u32[]{:S(2)}) %collective-permute-start.2) | collective-permute-done | bytes 131104 | tf_op jit(solution)/shard_map/ppermute | solution.py:221
  7.4 3.0 %collective-permute-done.3.p2 = bf16[128,512]{1,0:T(8,128)(2,1)S(1)} collective-permute-done((bf16[128,512]{1,0:T(8,128)(2,1)S(1)}, bf16[128,512]{1,0:T(8,128)(2,1)S(1)}, u32[]{:S(2)}, u32[]{:S(2)}) %collective-permute-start.3) | collective-permute-done | bytes 131104 | tf_op jit(solution)/shard_map/ppermute | solution.py:221
  10.4 0.9 %edges.1 = (bf16[3,128,512]{2,1,0:T(8,128)(2,1)}, bf16[3,128,512]{2,1,0:T(8,128)(2,1)}) custom-call(bf16[128,512]{1,0:T(8,128)(2,1)S(1)} %get-tuple-element.33.p0, bf16[128,512]{1,0:T(8,128)(2,1)S(1)} %collective-permute-done.1.p1, bf16[128,512]{1,0:T(8,128)(2,1)S(1)} %collective-permute-done.2.p3, bf16[128,512]{1,0:T(8,128)(2,1)S(1)} %collective-permute-done.3.p2), custom_call_target="tpu_custom_call" | custom-call | bytes 1572864 | tf_op jit(solution)/shard_map/edges/pallas_call | solution.py:63
  11.4 1.6 %collective-permute-start.4 = (bf16[3,128,512]{2,1,0:T(8,128)(2,1)}, bf16[3,128,512]{2,1,0:T(8,128)(2,1)S(1)}, u32[]{:S(2)}, u32[]{:S(2)}) collective-permute-start(bf16[3,128,512]{2,1,0:T(8,128)(2,1)} %get-tuple-element.37), channel_id=1, source_target_pairs={{0,8},{16,24},{32,40},{48,56},{64,72},{80,88},{96,104},{112,120},{... | collective-permute-start | bytes 1179656 | tf_op jit(solution)/shard_map/ppermute | solution.py:231
  13.0 6.7 %collective-permute-start.5 = (bf16[3,128,512]{2,1,0:T(8,128)(2,1)}, bf16[3,128,512]{2,1,0:T(8,128)(2,1)S(1)}, u32[]{:S(2)}, u32[]{:S(2)}) collective-permute-start(bf16[3,128,512]{2,1,0:T(8,128)(2,1)} %get-tuple-element.38), channel_id=1, source_target_pairs={{8,16},{24,32},{40,48},{56,64},{72,80},{88,96},{104,112},{120,128}... | collective-permute-start | bytes 1179656 | tf_op jit(solution)/shard_map/ppermute | solution.py:231
  19.8 0.7 %copy-done.10 = s32[128,3]{0,1:T(4,128)S(1)} copy-done((s32[128,3]{0,1:T(4,128)S(1)}, s32[128,3]{0,1:T(4,128)}, u32[]{:S(2)}) %copy-start.10) | copy-done | bytes 1560
  22.2 0.6 %copy-done.7 = s32[16,8]{0,1:T(8,128)S(1)} copy-done((s32[16,8]{0,1:T(8,128)S(1)}, s32[16,8]{0,1:T(8,128)}, u32[]{:S(2)}) %copy-start.7) | copy-done | bytes 536
  22.9 2.7 %same.1 = (f32[128,2048]{1,0:T(8,128)S(1)}, bf16[8,128,128]{2,1,0:T(8,128)(2,1)S(1)}) custom-call(s32[16,8]{1,0:T(8,128)S(1)} %copy.19.sources, s32[16,8]{1,0:T(8,128)S(1)} %copy.14.kinds, bf16[128,2048]{1,0:T(8,128)(2,1)} %bitcast.own.whole, bf16[128,2048]{1,0:T(8,128)(2,1)S(1)} %collective-permute-done.other, bf16[8,128,128]{2,1,0:T(8,128)(2,1)S(1)} %copy-done, ...), custom_call_target="tpu_custom_call" | custom-call | bytes 262144 | tf_op jit(solution)/shard_map/same/pallas_call | solution.py:146
  25.6 1.6 %collective-permute-done.5.odd = bf16[3,128,512]{2,1,0:T(8,128)(2,1)S(1)} collective-permute-done((bf16[3,128,512]{2,1,0:T(8,128)(2,1)}, bf16[3,128,512]{2,1,0:T(8,128)(2,1)S(1)}, u32[]{:S(2)}, u32[]{:S(2)}) %collective-permute-start.5) | collective-permute-done | bytes 393248 | tf_op jit(solution)/shard_map/ppermute | solution.py:231
  27.2 1.1 %half.1 = (bf16[128,512]{1,0:T(8,128)(2,1)S(1)}, bf16[128,512]{1,0:T(8,128)(2,1)S(1)}, bf16[128,512]{1,0:T(8,128)(2,1)S(1)}, bf16[128,512]{1,0:T(8,128)(2,1)S(1)}) custom-call(s32[4,3]{1,0:T(4,128)S(1)} %copy.21.sources, s32[4,3]{1,0:T(4,128)S(1)} %copy.22.kinds, bf16[128,512]{1,0:T(8,128)(2,1)S(1)} %get-tuple-element.33.p0, ...), custom_call_target="tpu_custom_call" | custom-call | bytes 65536 | tf_op jit(solution)/shard_map/half/pallas_call | solution.py:101
  28.9 2.8 %collective-permute-start.9 = (bf16[128,512]{1,0:T(8,128)(2,1)S(1)}, bf16[128,512]{1,0:T(8,128)(2,1)S(1)}, u32[]{:S(2)}, u32[]{:S(2)}) collective-permute-start(bf16[128,512]{1,0:T(8,128)(2,1)S(1)} %get-tuple-element.51), channel_id=1, source_target_pairs={{0,4},{2,6},{4,0},{6,2},{1,5},{3,7},{5,1},{7,3},{8,12},{10,14},{12... | collective-permute-start | bytes 393224 | tf_op jit(solution)/shard_map/ppermute | solution.py:221
  31.7 1.1 %alpha.1 = (bf16[128,512]{1,0:T(8,128)(2,1)S(1)}, bf16[128,512]{1,0:T(8,128)(2,1)S(1)}, bf16[128,512]{1,0:T(8,128)(2,1)S(1)}, bf16[128,512]{1,0:T(8,128)(2,1)S(1)}) custom-call(s32[4,4]{1,0:T(4,128)S(1)} %copy.23.sources, s32[4,4]{1,0:T(4,128)S(1)} %copy.24.kinds, bf16[128,512]{1,0:T(8,128)(2,1)S(1)} %get-tuple-element.33.p0, ...), custom_call_target="tpu_custom_call" | custom-call | bytes 65536 | tf_op jit(solution)/shard_map/alpha/pallas_call | solution.py:101
  33.0 0.6 %collective-permute-start.7 = (bf16[128,512]{1,0:T(8,128)(2,1)S(1)}, bf16[128,512]{1,0:T(8,128)(2,1)S(1)}, u32[]{:S(2)}, u32[]{:S(2)}) collective-permute-start(bf16[128,512]{1,0:T(8,128)(2,1)S(1)} %get-tuple-element.46), channel_id=1, source_target_pairs={{0,6},{2,4},{4,2},{6,0},{1,7},{3,5},{5,3},{7,1},{8,14},{10,12},{12... | collective-permute-start | bytes 393224 | tf_op jit(solution)/shard_map/ppermute | solution.py:221
  33.7 2.6 %collective-permute-start.8 = (bf16[128,512]{1,0:T(8,128)(2,1)S(1)}, bf16[128,512]{1,0:T(8,128)(2,1)S(1)}, u32[]{:S(2)}, u32[]{:S(2)}) collective-permute-start(bf16[128,512]{1,0:T(8,128)(2,1)S(1)} %get-tuple-element.47), channel_id=1, source_target_pairs={{0,4},{2,6},{4,0},{6,2},{1,5},{3,7},{5,1},{7,3},{8,12},{10,14},{12... | collective-permute-start | bytes 393224 | tf_op jit(solution)/shard_map/ppermute | solution.py:221
  36.2 4.7 %collective-permute-start.12 = (bf16[128,512]{1,0:T(8,128)(2,1)S(1)}, bf16[128,512]{1,0:T(8,128)(2,1)S(1)}, u32[]{:S(2)}, u32[]{:S(2)}) collective-permute-start(bf16[128,512]{1,0:T(8,128)(2,1)S(1)} %get-tuple-element.55.rest_0_), channel_id=1, source_target_pairs={{0,1},{1,0},{2,3},{3,2},{4,5},{5,4},{6,7},{7,6},{8,9},{9,8},{10,11... | collective-permute-start | bytes 393224 | tf_op jit(solution)/shard_map/ppermute | solution.py:221
  40.9 1.0 %collective-permute-start.14 = (bf16[128,512]{1,0:T(8,128)(2,1)S(1)}, bf16[128,512]{1,0:T(8,128)(2,1)S(1)}, u32[]{:S(2)}, u32[]{:S(2)}) collective-permute-start(bf16[128,512]{1,0:T(8,128)(2,1)S(1)} %collective-permute-done.9.rest_2_), channel_id=1, source_target_pairs={{0,1},{1,0},{2,3},{3,2},{4,5},{5,4},{6,7},{7,6},{8,9},{9,8},{10,11... | collective-permute-start | bytes 393224 | tf_op jit(solution)/shard_map/ppermute | solution.py:221
  41.9 1.3 %collective-permute-start.15 = (bf16[128,512]{1,0:T(8,128)(2,1)S(1)}, bf16[128,512]{1,0:T(8,128)(2,1)S(1)}, u32[]{:S(2)}, u32[]{:S(2)}) collective-permute-start(bf16[128,512]{1,0:T(8,128)(2,1)S(1)} %collective-permute-done.11.rest_3_), channel_id=1, source_target_pairs={{0,1},{1,0},{2,3},{3,2},{4,5},{5,4},{6,7},{7,6},{8,9},{9,8},{10,11... | collective-permute-start | bytes 393224 | tf_op jit(solution)/shard_map/ppermute | solution.py:221
  43.3 0.9 %collective-permute-done.15.rest_7_ = bf16[128,512]{1,0:T(8,128)(2,1)S(1)} collective-permute-done((bf16[128,512]{1,0:T(8,128)(2,1)S(1)}, bf16[128,512]{1,0:T(8,128)(2,1)S(1)}, u32[]{:S(2)}, u32[]{:S(2)}) %collective-permute-start.15) | collective-permute-done | bytes 131104 | tf_op jit(solution)/shard_map/ppermute | solution.py:221
  44.2 3.2 %mixed.1 = bf16[128,2048]{1,0:T(8,128)(2,1)} custom-call(s32[16,8]{1,0:T(8,128)S(1)} %copy.19.sources, s32[16,8]{1,0:T(8,128)S(1)} %copy.20.kinds, bf16[8,128,128]{2,1,0:T(8,128)(2,1)S(1)} %copy-done.5, f32[128,2048]{1,0:T(8,128)S(1)} %get-tuple-element.40.start, f32[8,128]{1,0:T(8,128)S(1)} %mark.1, bf16[128,512]{1,0:T(8,128)(2,1)S(1)} %get-tuple-element.55.rest_0_, ...), custom_call_target="tpu_custom_call" | custom-call | bytes 262144 | tf_op jit(solution)/shard_map/mixed/pallas_call | solution.py:189
  (50 shorter events, 2.6 us)
Async XLA Ops:
  1.1 5.0 %collective-permute-start.1 = (bf16[128,512]{1,0:T(8,128)(2,1)S(1)}, bf16[128,512]{1,0:T(8,128)(2,1)S(1)}, u32[]{:S(2)}, u32[]{:S(2)}) collective-permute-start(bf16[128,512]{1,0:T(8,128)(2,1)S(1)} %get-tuple-element.34), channel_id=1, source_target_pairs={{0,2},{2,0},{4,6},{6,4},{1,3},{3,1},{5,7},{7,5},{8,10},{10,8},{12,... | collective-permute-start | bytes 393224 | tf_op jit(solution)/shard_map/ppermute | solution.py:221
  2.4 5.0 %collective-permute-start.2 = (bf16[128,512]{1,0:T(8,128)(2,1)S(1)}, bf16[128,512]{1,0:T(8,128)(2,1)S(1)}, u32[]{:S(2)}, u32[]{:S(2)}) collective-permute-start(bf16[128,512]{1,0:T(8,128)(2,1)S(1)} %get-tuple-element.35), channel_id=1, source_target_pairs={{0,6},{2,4},{4,2},{6,0},{1,7},{3,5},{5,3},{7,1},{8,14},{10,12},{12... | collective-permute-start | bytes 393224 | tf_op jit(solution)/shard_map/ppermute | solution.py:221
  4.2 6.2 %collective-permute-start.3 = (bf16[128,512]{1,0:T(8,128)(2,1)S(1)}, bf16[128,512]{1,0:T(8,128)(2,1)S(1)}, u32[]{:S(2)}, u32[]{:S(2)}) collective-permute-start(bf16[128,512]{1,0:T(8,128)(2,1)S(1)} %get-tuple-element.36), channel_id=1, source_target_pairs={{0,4},{2,6},{4,0},{6,2},{1,5},{3,7},{5,1},{7,3},{8,12},{10,14},{12... | collective-permute-start | bytes 393224 | tf_op jit(solution)/shard_map/ppermute | solution.py:221
  4.8 18.1 %collective-permute-start = (bf16[128,2048]{1,0:T(8,128)(2,1)}, bf16[128,2048]{1,0:T(8,128)(2,1)S(1)}, u32[]{:S(2)}, u32[]{:S(2)}) collective-permute-start(bf16[128,2048]{1,0:T(8,128)(2,1)} %bitcast.own.whole), channel_id=1, source_target_pairs={{0,1},{1,0},{2,3},{3,2},{4,5},{5,4},{6,7},{7,6},{8,9},{9,8},{10,11... | collective-permute-start | bytes 1572872 | tf_op jit(solution)/shard_map/ppermute | solution.py:221
  10.4 12.4 %copy-start = (bf16[8,128,128]{2,1,0:T(8,128)(2,1)S(1)}, bf16[8,128,128]{2,1,0:T(8,128)(2,1)}, u32[]{:S(2)}) copy-start(bf16[8,128,128]{2,1,0:T(8,128)(2,1)} %table.3) | copy-start | bytes 786436
  10.4 12.4 %copy-start.1 = (bf16[8,128,128]{2,1,0:T(8,128)(2,1)S(1)}, bf16[8,128,128]{2,1,0:T(8,128)(2,1)}, u32[]{:S(2)}) copy-start(bf16[8,128,128]{2,1,0:T(8,128)(2,1)} %opp_table.1) | copy-start | bytes 786436
  11.4 14.2 %collective-permute-start.4 = (bf16[3,128,512]{2,1,0:T(8,128)(2,1)}, bf16[3,128,512]{2,1,0:T(8,128)(2,1)S(1)}, u32[]{:S(2)}, u32[]{:S(2)}) collective-permute-start(bf16[3,128,512]{2,1,0:T(8,128)(2,1)} %get-tuple-element.37), channel_id=1, source_target_pairs={{0,8},{16,24},{32,40},{48,56},{64,72},{80,88},{96,104},{112,120},{... | collective-permute-start | bytes 1179656 | tf_op jit(solution)/shard_map/ppermute | solution.py:231
  13.0 14.2 %collective-permute-start.5 = (bf16[3,128,512]{2,1,0:T(8,128)(2,1)}, bf16[3,128,512]{2,1,0:T(8,128)(2,1)S(1)}, u32[]{:S(2)}, u32[]{:S(2)}) collective-permute-start(bf16[3,128,512]{2,1,0:T(8,128)(2,1)} %get-tuple-element.38), channel_id=1, source_target_pairs={{8,16},{24,32},{40,48},{56,64},{72,80},{88,96},{104,112},{120,128}... | collective-permute-start | bytes 1179656 | tf_op jit(solution)/shard_map/ppermute | solution.py:231
  20.7 0.7 %copy-start.12 = (s32[128,4]{0,1:T(4,128)S(1)}, s32[128,4]{0,1:T(4,128)}, u32[]{:S(2)}) copy-start(s32[128,4]{0,1:T(4,128)} %param.16) | copy-start | bytes 6148
  22.9 4.3 %copy-start.2 = (bf16[8,128,128]{2,1,0:T(8,128)(2,1)S(1)}, bf16[8,128,128]{2,1,0:T(8,128)(2,1)}, u32[]{:S(2)}) copy-start(bf16[8,128,128]{2,1,0:T(8,128)(2,1)} %table.5) | copy-start | bytes 786436
  25.6 2.7 %copy-start.4 = (bf16[8,128,128]{2,1,0:T(8,128)(2,1)}, bf16[8,128,128]{2,1,0:T(8,128)(2,1)S(1)}, u32[]{:S(2)}) copy-start(bf16[8,128,128]{2,1,0:T(8,128)(2,1)S(1)} %get-tuple-element.32.table) | copy-start | bytes 786436
  27.2 4.5 %copy-start.3 = (bf16[8,128,128]{2,1,0:T(8,128)(2,1)S(1)}, bf16[8,128,128]{2,1,0:T(8,128)(2,1)}, u32[]{:S(2)}) copy-start(bf16[8,128,128]{2,1,0:T(8,128)(2,1)} %table.4) | copy-start | bytes 786436
  28.4 5.3 %collective-permute-start.10 = (bf16[128,512]{1,0:T(8,128)(2,1)S(1)}, bf16[128,512]{1,0:T(8,128)(2,1)S(1)}, u32[]{:S(2)}, u32[]{:S(2)}) collective-permute-start(bf16[128,512]{1,0:T(8,128)(2,1)S(1)} %get-tuple-element.52), channel_id=1, source_target_pairs={{0,2},{2,0},{4,6},{6,4},{1,3},{3,1},{5,7},{7,5},{8,10},{10,8},{12,... | collective-permute-start | bytes 393224 | tf_op jit(solution)/shard_map/ppermute | solution.py:221
  28.5 7.7 %collective-permute-start.11 = (bf16[128,512]{1,0:T(8,128)(2,1)S(1)}, bf16[128,512]{1,0:T(8,128)(2,1)S(1)}, u32[]{:S(2)}, u32[]{:S(2)}) collective-permute-start(bf16[128,512]{1,0:T(8,128)(2,1)S(1)} %get-tuple-element.53), channel_id=1, source_target_pairs={{0,6},{2,4},{4,2},{6,0},{1,7},{3,5},{5,3},{7,1},{8,14},{10,12},{12... | collective-permute-start | bytes 393224 | tf_op jit(solution)/shard_map/ppermute | solution.py:221
  28.9 7.3 %collective-permute-start.9 = (bf16[128,512]{1,0:T(8,128)(2,1)S(1)}, bf16[128,512]{1,0:T(8,128)(2,1)S(1)}, u32[]{:S(2)}, u32[]{:S(2)}) collective-permute-start(bf16[128,512]{1,0:T(8,128)(2,1)S(1)} %get-tuple-element.51), channel_id=1, source_target_pairs={{0,4},{2,6},{4,0},{6,2},{1,5},{3,7},{5,1},{7,3},{8,12},{10,14},{12... | collective-permute-start | bytes 393224 | tf_op jit(solution)/shard_map/ppermute | solution.py:221
  31.7 11.5 %copy-start.8 = (s32[16,8]{0,1:T(8,128)S(1)}, s32[16,8]{0,1:T(8,128)}, u32[]{:S(2)}) copy-start(s32[16,8]{0,1:T(8,128)} %param.15) | copy-start | bytes 1540
  32.9 11.3 %copy-start.5 = (bf16[8,128,128]{2,1,0:T(8,128)(2,1)S(1)}, bf16[8,128,128]{2,1,0:T(8,128)(2,1)}, u32[]{:S(2)}) copy-start(bf16[8,128,128]{2,1,0:T(8,128)(2,1)} %copy-done.4) | copy-start | bytes 786436
  32.9 8.0 %collective-permute-start.6 = (bf16[128,512]{1,0:T(8,128)(2,1)S(1)}, bf16[128,512]{1,0:T(8,128)(2,1)S(1)}, u32[]{:S(2)}, u32[]{:S(2)}) collective-permute-start(bf16[128,512]{1,0:T(8,128)(2,1)S(1)} %get-tuple-element.45), channel_id=1, source_target_pairs={{0,2},{2,0},{4,6},{6,4},{1,3},{3,1},{5,7},{7,5},{8,10},{10,8},{12,... | collective-permute-start | bytes 393224 | tf_op jit(solution)/shard_map/ppermute | solution.py:221
  33.0 8.8 %collective-permute-start.7 = (bf16[128,512]{1,0:T(8,128)(2,1)S(1)}, bf16[128,512]{1,0:T(8,128)(2,1)S(1)}, u32[]{:S(2)}, u32[]{:S(2)}) collective-permute-start(bf16[128,512]{1,0:T(8,128)(2,1)S(1)} %get-tuple-element.46), channel_id=1, source_target_pairs={{0,6},{2,4},{4,2},{6,0},{1,7},{3,5},{5,3},{7,1},{8,14},{10,12},{12... | collective-permute-start | bytes 393224 | tf_op jit(solution)/shard_map/ppermute | solution.py:221
  33.7 9.6 %collective-permute-start.8 = (bf16[128,512]{1,0:T(8,128)(2,1)S(1)}, bf16[128,512]{1,0:T(8,128)(2,1)S(1)}, u32[]{:S(2)}, u32[]{:S(2)}) collective-permute-start(bf16[128,512]{1,0:T(8,128)(2,1)S(1)} %get-tuple-element.47), channel_id=1, source_target_pairs={{0,4},{2,6},{4,0},{6,2},{1,5},{3,7},{5,1},{7,3},{8,12},{10,14},{12... | collective-permute-start | bytes 393224 | tf_op jit(solution)/shard_map/ppermute | solution.py:221
  36.2 7.0 %collective-permute-start.12 = (bf16[128,512]{1,0:T(8,128)(2,1)S(1)}, bf16[128,512]{1,0:T(8,128)(2,1)S(1)}, u32[]{:S(2)}, u32[]{:S(2)}) collective-permute-start(bf16[128,512]{1,0:T(8,128)(2,1)S(1)} %get-tuple-element.55.rest_0_), channel_id=1, source_target_pairs={{0,1},{1,0},{2,3},{3,2},{4,5},{5,4},{6,7},{7,6},{8,9},{9,8},{10,11... | collective-permute-start | bytes 393224 | tf_op jit(solution)/shard_map/ppermute | solution.py:221
  40.9 2.4 %collective-permute-start.13 = (bf16[128,512]{1,0:T(8,128)(2,1)S(1)}, bf16[128,512]{1,0:T(8,128)(2,1)S(1)}, u32[]{:S(2)}, u32[]{:S(2)}) collective-permute-start(bf16[128,512]{1,0:T(8,128)(2,1)S(1)} %collective-permute-done.10.rest_1_), channel_id=1, source_target_pairs={{0,1},{1,0},{2,3},{3,2},{4,5},{5,4},{6,7},{7,6},{8,9},{9,8},{10,11... | collective-permute-start | bytes 393224 | tf_op jit(solution)/shard_map/ppermute | solution.py:221
  40.9 2.4 %collective-permute-start.14 = (bf16[128,512]{1,0:T(8,128)(2,1)S(1)}, bf16[128,512]{1,0:T(8,128)(2,1)S(1)}, u32[]{:S(2)}, u32[]{:S(2)}) collective-permute-start(bf16[128,512]{1,0:T(8,128)(2,1)S(1)} %collective-permute-done.9.rest_2_), channel_id=1, source_target_pairs={{0,1},{1,0},{2,3},{3,2},{4,5},{5,4},{6,7},{7,6},{8,9},{9,8},{10,11... | collective-permute-start | bytes 393224 | tf_op jit(solution)/shard_map/ppermute | solution.py:221
  41.9 2.3 %collective-permute-start.15 = (bf16[128,512]{1,0:T(8,128)(2,1)S(1)}, bf16[128,512]{1,0:T(8,128)(2,1)S(1)}, u32[]{:S(2)}, u32[]{:S(2)}) collective-permute-start(bf16[128,512]{1,0:T(8,128)(2,1)S(1)} %collective-permute-done.11.rest_3_), channel_id=1, source_target_pairs={{0,1},{1,0},{2,3},{3,2},{4,5},{5,4},{6,7},{7,6},{8,9},{9,8},{10,11... | collective-permute-start | bytes 393224 | tf_op jit(solution)/shard_map/ppermute | solution.py:221
  (5 other events, 3.4 us)

commit v6 on v5

--- a/solution.py
+++ b/solution.py
@@ -21,13 +21,19 @@
     return pl.CostEstimate(flops=flops, bytes_accessed=moved, transcendentals=0)
 
 
-def cut_kernel(whole, *pieces):
+def cut_kernel(whole, *rest):
+    pieces, sems = rest[:RING], rest[RING]
     spot = lax.axis_index("ring")
     width = whole.shape[1] // RING
+    copies = []
     for d in range(RING):
         quarter = lax.bitwise_xor(spot, d)
         cols = pl.ds(pl.multiple_of(quarter * width, width), width)
-        pieces[d][...] = whole[:, cols]
+        copies.append(pltpu.make_async_copy(whole.at[:, cols], pieces[d], sems.at[d]))
+    for copy in copies:
+        copy.start()
+    for copy in copies:
+        copy.wait()
 
 
 def cut(whole):
@@ -36,8 +42,9 @@
     return pl.pallas_call(
         cut_kernel,
         out_shape=[piece] * RING,
-        in_specs=[VMEM],
+        in_specs=[ANY],
         out_specs=[VMEM] * RING,
+        scratch_shapes=[pltpu.SemaphoreType.DMA((RING,))],
         cost_estimate=cost(0, 4 * rows * cols),
         compiler_params=pltpu.CompilerParams(vmem_limit_bytes=LIMIT),
         name="cut",

time: 47.6 us -> 47.7 us (level)
  no operation moved by 1% of the time
where the time goes in v6:
time: 47.7 us; the launch traced here: 47.4 us
  starting transfers between devices  27 us (57%)
  Pallas kernels  10.2 us (21%)
  waiting for transfers between devices  6.89 us (14%)
  local copies, waits for them, and re-layouts  3.16 us (7%)
    ppermute x14, starting transfers between devices, swapped(): lax.ppermute(value, axis, [(i, i ^ flip) for i in range(lax.axis_size(axi...  18.6 us
    ppermute x2, starting transfers between devices, handed(): lax.ppermute(value, 'row', pairs + [(there, here) for here, there in pairs])  8.38 us
    ppermute x14, waiting for transfers between devices, swapped(): lax.ppermute(value, axis, [(i, i ^ flip) for i in range(lax.axis_size(axi...  5.28 us
    pallas_call x1, Pallas kernels, mixed_part(): pl.pallas_call(functools.partial(mixed_kernel, sources.shape[1]), out_sha...  3.17 us
    pallas_call x1, Pallas kernels, same_part(): pl.pallas_call(functools.partial(same_kernel, sources.shape[1]), out_shap...  2.7 us
    unnamed x29, local copies, waits for them, and re-layouts  2.64 us
    pallas_call x2, Pallas kernels, near(): pl.pallas_call(functools.partial(near_kernel, links), out_shape=[piece] *...  2.25 us
    ppermute x2, waiting for transfers between devices, handed(): lax.ppermute(value, 'row', pairs + [(there, here) for here, there in pairs])  1.6 us
  transfers between devices with their start and end apart: 16, of which 4 were waited for; matrix products, arithmetic and copies ran while one was open for 2% of the time, Pallas kernels for 10%

profile of v6, /device:TPU:25, one launch (start us, length us, event | category | flops | bytes accessed | tf_op | source)
XLA Modules:
  0.0 47.4 jit_solution(15281212206388033561)
XLA Ops:
  0.0 1.1 %cut.1 = (bf16[128,512]{1,0:T(8,128)(2,1)S(1)}, bf16[128,512]{1,0:T(8,128)(2,1)S(1)}, bf16[128,512]{1,0:T(8,128)(2,1)S(1)}, bf16[128,512]{1,0:T(8,128)(2,1)S(1)}) custom-call(bf16[128,2048]{1,0:T(8,128)(2,1)} %bitcast.own.whole), custom_call_target="tpu_custom_call" | custom-call | bytes 1048576 | tf_op jit(solution)/shard_map/cut/pallas_call | solution.py:42
  1.1 1.3 %collective-permute-start.1 = (bf16[128,512]{1,0:T(8,128)(2,1)S(1)}, bf16[128,512]{1,0:T(8,128)(2,1)S(1)}, u32[]{:S(2)}, u32[]{:S(2)}) collective-permute-start(bf16[128,512]{1,0:T(8,128)(2,1)S(1)} %get-tuple-element.34), channel_id=1, source_target_pairs={{0,2},{2,0},{4,6},{6,4},{1,3},{3,1},{5,7},{7,5},{8,10},{10,8},{12,... | collective-permute-start | bytes 393224 | tf_op jit(solution)/shard_map/ppermute | solution.py:228
  2.4 1.8 %collective-permute-start.2 = (bf16[128,512]{1,0:T(8,128)(2,1)S(1)}, bf16[128,512]{1,0:T(8,128)(2,1)S(1)}, u32[]{:S(2)}, u32[]{:S(2)}) collective-permute-start(bf16[128,512]{1,0:T(8,128)(2,1)S(1)} %get-tuple-element.35), channel_id=1, source_target_pairs={{0,6},{2,4},{4,2},{6,0},{1,7},{3,5},{5,3},{7,1},{8,14},{10,12},{12... | collective-permute-start | bytes 393224 | tf_op jit(solution)/shard_map/ppermute | solution.py:228
  4.3 0.6 %collective-permute-start.3 = (bf16[128,512]{1,0:T(8,128)(2,1)S(1)}, bf16[128,512]{1,0:T(8,128)(2,1)S(1)}, u32[]{:S(2)}, u32[]{:S(2)}) collective-permute-start(bf16[128,512]{1,0:T(8,128)(2,1)S(1)} %get-tuple-element.36), channel_id=1, source_target_pairs={{0,4},{2,6},{4,0},{6,2},{1,5},{3,7},{5,1},{7,3},{8,12},{10,14},{12... | collective-permute-start | bytes 393224 | tf_op jit(solution)/shard_map/ppermute | solution.py:228
  4.9 1.2 %collective-permute-start = (bf16[128,2048]{1,0:T(8,128)(2,1)}, bf16[128,2048]{1,0:T(8,128)(2,1)S(1)}, u32[]{:S(2)}, u32[]{:S(2)}) collective-permute-start(bf16[128,2048]{1,0:T(8,128)(2,1)} %bitcast.own.whole), channel_id=1, source_target_pairs={{0,1},{1,0},{2,3},{3,2},{4,5},{5,4},{6,7},{7,6},{8,9},{9,8},{10,11... | collective-permute-start | bytes 1572872 | tf_op jit(solution)/shard_map/ppermute | solution.py:228
  6.1 1.3 %collective-permute-done.2.p3 = bf16[128,512]{1,0:T(8,128)(2,1)S(1)} collective-permute-done((bf16[128,512]{1,0:T(8,128)(2,1)S(1)}, bf16[128,512]{1,0:T(8,128)(2,1)S(1)}, u32[]{:S(2)}, u32[]{:S(2)}) %collective-permute-start.2) | collective-permute-done | bytes 131104 | tf_op jit(solution)/shard_map/ppermute | solution.py:228
  7.5 3.0 %collective-permute-done.3.p2 = bf16[128,512]{1,0:T(8,128)(2,1)S(1)} collective-permute-done((bf16[128,512]{1,0:T(8,128)(2,1)S(1)}, bf16[128,512]{1,0:T(8,128)(2,1)S(1)}, u32[]{:S(2)}, u32[]{:S(2)}) %collective-permute-start.3) | collective-permute-done | bytes 131104 | tf_op jit(solution)/shard_map/ppermute | solution.py:228
  10.5 0.9 %edges.1 = (bf16[3,128,512]{2,1,0:T(8,128)(2,1)}, bf16[3,128,512]{2,1,0:T(8,128)(2,1)}) custom-call(bf16[128,512]{1,0:T(8,128)(2,1)S(1)} %get-tuple-element.33.p0, bf16[128,512]{1,0:T(8,128)(2,1)S(1)} %collective-permute-done.1.p1, bf16[128,512]{1,0:T(8,128)(2,1)S(1)} %collective-permute-done.2.p3, bf16[128,512]{1,0:T(8,128)(2,1)S(1)} %collective-permute-done.3.p2), custom_call_target="tpu_custom_call" | custom-call | bytes 1572864 | tf_op jit(solution)/shard_map/edges/pallas_call | solution.py:70
  11.5 1.6 %collective-permute-start.4 = (bf16[3,128,512]{2,1,0:T(8,128)(2,1)}, bf16[3,128,512]{2,1,0:T(8,128)(2,1)S(1)}, u32[]{:S(2)}, u32[]{:S(2)}) collective-permute-start(bf16[3,128,512]{2,1,0:T(8,128)(2,1)} %get-tuple-element.37), channel_id=1, source_target_pairs={{0,8},{16,24},{32,40},{48,56},{64,72},{80,88},{96,104},{112,120},{... | collective-permute-start | bytes 1179656 | tf_op jit(solution)/shard_map/ppermute | solution.py:238
  13.1 6.7 %collective-permute-start.5 = (bf16[3,128,512]{2,1,0:T(8,128)(2,1)}, bf16[3,128,512]{2,1,0:T(8,128)(2,1)S(1)}, u32[]{:S(2)}, u32[]{:S(2)}) collective-permute-start(bf16[3,128,512]{2,1,0:T(8,128)(2,1)} %get-tuple-element.38), channel_id=1, source_target_pairs={{8,16},{24,32},{40,48},{56,64},{72,80},{88,96},{104,112},{120,128}... | collective-permute-start | bytes 1179656 | tf_op jit(solution)/shard_map/ppermute | solution.py:238
  19.9 0.7 %copy-done.10 = s32[128,3]{0,1:T(4,128)S(1)} copy-done((s32[128,3]{0,1:T(4,128)S(1)}, s32[128,3]{0,1:T(4,128)}, u32[]{:S(2)}) %copy-start.10) | copy-done | bytes 1560
  22.3 0.6 %copy-done.7 = s32[16,8]{0,1:T(8,128)S(1)} copy-done((s32[16,8]{0,1:T(8,128)S(1)}, s32[16,8]{0,1:T(8,128)}, u32[]{:S(2)}) %copy-start.7) | copy-done | bytes 536
  23.0 2.7 %same.1 = (f32[128,2048]{1,0:T(8,128)S(1)}, bf16[8,128,128]{2,1,0:T(8,128)(2,1)S(1)}) custom-call(s32[16,8]{1,0:T(8,128)S(1)} %copy.19.sources, s32[16,8]{1,0:T(8,128)S(1)} %copy.14.kinds, bf16[128,2048]{1,0:T(8,128)(2,1)} %bitcast.own.whole, bf16[128,2048]{1,0:T(8,128)(2,1)S(1)} %collective-permute-done.other, bf16[8,128,128]{2,1,0:T(8,128)(2,1)S(1)} %copy-done, ...), custom_call_target="tpu_custom_call" | custom-call | bytes 262144 | tf_op jit(solution)/shard_map/same/pallas_call | solution.py:153
  25.7 1.6 %collective-permute-done.5.odd = bf16[3,128,512]{2,1,0:T(8,128)(2,1)S(1)} collective-permute-done((bf16[3,128,512]{2,1,0:T(8,128)(2,1)}, bf16[3,128,512]{2,1,0:T(8,128)(2,1)S(1)}, u32[]{:S(2)}, u32[]{:S(2)}) %collective-permute-start.5) | collective-permute-done | bytes 393248 | tf_op jit(solution)/shard_map/ppermute | solution.py:238
  27.3 1.1 %half.1 = (bf16[128,512]{1,0:T(8,128)(2,1)S(1)}, bf16[128,512]{1,0:T(8,128)(2,1)S(1)}, bf16[128,512]{1,0:T(8,128)(2,1)S(1)}, bf16[128,512]{1,0:T(8,128)(2,1)S(1)}) custom-call(s32[4,3]{1,0:T(4,128)S(1)} %copy.21.sources, s32[4,3]{1,0:T(4,128)S(1)} %copy.22.kinds, bf16[128,512]{1,0:T(8,128)(2,1)S(1)} %get-tuple-element.33.p0, ...), custom_call_target="tpu_custom_call" | custom-call | bytes 65536 | tf_op jit(solution)/shard_map/half/pallas_call | solution.py:108
  29.0 2.8 %collective-permute-start.9 = (bf16[128,512]{1,0:T(8,128)(2,1)S(1)}, bf16[128,512]{1,0:T(8,128)(2,1)S(1)}, u32[]{:S(2)}, u32[]{:S(2)}) collective-permute-start(bf16[128,512]{1,0:T(8,128)(2,1)S(1)} %get-tuple-element.51), channel_id=1, source_target_pairs={{0,4},{2,6},{4,0},{6,2},{1,5},{3,7},{5,1},{7,3},{8,12},{10,14},{12... | collective-permute-start | bytes 393224 | tf_op jit(solution)/shard_map/ppermute | solution.py:228
  31.8 1.1 %alpha.1 = (bf16[128,512]{1,0:T(8,128)(2,1)S(1)}, bf16[128,512]{1,0:T(8,128)(2,1)S(1)}, bf16[128,512]{1,0:T(8,128)(2,1)S(1)}, bf16[128,512]{1,0:T(8,128)(2,1)S(1)}) custom-call(s32[4,4]{1,0:T(4,128)S(1)} %copy.23.sources, s32[4,4]{1,0:T(4,128)S(1)} %copy.24.kinds, bf16[128,512]{1,0:T(8,128)(2,1)S(1)} %get-tuple-element.33.p0, ...), custom_call_target="tpu_custom_call" | custom-call | bytes 65536 | tf_op jit(solution)/shard_map/alpha/pallas_call | solution.py:108
  33.1 0.6 %collective-permute-start.7 = (bf16[128,512]{1,0:T(8,128)(2,1)S(1)}, bf16[128,512]{1,0:T(8,128)(2,1)S(1)}, u32[]{:S(2)}, u32[]{:S(2)}) collective-permute-start(bf16[128,512]{1,0:T(8,128)(2,1)S(1)} %get-tuple-element.46), channel_id=1, source_target_pairs={{0,6},{2,4},{4,2},{6,0},{1,7},{3,5},{5,3},{7,1},{8,14},{10,12},{12... | collective-permute-start | bytes 393224 | tf_op jit(solution)/shard_map/ppermute | solution.py:228
  33.7 2.5 %collective-permute-start.8 = (bf16[128,512]{1,0:T(8,128)(2,1)S(1)}, bf16[128,512]{1,0:T(8,128)(2,1)S(1)}, u32[]{:S(2)}, u32[]{:S(2)}) collective-permute-start(bf16[128,512]{1,0:T(8,128)(2,1)S(1)} %get-tuple-element.47), channel_id=1, source_target_pairs={{0,4},{2,6},{4,0},{6,2},{1,5},{3,7},{5,1},{7,3},{8,12},{10,14},{12... | collective-permute-start | bytes 393224 | tf_op jit(solution)/shard_map/ppermute | solution.py:228
  36.3 4.7 %collective-permute-start.12 = (bf16[128,512]{1,0:T(8,128)(2,1)S(1)}, bf16[128,512]{1,0:T(8,128)(2,1)S(1)}, u32[]{:S(2)}, u32[]{:S(2)}) collective-permute-start(bf16[128,512]{1,0:T(8,128)(2,1)S(1)} %get-tuple-element.55.rest_0_), channel_id=1, source_target_pairs={{0,1},{1,0},{2,3},{3,2},{4,5},{5,4},{6,7},{7,6},{8,9},{9,8},{10,11... | collective-permute-start | bytes 393224 | tf_op jit(solution)/shard_map/ppermute | solution.py:228
  40.9 1.0 %collective-permute-start.14 = (bf16[128,512]{1,0:T(8,128)(2,1)S(1)}, bf16[128,512]{1,0:T(8,128)(2,1)S(1)}, u32[]{:S(2)}, u32[]{:S(2)}) collective-permute-start(bf16[128,512]{1,0:T(8,128)(2,1)S(1)} %collective-permute-done.9.rest_2_), channel_id=1, source_target_pairs={{0,1},{1,0},{2,3},{3,2},{4,5},{5,4},{6,7},{7,6},{8,9},{9,8},{10,11... | collective-permute-start | bytes 393224 | tf_op jit(solution)/shard_map/ppermute | solution.py:228
  41.9 1.3 %collective-permute-start.15 = (bf16[128,512]{1,0:T(8,128)(2,1)S(1)}, bf16[128,512]{1,0:T(8,128)(2,1)S(1)}, u32[]{:S(2)}, u32[]{:S(2)}) collective-permute-start(bf16[128,512]{1,0:T(8,128)(2,1)S(1)} %collective-permute-done.11.rest_3_), channel_id=1, source_target_pairs={{0,1},{1,0},{2,3},{3,2},{4,5},{5,4},{6,7},{7,6},{8,9},{9,8},{10,11... | collective-permute-start | bytes 393224 | tf_op jit(solution)/shard_map/ppermute | solution.py:228
  43.4 0.9 %collective-permute-done.15.rest_7_ = bf16[128,512]{1,0:T(8,128)(2,1)S(1)} collective-permute-done((bf16[128,512]{1,0:T(8,128)(2,1)S(1)}, bf16[128,512]{1,0:T(8,128)(2,1)S(1)}, u32[]{:S(2)}, u32[]{:S(2)}) %collective-permute-start.15) | collective-permute-done | bytes 131104 | tf_op jit(solution)/shard_map/ppermute | solution.py:228
  44.2 3.2 %mixed.1 = bf16[128,2048]{1,0:T(8,128)(2,1)} custom-call(s32[16,8]{1,0:T(8,128)S(1)} %copy.19.sources, s32[16,8]{1,0:T(8,128)S(1)} %copy.20.kinds, bf16[8,128,128]{2,1,0:T(8,128)(2,1)S(1)} %copy-done.5, f32[128,2048]{1,0:T(8,128)S(1)} %get-tuple-element.40.start, f32[8,128]{1,0:T(8,128)S(1)} %mark.1, bf16[128,512]{1,0:T(8,128)(2,1)S(1)} %get-tuple-element.55.rest_0_, ...), custom_call_target="tpu_custom_call" | custom-call | bytes 262144 | tf_op jit(solution)/shard_map/mixed/pallas_call | solution.py:196
  (50 shorter events, 2.6 us)
Async XLA Ops:
  1.1 5.0 %collective-permute-start.1 = (bf16[128,512]{1,0:T(8,128)(2,1)S(1)}, bf16[128,512]{1,0:T(8,128)(2,1)S(1)}, u32[]{:S(2)}, u32[]{:S(2)}) collective-permute-start(bf16[128,512]{1,0:T(8,128)(2,1)S(1)} %get-tuple-element.34), channel_id=1, source_target_pairs={{0,2},{2,0},{4,6},{6,4},{1,3},{3,1},{5,7},{7,5},{8,10},{10,8},{12,... | collective-permute-start | bytes 393224 | tf_op jit(solution)/shard_map/ppermute | solution.py:228
  2.4 5.0 %collective-permute-start.2 = (bf16[128,512]{1,0:T(8,128)(2,1)S(1)}, bf16[128,512]{1,0:T(8,128)(2,1)S(1)}, u32[]{:S(2)}, u32[]{:S(2)}) collective-permute-start(bf16[128,512]{1,0:T(8,128)(2,1)S(1)} %get-tuple-element.35), channel_id=1, source_target_pairs={{0,6},{2,4},{4,2},{6,0},{1,7},{3,5},{5,3},{7,1},{8,14},{10,12},{12... | collective-permute-start | bytes 393224 | tf_op jit(solution)/shard_map/ppermute | solution.py:228
  4.3 6.2 %collective-permute-start.3 = (bf16[128,512]{1,0:T(8,128)(2,1)S(1)}, bf16[128,512]{1,0:T(8,128)(2,1)S(1)}, u32[]{:S(2)}, u32[]{:S(2)}) collective-permute-start(bf16[128,512]{1,0:T(8,128)(2,1)S(1)} %get-tuple-element.36), channel_id=1, source_target_pairs={{0,4},{2,6},{4,0},{6,2},{1,5},{3,7},{5,1},{7,3},{8,12},{10,14},{12... | collective-permute-start | bytes 393224 | tf_op jit(solution)/shard_map/ppermute | solution.py:228
  4.9 18.1 %collective-permute-start = (bf16[128,2048]{1,0:T(8,128)(2,1)}, bf16[128,2048]{1,0:T(8,128)(2,1)S(1)}, u32[]{:S(2)}, u32[]{:S(2)}) collective-permute-start(bf16[128,2048]{1,0:T(8,128)(2,1)} %bitcast.own.whole), channel_id=1, source_target_pairs={{0,1},{1,0},{2,3},{3,2},{4,5},{5,4},{6,7},{7,6},{8,9},{9,8},{10,11... | collective-permute-start | bytes 1572872 | tf_op jit(solution)/shard_map/ppermute | solution.py:228
  10.5 12.4 %copy-start = (bf16[8,128,128]{2,1,0:T(8,128)(2,1)S(1)}, bf16[8,128,128]{2,1,0:T(8,128)(2,1)}, u32[]{:S(2)}) copy-start(bf16[8,128,128]{2,1,0:T(8,128)(2,1)} %table.3) | copy-start | bytes 786436
  10.5 12.4 %copy-start.1 = (bf16[8,128,128]{2,1,0:T(8,128)(2,1)S(1)}, bf16[8,128,128]{2,1,0:T(8,128)(2,1)}, u32[]{:S(2)}) copy-start(bf16[8,128,128]{2,1,0:T(8,128)(2,1)} %opp_table.1) | copy-start | bytes 786436
  11.5 14.2 %collective-permute-start.4 = (bf16[3,128,512]{2,1,0:T(8,128)(2,1)}, bf16[3,128,512]{2,1,0:T(8,128)(2,1)S(1)}, u32[]{:S(2)}, u32[]{:S(2)}) collective-permute-start(bf16[3,128,512]{2,1,0:T(8,128)(2,1)} %get-tuple-element.37), channel_id=1, source_target_pairs={{0,8},{16,24},{32,40},{48,56},{64,72},{80,88},{96,104},{112,120},{... | collective-permute-start | bytes 1179656 | tf_op jit(solution)/shard_map/ppermute | solution.py:238
  13.1 14.2 %collective-permute-start.5 = (bf16[3,128,512]{2,1,0:T(8,128)(2,1)}, bf16[3,128,512]{2,1,0:T(8,128)(2,1)S(1)}, u32[]{:S(2)}, u32[]{:S(2)}) collective-permute-start(bf16[3,128,512]{2,1,0:T(8,128)(2,1)} %get-tuple-element.38), channel_id=1, source_target_pairs={{8,16},{24,32},{40,48},{56,64},{72,80},{88,96},{104,112},{120,128}... | collective-permute-start | bytes 1179656 | tf_op jit(solution)/shard_map/ppermute | solution.py:238
  20.7 0.7 %copy-start.12 = (s32[128,4]{0,1:T(4,128)S(1)}, s32[128,4]{0,1:T(4,128)}, u32[]{:S(2)}) copy-start(s32[128,4]{0,1:T(4,128)} %param.16) | copy-start | bytes 6148
  22.9 4.3 %copy-start.2 = (bf16[8,128,128]{2,1,0:T(8,128)(2,1)S(1)}, bf16[8,128,128]{2,1,0:T(8,128)(2,1)}, u32[]{:S(2)}) copy-start(bf16[8,128,128]{2,1,0:T(8,128)(2,1)} %table.5) | copy-start | bytes 786436
  25.7 2.8 %copy-start.4 = (bf16[8,128,128]{2,1,0:T(8,128)(2,1)}, bf16[8,128,128]{2,1,0:T(8,128)(2,1)S(1)}, u32[]{:S(2)}) copy-start(bf16[8,128,128]{2,1,0:T(8,128)(2,1)S(1)} %get-tuple-element.32.table) | copy-start | bytes 786436
  27.3 4.5 %copy-start.3 = (bf16[8,128,128]{2,1,0:T(8,128)(2,1)S(1)}, bf16[8,128,128]{2,1,0:T(8,128)(2,1)}, u32[]{:S(2)}) copy-start(bf16[8,128,128]{2,1,0:T(8,128)(2,1)} %table.4) | copy-start | bytes 786436
  28.4 5.3 %collective-permute-start.10 = (bf16[128,512]{1,0:T(8,128)(2,1)S(1)}, bf16[128,512]{1,0:T(8,128)(2,1)S(1)}, u32[]{:S(2)}, u32[]{:S(2)}) collective-permute-start(bf16[128,512]{1,0:T(8,128)(2,1)S(1)} %get-tuple-element.52), channel_id=1, source_target_pairs={{0,2},{2,0},{4,6},{6,4},{1,3},{3,1},{5,7},{7,5},{8,10},{10,8},{12,... | collective-permute-start | bytes 393224 | tf_op jit(solution)/shard_map/ppermute | solution.py:228
  28.5 7.7 %collective-permute-start.11 = (bf16[128,512]{1,0:T(8,128)(2,1)S(1)}, bf16[128,512]{1,0:T(8,128)(2,1)S(1)}, u32[]{:S(2)}, u32[]{:S(2)}) collective-permute-start(bf16[128,512]{1,0:T(8,128)(2,1)S(1)} %get-tuple-element.53), channel_id=1, source_target_pairs={{0,6},{2,4},{4,2},{6,0},{1,7},{3,5},{5,3},{7,1},{8,14},{10,12},{12... | collective-permute-start | bytes 393224 | tf_op jit(solution)/shard_map/ppermute | solution.py:228
  29.0 7.3 %collective-permute-start.9 = (bf16[128,512]{1,0:T(8,128)(2,1)S(1)}, bf16[128,512]{1,0:T(8,128)(2,1)S(1)}, u32[]{:S(2)}, u32[]{:S(2)}) collective-permute-start(bf16[128,512]{1,0:T(8,128)(2,1)S(1)} %get-tuple-element.51), channel_id=1, source_target_pairs={{0,4},{2,6},{4,0},{6,2},{1,5},{3,7},{5,1},{7,3},{8,12},{10,14},{12... | collective-permute-start | bytes 393224 | tf_op jit(solution)/shard_map/ppermute | solution.py:228
  31.8 11.5 %copy-start.8 = (s32[16,8]{0,1:T(8,128)S(1)}, s32[16,8]{0,1:T(8,128)}, u32[]{:S(2)}) copy-start(s32[16,8]{0,1:T(8,128)} %param.15) | copy-start | bytes 1540
  32.9 11.3 %copy-start.5 = (bf16[8,128,128]{2,1,0:T(8,128)(2,1)S(1)}, bf16[8,128,128]{2,1,0:T(8,128)(2,1)}, u32[]{:S(2)}) copy-start(bf16[8,128,128]{2,1,0:T(8,128)(2,1)} %copy-done.4) | copy-start | bytes 786436
  32.9 8.0 %collective-permute-start.6 = (bf16[128,512]{1,0:T(8,128)(2,1)S(1)}, bf16[128,512]{1,0:T(8,128)(2,1)S(1)}, u32[]{:S(2)}, u32[]{:S(2)}) collective-permute-start(bf16[128,512]{1,0:T(8,128)(2,1)S(1)} %get-tuple-element.45), channel_id=1, source_target_pairs={{0,2},{2,0},{4,6},{6,4},{1,3},{3,1},{5,7},{7,5},{8,10},{10,8},{12,... | collective-permute-start | bytes 393224 | tf_op jit(solution)/shard_map/ppermute | solution.py:228
  33.1 8.8 %collective-permute-start.7 = (bf16[128,512]{1,0:T(8,128)(2,1)S(1)}, bf16[128,512]{1,0:T(8,128)(2,1)S(1)}, u32[]{:S(2)}, u32[]{:S(2)}) collective-permute-start(bf16[128,512]{1,0:T(8,128)(2,1)S(1)} %get-tuple-element.46), channel_id=1, source_target_pairs={{0,6},{2,4},{4,2},{6,0},{1,7},{3,5},{5,3},{7,1},{8,14},{10,12},{12... | collective-permute-start | bytes 393224 | tf_op jit(solution)/shard_map/ppermute | solution.py:228
  33.7 9.6 %collective-permute-start.8 = (bf16[128,512]{1,0:T(8,128)(2,1)S(1)}, bf16[128,512]{1,0:T(8,128)(2,1)S(1)}, u32[]{:S(2)}, u32[]{:S(2)}) collective-permute-start(bf16[128,512]{1,0:T(8,128)(2,1)S(1)} %get-tuple-element.47), channel_id=1, source_target_pairs={{0,4},{2,6},{4,0},{6,2},{1,5},{3,7},{5,1},{7,3},{8,12},{10,14},{12... | collective-permute-start | bytes 393224 | tf_op jit(solution)/shard_map/ppermute | solution.py:228
  36.3 7.1 %collective-permute-start.12 = (bf16[128,512]{1,0:T(8,128)(2,1)S(1)}, bf16[128,512]{1,0:T(8,128)(2,1)S(1)}, u32[]{:S(2)}, u32[]{:S(2)}) collective-permute-start(bf16[128,512]{1,0:T(8,128)(2,1)S(1)} %get-tuple-element.55.rest_0_), channel_id=1, source_target_pairs={{0,1},{1,0},{2,3},{3,2},{4,5},{5,4},{6,7},{7,6},{8,9},{9,8},{10,11... | collective-permute-start | bytes 393224 | tf_op jit(solution)/shard_map/ppermute | solution.py:228
  40.9 2.4 %collective-permute-start.13 = (bf16[128,512]{1,0:T(8,128)(2,1)S(1)}, bf16[128,512]{1,0:T(8,128)(2,1)S(1)}, u32[]{:S(2)}, u32[]{:S(2)}) collective-permute-start(bf16[128,512]{1,0:T(8,128)(2,1)S(1)} %collective-permute-done.10.rest_1_), channel_id=1, source_target_pairs={{0,1},{1,0},{2,3},{3,2},{4,5},{5,4},{6,7},{7,6},{8,9},{9,8},{10,11... | collective-permute-start | bytes 393224 | tf_op jit(solution)/shard_map/ppermute | solution.py:228
  40.9 2.4 %collective-permute-start.14 = (bf16[128,512]{1,0:T(8,128)(2,1)S(1)}, bf16[128,512]{1,0:T(8,128)(2,1)S(1)}, u32[]{:S(2)}, u32[]{:S(2)}) collective-permute-start(bf16[128,512]{1,0:T(8,128)(2,1)S(1)} %collective-permute-done.9.rest_2_), channel_id=1, source_target_pairs={{0,1},{1,0},{2,3},{3,2},{4,5},{5,4},{6,7},{7,6},{8,9},{9,8},{10,11... | collective-permute-start | bytes 393224 | tf_op jit(solution)/shard_map/ppermute | solution.py:228
  41.9 2.3 %collective-permute-start.15 = (bf16[128,512]{1,0:T(8,128)(2,1)S(1)}, bf16[128,512]{1,0:T(8,128)(2,1)S(1)}, u32[]{:S(2)}, u32[]{:S(2)}) collective-permute-start(bf16[128,512]{1,0:T(8,128)(2,1)S(1)} %collective-permute-done.11.rest_3_), channel_id=1, source_target_pairs={{0,1},{1,0},{2,3},{3,2},{4,5},{5,4},{6,7},{7,6},{8,9},{9,8},{10,11... | collective-permute-start | bytes 393224 | tf_op jit(solution)/shard_map/ppermute | solution.py:228
  (5 other events, 3.4 us)
